TPU v7x, 256 devices: a whole 4x4x8 slice. The times are simulated.
256 devices in a mesh: ctx: 32 (over x, y, core), head: 8 (over z).
Axes of the slice: x: 4, y: 4, z: 8, core: 2. Of those that a mesh axis runs over, the one named last changes fastest.
Arguments:
- queries: bfloat16 [32768, 4096], P(('ctx', 'head')), may hold values from -6 to 6
- keys: bfloat16 [32768, 4096], P(('ctx', 'head')), may hold values from -6 to 6
- values: bfloat16 [32768, 4096], P(('ctx', 'head')), may hold values from -6 to 6
- out_grad: bfloat16 [32768, 4096], P(('ctx', 'head')), may hold values from -1024 to 1024, as said below
Outputs:
- grad_queries: bfloat16 [32768, 4096], P(('ctx', 'head'))
- grad_keys: bfloat16 [32768, 4096], P(('ctx', 'head'))
- grad_values: bfloat16 [32768, 4096], P(('ctx', 'head'))
Inputs may be any that keep to these rules, and one draw needn't show every extreme that they name: `out_grad`: output gradients of varying size along the sequence.
All inputs are finite; a program needn't handle non-finite values.
Results may differ from a plain program's by a relative error of at most 0.011.
Values may be sent and summed in bfloat16 or wider, within the bound.
No kernel may reach another device: no remote copies, remote signals or barrier semaphores. Data moves between devices by JAX's collectives and lax.ppermute only.
A program may use at most 128 MiB of HBM per device.

v0:
```python
import math

import jax
import jax.numpy as jnp
from jax import lax
from jax.sharding import PartitionSpec as P

HD = 128
BLOCK = 512


def sent_together(arrays, axis, dim, along):
    widths = [math.prod(a.shape[along:]) for a in arrays]
    both = jnp.concatenate(
        [a.reshape(*a.shape[:along], w) for a, w in zip(arrays, widths)], axis=along
    )
    whole = lax.all_gather(both, axis, axis=dim, tiled=True)
    parts = jnp.split(whole, [sum(widths[:k]) for k in range(1, len(widths))], axis=along)
    return tuple((b.reshape(*whole.shape[:along], *a.shape[along:]) for a, b in zip(arrays, parts)))


def feature(inputs):
    real = inputs.astype(jnp.float32)
    return jnp.where(real > 0, real + 1.0, jnp.exp(jnp.minimum(real, 0.0)))


def slope(inputs):
    real = inputs.astype(jnp.float32)
    return jnp.where(real > 0, 1.0, jnp.exp(jnp.minimum(real, 0.0)))


def forward_block(query_feat, key_feat, value_rows, grad_rows, prefix_state, prefix_sum):
    length = query_feat.shape[0]
    causal = jnp.arange(length)[:, None] >= jnp.arange(length)[None, :]
    scores = jnp.where(
        causal, jnp.dot(query_feat, key_feat.T, preferred_element_type=jnp.float32), 0.0
    )
    weights = scores.astype(jnp.bfloat16)
    state_half = prefix_state.astype(jnp.bfloat16)
    numerator = jnp.dot(weights, value_rows, preferred_element_type=jnp.float32) + jnp.dot(
        query_feat, state_half, preferred_element_type=jnp.float32
    )
    denominator = jnp.sum(scores, axis=1) + jnp.dot(
        query_feat.astype(jnp.float32), prefix_sum, precision=lax.Precision.HIGHEST
    )
    attended = numerator / denominator[:, None]
    grad_real = grad_rows.astype(jnp.float32)
    grad_numerator = (grad_real / denominator[:, None]).astype(jnp.bfloat16)
    grad_denominator = -jnp.sum(grad_real * attended, axis=1) / denominator
    mixing = jnp.where(
        causal,
        jnp.dot(grad_numerator, value_rows.T, preferred_element_type=jnp.float32)
        + grad_denominator[:, None],
        0.0,
    ).astype(jnp.bfloat16)
    grad_query_feat = (
        jnp.dot(mixing, key_feat, preferred_element_type=jnp.float32)
        + jnp.dot(grad_numerator, state_half.T, preferred_element_type=jnp.float32)
        + grad_denominator[:, None] * prefix_sum[None, :]
    )
    return (grad_query_feat, grad_numerator, grad_denominator, weights, mixing)


def backward_block(
    query_feat, key_feat, value_rows, grad_numerator, weights, mixing, suffix_state, suffix_sum
):
    state_half = suffix_state.astype(jnp.bfloat16)
    grad_key_feat = (
        jnp.dot(mixing.T, query_feat, preferred_element_type=jnp.float32)
        + jnp.dot(value_rows, state_half.T, preferred_element_type=jnp.float32)
        + suffix_sum[None, :]
    )
    grad_value = jnp.dot(weights.T, grad_numerator, preferred_element_type=jnp.float32) + jnp.dot(
        key_feat, state_half, preferred_element_type=jnp.float32
    )
    return (grad_key_feat, grad_value.astype(jnp.bfloat16))


def earlier_blocks(totals):
    running = jnp.cumsum(totals, axis=1)
    return jnp.concatenate([jnp.zeros_like(totals[:, :1]), running[:, :-1]], axis=1)


def later_blocks(totals):
    running = jnp.flip(jnp.cumsum(jnp.flip(totals, 1), axis=1), 1)
    return jnp.concatenate([running[:, 1:], jnp.zeros_like(totals[:, :1])], axis=1)


def attention_core(query_rows, key_rows, value_rows, grad_rows):
    length = query_rows.shape[0]
    heads = query_rows.shape[1] // HD
    blocks = length // BLOCK

    def heads_first(inputs):
        return inputs.reshape(blocks, BLOCK, heads, HD).transpose(2, 0, 1, 3)

    def tokens_first(inputs):
        return inputs.transpose(1, 2, 0, 3).reshape(length, heads * HD)

    query_blocks = heads_first(query_rows)
    key_blocks = heads_first(key_rows)
    value_blocks = heads_first(value_rows)
    grad_blocks = heads_first(grad_rows)
    query_feat = feature(query_blocks).astype(jnp.bfloat16)
    key_feat = feature(key_blocks).astype(jnp.bfloat16)
    updates = jnp.einsum(
        "hnsk,hnsv->hnkv", key_feat, value_blocks, preferred_element_type=jnp.float32
    )
    key_totals = jnp.sum(key_feat.astype(jnp.float32), axis=2)
    own_forward = (jnp.sum(updates, axis=1), jnp.sum(key_totals, axis=1))
    place = lax.axis_index("ctx")
    pieces = sent_together((own_forward[0][None], own_forward[1][None]), "ctx", 0, 3)
    ranks = jnp.arange(pieces[0].shape[0])
    keep = (ranks < place).astype(jnp.float32)
    device_state = jnp.sum(keep[:, None, None, None] * pieces[0], axis=0)
    device_sum = jnp.sum(keep[:, None, None] * pieces[1], axis=0)
    block_state = device_state[:, None] + earlier_blocks(updates)
    block_sum = device_sum[:, None] + earlier_blocks(key_totals)
    forward_many = jax.vmap(jax.vmap(forward_block))
    grad_query_feat, grad_numerator, grad_denominator, weights, mixing = forward_many(
        query_feat, key_feat, value_blocks, grad_blocks, block_state, block_sum
    )
    grad_updates = jnp.einsum(
        "hnsk,hnsv->hnkv", query_feat, grad_numerator, preferred_element_type=jnp.float32
    )
    query_totals = jnp.sum(grad_denominator[..., None] * query_feat.astype(jnp.float32), axis=2)
    own_backward = (jnp.sum(grad_updates, axis=1), jnp.sum(query_totals, axis=1))
    pieces = (
        lax.all_gather(own_backward[0][None], "ctx", axis=0, tiled=True),
        lax.all_gather(own_backward[1][None], "ctx", axis=0, tiled=True),
    )
    ranks = jnp.arange(pieces[0].shape[0])
    keep = (ranks > place).astype(jnp.float32)
    suffix_state = jnp.sum(keep[:, None, None, None] * pieces[0], axis=0)
    suffix_sum = jnp.sum(keep[:, None, None] * pieces[1], axis=0)
    block_suffix = suffix_state[:, None] + later_blocks(grad_updates)
    block_suffix_sum = suffix_sum[:, None] + later_blocks(query_totals)
    backward_many = jax.vmap(jax.vmap(backward_block))
    grad_key_feat, grad_value = backward_many(
        query_feat,
        key_feat,
        value_blocks,
        grad_numerator,
        weights,
        mixing,
        block_suffix,
        block_suffix_sum,
    )
    grad_query = (grad_query_feat * slope(query_blocks)).astype(jnp.bfloat16)
    grad_key = (grad_key_feat * slope(key_blocks)).astype(jnp.bfloat16)
    return (tokens_first(grad_query), tokens_first(grad_key), tokens_first(grad_value))


def shards(queries, keys, values, out_grad):
    query_rows, key_rows, value_rows, grad_rows = (
        lax.all_to_all(queries, "head", split_axis=1, concat_axis=0, tiled=True),
        lax.all_to_all(keys, "head", split_axis=1, concat_axis=0, tiled=True),
        lax.all_to_all(values, "head", split_axis=1, concat_axis=0, tiled=True),
        lax.all_to_all(out_grad, "head", split_axis=1, concat_axis=0, tiled=True),
    )
    results = attention_core(query_rows, key_rows, value_rows, grad_rows)
    return (
        lax.all_to_all(results[0], "head", split_axis=0, concat_axis=1, tiled=True),
        lax.all_to_all(results[1], "head", split_axis=0, concat_axis=1, tiled=True),
        lax.all_to_all(results[2], "head", split_axis=0, concat_axis=1, tiled=True),
    )


def solution(mesh):
    return jax.shard_map(
        shards,
        mesh=mesh,
        in_specs=(
            P(("ctx", "head"), None),
            P(("ctx", "head"), None),
            P(("ctx", "head"), None),
            P(("ctx", "head"), None),
        ),
        out_specs=(P(("ctx", "head"), None), P(("ctx", "head"), None), P(("ctx", "head"), None)),
        check_vma=False,
    )
```

profile of v0, /device:TPU:1, one launch (start us, length us, event | category | flops | bytes accessed | tf_op | source)
XLA Modules:
  0.0 330.9 jit_solution(16789274986668472562)
XLA Ops:
  7.2 2.4 copy.316
  9.6 9.0 %all-to-all-start.2 = ((bf16[128,8,512]{2,0,1:T(8,128)(2,1)}), bf16[128,8,512]{2,0,1:T(8,128)(2,1)S(1)}, u32[]{:S(2)}, u32[]{:S(2)}) async-start(bf16[128,8,512]{2,0,1:T(8,128)(2,1)} %bitcast.112), calls=%async_computation.2 | async-start | bytes 2097152 | tf_op jit(solution)/shard_map/all_to_all | solution.py:157
  18.6 1.1 copy.314
  19.6 28.1 %all-to-all-done.2 = bf16[128,8,512]{2,0,1:T(8,128)(2,1)S(1)} async-done(((bf16[128,8,512]{2,0,1:T(8,128)(2,1)}), bf16[128,8,512]{2,0,1:T(8,128)(2,1)S(1)}, u32[]{:S(2)}, u32[]{:S(2)}) %all-to-all-start.2) | async-done | bytes 1048608 | tf_op jit(solution)/shard_map/all_to_all | solution.py:157
  47.8 3.6 %all-to-all-start.3 = ((bf16[128,8,512]{2,0,1:T(8,128)(2,1)}), bf16[128,8,512]{2,0,1:T(8,128)(2,1)S(1)}, u32[]{:S(2)}, u32[]{:S(2)}) async-start(bf16[128,8,512]{2,0,1:T(8,128)(2,1)} %bitcast.110), calls=%async_computation.3 | async-start | bytes 2097152 | tf_op jit(solution)/shard_map/all_to_all | solution.py:158
  51.4 1.9 fusion.10
  53.5 1.1 convert_reduce_fusion.1
  54.8 25.7 %all-to-all-done.3 = bf16[128,8,512]{2,0,1:T(8,128)(2,1)S(1)} async-done(((bf16[128,8,512]{2,0,1:T(8,128)(2,1)}), bf16[128,8,512]{2,0,1:T(8,128)(2,1)S(1)}, u32[]{:S(2)}, u32[]{:S(2)}) %all-to-all-start.3) | async-done | bytes 1048608 | tf_op jit(solution)/shard_map/all_to_all | solution.py:158
  80.8 1.4 fusion.53
  82.2 0.9 copy.222
  83.1 2.3 copy.315
  85.4 3.6 %all-to-all-start.1 = ((bf16[128,8,512]{2,0,1:T(8,128)(2,1)}), bf16[128,8,512]{2,0,1:T(8,128)(2,1)S(1)}, u32[]{:S(2)}, u32[]{:S(2)}) async-start(bf16[128,8,512]{2,0,1:T(8,128)(2,1)} %bitcast.111), calls=%async_computation.1 | async-start | bytes 2097152 | tf_op jit(solution)/shard_map/all_to_all | solution.py:156
  89.0 2.3 copy.317
  91.3 26.9 %all-to-all-done.1 = bf16[128,8,512]{2,0,1:T(8,128)(2,1)S(1)} async-done(((bf16[128,8,512]{2,0,1:T(8,128)(2,1)}), bf16[128,8,512]{2,0,1:T(8,128)(2,1)S(1)}, u32[]{:S(2)}, u32[]{:S(2)}) %all-to-all-start.1) | async-done | bytes 1048608 | tf_op jit(solution)/shard_map/all_to_all | solution.py:156
  118.2 4.2 %all-to-all-start = ((bf16[128,8,512]{2,0,1:T(8,128)(2,1)}), bf16[128,8,512]{2,0,1:T(8,128)(2,1)}, u32[]{:S(2)}, u32[]{:S(2)}) async-start(bf16[128,8,512]{2,0,1:T(8,128)(2,1)} %bitcast.113), calls=%async_computation | async-start | bytes 2097152 | tf_op jit(solution)/shard_map/all_to_all | solution.py:159
  122.6 2.2 fusion.28
  124.8 2.2 reshape.112
  127.0 1.6 copy.240
  128.6 23.0 %all-to-all-done = bf16[128,8,512]{2,0,1:T(8,128)(2,1)} async-done(((bf16[128,8,512]{2,0,1:T(8,128)(2,1)}), bf16[128,8,512]{2,0,1:T(8,128)(2,1)}, u32[]{:S(2)}, u32[]{:S(2)}) %all-to-all-start) | async-done | bytes 1048608 | tf_op jit(solution)/shard_map/all_to_all | solution.py:159
  151.6 2.9 convert_bitcast_fusion
  154.5 2.9 reshape.114
  157.4 2.9 copy.213
  160.3 3.3 select_reduce_fusion
  163.6 0.8 split.8
  165.1 1.9 fusion.16
  167.0 1.0 copy-done.3
  168.0 2.0 fusion.54
  170.0 1.5 copy.224
  171.4 2.9 reshape.109
  174.3 1.1 fusion.56
  175.4 2.9 reshape.111
  178.4 4.5 %fusion.21 = f32[4,2,512,128]{2,3,1,0:T(8,128)} fusion(bf16[4,2,512,512]{2,3,1,0:T(8,128)(2,1)} %get-tuple-element.29, pred[512,512]{0,1:T(8,128)(4,1)} %copy-done.10, bf16[2,512,4,128]{3,2,1,0:T(4,128)(2,1)S(1)} %reshape.104), kind=kOutput, calls=%fused_computation.41 | convolution fusion | flops 538968064 | bytes 7602176 | tf_op jit(solution)/shard_map/vmap(vmap())/dot_general | solution.py:40
  182.9 6.3 %fusion = f32[4,128,128]{1,0,2:T(4,128)} fusion(f32[32,4,128,129]{2,1,3,0:T(4,128)} %all-gather.6.cloned.1.call-done, f32[32]{0:T(128)S(1)} %compare_convert_fusion.1), kind=kLoop, calls=%fused_computation.1 | loop fusion | flops 4128768 | bytes 8650880 | tf_op jit(solution)/shard_map/reduce_sum | solution.py:115
  189.2 1.8 copy.228
  191.0 2.8 fusion.17
  193.8 1.0 copy.243
  194.9 3.0 select_convert_fusion
  197.9 1.5 fusion.39
  200.0 1.3 copy-done.6
  201.3 1.3 fusion.15
  202.6 1.8 copy.237
  204.4 2.3 all_to_all.93
  206.6 4.4 %all-to-all-start.4 = ((bf16[8,128,512]{2,1,0:T(8,128)(2,1)}), bf16[8,128,512]{2,1,0:T(8,128)(2,1)}, u32[]{:S(2)}, u32[]{:S(2)}) async-start(bf16[8,128,512]{2,1,0:T(8,128)(2,1)} %all_to_all.93), calls=%async_computation.4 | async-start | bytes 2097152 | tf_op jit(solution)/shard_map/all_to_all | solution.py:163
  211.0 1.9 rev.10
  212.9 3.1 fusion.19
  216.0 24.8 %all-gather.2 = f32[32,4,128]{2,1,0:T(4,128)S(1)} all-gather(f32[1,4,128]{2,1,0:T(4,128)S(1)} %bitcast.140), channel_id=3, replica_groups=mesh['ctx'=32,'head'=8] {'ctx'}, dimensions={0}, use_global_device_ids=true | all-gather | bytes 67584 | tf_op jit(solution)/shard_map/all_gather | solution.py:130
  241.0 4.7 %fusion.57 = f32[4,2,512,128]{3,2,1,0:T(8,128)} fusion(bf16[4,2,512,512]{2,3,1,0:T(8,128)(2,1)} %copy-done, bf16[4,2,512,128]{2,3,1,0:T(8,128)(2,1)S(1)} %copy.240), kind=kOutput, calls=%fused_computation.93 | convolution fusion | flops 536870912 | bytes 7340032 | tf_op jit(solution)/shard_map/vmap(vmap())/dot_general | solution.py:69
  245.8 4.7 %multiply_reduce_fusion = f32[4,128,128]{2,1,0:T(8,128)S(1)} fusion(f32[32,4,128,128]{3,2,1,0:T(8,128)} %bitcast.122, f32[32]{0:T(128)S(1)} %compare_convert_fusion), kind=kLoop, calls=%fused_computation.2 | loop fusion | flops 4128768 | bytes 8650880 | tf_op jit(solution)/shard_map/reduce_sum | solution.py:134
  250.6 0.6 fusion.13
  251.2 0.8 copy.246
  252.1 1.2 all_to_all.97
  253.3 6.8 %all-to-all-start.5 = ((bf16[8,128,512]{2,1,0:T(8,128)(2,1)}), bf16[8,128,512]{2,1,0:T(8,128)(2,1)S(1)}, u32[]{:S(2)}, u32[]{:S(2)}) async-start(bf16[8,128,512]{2,1,0:T(8,128)(2,1)} %all_to_all.97), calls=%async_computation.5 | async-start | bytes 2097152 | tf_op jit(solution)/shard_map/all_to_all | solution.py:164
  260.1 3.5 %fusion.20 = f32[4,2,512,128]{3,2,1,0:T(8,128)S(1)} fusion(bf16[4,2,512,128]{2,3,1,0:T(8,128)(2,1)S(1)} %copy-done.5, bf16[4,2,512,512]{2,3,1,0:T(8,128)(2,1)} %get-tuple-element.29, pred[512,512]{0,1:T(8,128)(4,1)} %copy-done.10), kind=kOutput, calls=%fused_computation.40 | convolution fusion | flops 538968064 | bytes 7602176 | tf_op jit(solution)/shard_map/vmap(vmap())/dot_general | solution.py:73
  264.1 0.8 copy.250
  264.9 1.2 all_to_all.101
  266.1 23.3 %all-to-all-done.5 = bf16[8,128,512]{2,1,0:T(8,128)(2,1)S(1)} async-done(((bf16[8,128,512]{2,1,0:T(8,128)(2,1)}), bf16[8,128,512]{2,1,0:T(8,128)(2,1)S(1)}, u32[]{:S(2)}, u32[]{:S(2)}) %all-to-all-start.5) | async-done | bytes 1048608 | tf_op jit(solution)/shard_map/all_to_all | solution.py:164
  289.4 3.6 %all-to-all-start.6 = ((bf16[8,128,512]{2,1,0:T(8,128)(2,1)}), bf16[8,128,512]{2,1,0:T(8,128)(2,1)S(1)}, u32[]{:S(2)}, u32[]{:S(2)}) async-start(bf16[8,128,512]{2,1,0:T(8,128)(2,1)} %all_to_all.101), calls=%async_computation.6 | async-start | bytes 2097152 | tf_op jit(solution)/shard_map/all_to_all | solution.py:165
  292.9 1.6 copy.238
  294.6 1.3 copy.252
  295.9 0.7 copy.247
  296.5 1.3 copy.253
  297.8 24.2 %all-to-all-done.6 = bf16[8,128,512]{2,1,0:T(8,128)(2,1)S(1)} async-done(((bf16[8,128,512]{2,1,0:T(8,128)(2,1)}), bf16[8,128,512]{2,1,0:T(8,128)(2,1)S(1)}, u32[]{:S(2)}, u32[]{:S(2)}) %all-to-all-start.6) | async-done | bytes 1048608 | tf_op jit(solution)/shard_map/all_to_all | solution.py:165
  322.1 0.7 copy.251
  322.8 1.3 copy.254
  (54 shorter events, 3.0 us)
Async XLA Ops:
  7.2 11.4 %copy-start.9 = (bf16[128,4096]{1,0:T(8,128)(2,1)S(1)}, bf16[128,4096]{1,0:T(8,128)(2,1)}, u32[]{:S(2)}) copy-start(bf16[128,4096]{1,0:T(8,128)(2,1)} %param.6) | copy-start | bytes 3145732
  9.6 38.2 %all-to-all-start.2 = ((bf16[128,8,512]{2,0,1:T(8,128)(2,1)}), bf16[128,8,512]{2,0,1:T(8,128)(2,1)S(1)}, u32[]{:S(2)}, u32[]{:S(2)}) async-start(bf16[128,8,512]{2,0,1:T(8,128)(2,1)} %bitcast.112), calls=%async_computation.2 | async-start | bytes 2097152 | tf_op jit(solution)/shard_map/all_to_all | solution.py:157
  47.8 32.7 %all-to-all-start.3 = ((bf16[128,8,512]{2,0,1:T(8,128)(2,1)}), bf16[128,8,512]{2,0,1:T(8,128)(2,1)S(1)}, u32[]{:S(2)}, u32[]{:S(2)}) async-start(bf16[128,8,512]{2,0,1:T(8,128)(2,1)} %bitcast.110), calls=%async_computation.3 | async-start | bytes 2097152 | tf_op jit(solution)/shard_map/all_to_all | solution.py:158
  51.3 112.3 %all-gather.6.cloned.1.call-start = ((), (), s32[]{:S(2)}) async-start(), calls=%async_computation.7 | async-start | bytes 8718336 | tf_op jit(solution)/shard_map/all_gather | solution.py:17
  85.4 32.7 %all-to-all-start.1 = ((bf16[128,8,512]{2,0,1:T(8,128)(2,1)}), bf16[128,8,512]{2,0,1:T(8,128)(2,1)S(1)}, u32[]{:S(2)}, u32[]{:S(2)}) async-start(bf16[128,8,512]{2,0,1:T(8,128)(2,1)} %bitcast.111), calls=%async_computation.1 | async-start | bytes 2097152 | tf_op jit(solution)/shard_map/all_to_all | solution.py:156
  118.2 33.5 %all-to-all-start = ((bf16[128,8,512]{2,0,1:T(8,128)(2,1)}), bf16[128,8,512]{2,0,1:T(8,128)(2,1)}, u32[]{:S(2)}, u32[]{:S(2)}) async-start(bf16[128,8,512]{2,0,1:T(8,128)(2,1)} %bitcast.113), calls=%async_computation | async-start | bytes 2097152 | tf_op jit(solution)/shard_map/all_to_all | solution.py:159
  122.4 123.3 %all-gather.8.cloned.1.call-start = ((), (), s32[]{:S(2)}) async-start(), calls=%async_computation.8 | async-start | bytes 8650752 | tf_op jit(solution)/shard_map/all_gather | solution.py:129
  122.6 37.8 %copy-start.10 = (pred[512,512]{0,1:T(8,128)(4,1)}, pred[512,512]{0,1:T(8,128)(4,1)S(1)}, u32[]{:S(2)}) copy-start(pred[512,512]{0,1:T(8,128)(4,1)S(1)} %iota_compare_fusion) | copy-start | bytes 786436
  128.6 28.8 %copy-start.11 = (f32[4,2,128]{2,0,1:T(4,128)}, f32[4,2,128]{2,0,1:T(4,128)S(1)}, u32[]{:S(2)}) copy-start(f32[4,2,128]{2,0,1:T(4,128)S(1)} %fusion.55) | copy-start | bytes 12292
  160.3 4.2 %slice-start = ((f32[4,2,128]{2,0,1:T(4,128)}), f32[4,1,128]{2,0,1:T(4,128)S(1)}, s32[]{:S(2)}) async-start(f32[4,2,128]{2,0,1:T(4,128)} %copy-done.11), calls=%async_computation.9 | async-start | bytes 4096 | tf_op jit(solution)/shard_map/slice | solution.py:81
  167.0 1.0 copy-start.3
  197.9 2.1 copy-start
  197.9 2.1 copy-start.4
  197.9 3.4 %copy-start.6 = (f32[2,512,4,128]{3,2,1,0:T(4,128)S(1)}, f32[2,512,4,128]{3,2,1,0:T(4,128)}, u32[]{:S(2)}) copy-start(f32[2,512,4,128]{3,2,1,0:T(4,128)} %reshape.109) | copy-start | bytes 6291460
  197.9 3.4 %copy-start.8 = (f32[4,128,128]{2,1,0:T(8,128)S(1)}, f32[4,128,128]{2,1,0:T(8,128)}, u32[]{:S(2)}) copy-start(f32[4,128,128]{2,1,0:T(8,128)} %copy.228) | copy-start | bytes 786436
  206.6 34.3 %copy-start.12 = (pred[2]{0:T(512)(128)(4,1)S(1)}, pred[2]{0:T(512)(128)(4,1)}, u32[]{:S(2)}) copy-start(pred[2]{0:T(512)(128)(4,1)} %constant.24.clone.1) | copy-start | bytes 10
  206.6 46.7 %all-to-all-start.4 = ((bf16[8,128,512]{2,1,0:T(8,128)(2,1)}), bf16[8,128,512]{2,1,0:T(8,128)(2,1)}, u32[]{:S(2)}, u32[]{:S(2)}) async-start(bf16[8,128,512]{2,1,0:T(8,128)(2,1)} %all_to_all.93), calls=%async_computation.4 | async-start | bytes 2097152 | tf_op jit(solution)/shard_map/all_to_all | solution.py:163
  245.7 4.7 %copy-start.7 = (f32[4,2,128,128]{3,2,1,0:T(8,128)S(1)}, f32[4,2,128,128]{3,2,1,0:T(8,128)}, u32[]{:S(2)}) copy-start(f32[4,2,128,128]{3,2,1,0:T(8,128)} %rev.10) | copy-start | bytes 1572868
  245.7 4.8 %copy-start.1 = (f32[4,2,512,128]{3,2,1,0:T(8,128)S(1)}, f32[4,2,512,128]{3,2,1,0:T(8,128)}, u32[]{:S(2)}) copy-start(f32[4,2,512,128]{3,2,1,0:T(8,128)} %fusion.57) | copy-start | bytes 6291460
  245.8 4.8 %copy-start.2 = (f32[2,512,4,128]{3,2,1,0:T(4,128)S(1)}, f32[2,512,4,128]{3,2,1,0:T(4,128)}, u32[]{:S(2)}) copy-start(f32[2,512,4,128]{3,2,1,0:T(4,128)} %reshape.111) | copy-start | bytes 6291460
  252.1 8.1 %copy-start.5 = (bf16[4,2,512,128]{2,3,1,0:T(8,128)(2,1)S(1)}, bf16[4,2,512,128]{2,3,1,0:T(8,128)(2,1)}, u32[]{:S(2)}) copy-start(bf16[4,2,512,128]{2,3,1,0:T(8,128)(2,1)} %copy-done.3) | copy-start | bytes 3145732
  253.3 36.1 %all-to-all-start.5 = ((bf16[8,128,512]{2,1,0:T(8,128)(2,1)}), bf16[8,128,512]{2,1,0:T(8,128)(2,1)S(1)}, u32[]{:S(2)}, u32[]{:S(2)}) async-start(bf16[8,128,512]{2,1,0:T(8,128)(2,1)} %all_to_all.97), calls=%async_computation.5 | async-start | bytes 2097152 | tf_op jit(solution)/shard_map/all_to_all | solution.py:164
  289.4 32.7 %all-to-all-start.6 = ((bf16[8,128,512]{2,1,0:T(8,128)(2,1)}), bf16[8,128,512]{2,1,0:T(8,128)(2,1)S(1)}, u32[]{:S(2)}, u32[]{:S(2)}) async-start(bf16[8,128,512]{2,1,0:T(8,128)(2,1)} %all_to_all.101), calls=%async_computation.6 | async-start | bytes 2097152 | tf_op jit(solution)/shard_map/all_to_all | solution.py:165
Sparse Core Ops, SparseCore 0:
  83.3 54.4 all-gather.5
  170.1 54.3 all-gather.7
where the time goes:
time: 332 us; the launch traced here: 331 us
  waiting for transfers between devices  151 us (45%)
  local copies, waits for them, and re-layouts  49.9 us (15%)
  starting transfers between devices  35.2 us (11%)
  matrix products  29.6 us (9%)
  other arithmetic  25.7 us (8%)
  blocking collectives  24.8 us (7%)
  between operations  14.4 us (4%)
    all_to_all x1, waiting for transfers between devices, shards(): lax.all_to_all(keys, 'head', split_axis=1, concat_axis=0, tiled=True)  28.1 us
    all_to_all x1, waiting for transfers between devices, shards(): lax.all_to_all(queries, 'head', split_axis=1, concat_axis=0, tiled=True)  26.9 us
    all_to_all x1, waiting for transfers between devices, shards(): lax.all_to_all(values, 'head', split_axis=1, concat_axis=0, tiled=True)  25.7 us
    all_gather x1, blocking collectives, attention_core(): lax.all_gather(own_backward[1][None], 'ctx', axis=0, tiled=True)  24.8 us
    all_to_all x1, waiting for transfers between devices, shards(): lax.all_to_all(results[2], 'head', split_axis=0, concat_axis=1, tiled=True)  24.2 us
    all_to_all x1, waiting for transfers between devices, shards(): lax.all_to_all(results[1], 'head', split_axis=0, concat_axis=1, tiled=True)  23.3 us
    all_to_all x1, waiting for transfers between devices, shards(): lax.all_to_all(out_grad, 'head', split_axis=1, concat_axis=0, tiled=True)  23 us
    all_to_all x1, starting transfers between devices, shards(): lax.all_to_all(keys, 'head', split_axis=1, concat_axis=0, tiled=True)  9 us
  transfers between devices with their start and end apart: 9, of which 6 were waited for; matrix products, arithmetic and copies ran while one was open for 26% of the time, Pallas kernels for 0%

commit v1 on v0

v1 whole, which is shorter than its diff:
```python
import functools

import jax
import jax.numpy as jnp
from jax import lax
from jax.experimental import pallas as pl
from jax.experimental.pallas import tpu as pltpu
from jax.sharding import PartitionSpec as P

HD = 128

F32 = jnp.float32
BF16 = jnp.bfloat16


def feature(real):
    return jnp.where(real > 0, real + 1.0, jnp.exp(jnp.minimum(real, 0.0)))


def slope(real):
    return jnp.where(real > 0, 1.0, jnp.exp(jnp.minimum(real, 0.0)))


def dot_nn(a, b):
    return lax.dot_general(a, b, (((1,), (0,)), ((), ())), preferred_element_type=F32)


def dot_nt(a, b):
    return lax.dot_general(a, b, (((1,), (1,)), ((), ())), preferred_element_type=F32)


def dot_tn(a, b):
    return lax.dot_general(a, b, (((0,), (0,)), ((), ())), preferred_element_type=F32)


def causal(n):
    return lax.broadcasted_iota(jnp.int32, (n, n), 0) >= lax.broadcasted_iota(jnp.int32, (n, n), 1)


def columns(j):
    return slice(j * HD, (j + 1) * HD)


def head_row(ref, step, j):
    return ref[pl.ds(pl.program_id(0) * step + j, 1), :]


def put_head_row(ref, step, j, row):
    ref[pl.ds(pl.program_id(0) * step + j, 1), :] = row


def each(fn, *lists):
    return [fn(*items) for items in zip(*lists)]


def key_state_kernel(step, k_ref, v_ref, state_ref, sum_ref):
    heads = range(step)
    fk = [feature(k_ref[:, columns(j)].astype(F32)).astype(BF16) for j in heads]
    states = [dot_tn(fk[j], v_ref[:, columns(j)]) for j in heads]
    for j in heads:
        put_head_row(sum_ref, step, j, jnp.sum(fk[j].astype(F32), axis=0, keepdims=True))
    for j in heads:
        state_ref[j] = states[j].astype(BF16)


def scores_of(fq, fk, zrows, mask):
    scores = [jnp.where(mask, s, 0.0) for s in each(dot_nt, fq, fk)]
    dens = [
        jnp.sum(s + f.astype(F32) * zrow, axis=1, keepdims=True)
        for s, f, zrow in zip(scores, fq, zrows)
    ]
    return [s.astype(BF16) for s in scores], [1.0 / den for den in dens]


def query_state_kernel(step, q_ref, k_ref, g_ref, z_ref, state_ref):
    mask = causal(q_ref.shape[0])
    heads = range(step)
    fq = [feature(q_ref[:, columns(j)].astype(F32)).astype(BF16) for j in heads]
    fk = [feature(k_ref[:, columns(j)].astype(F32)).astype(BF16) for j in heads]
    _, inverse = scores_of(fq, fk, [head_row(z_ref, step, j) for j in heads], mask)
    dnum = [(g_ref[:, columns(j)].astype(F32) * inverse[j]).astype(BF16) for j in heads]
    states = each(dot_tn, fq, dnum)
    for j in heads:
        state_ref[j] = states[j].astype(BF16)


def query_grad_kernel(step, q_ref, k_ref, v_ref, g_ref, z_ref, s_ref, gq_ref, dfk_ref, gv_ref, sum_ref):
    mask = causal(q_ref.shape[0])
    heads = range(step)
    fq32 = [feature(q_ref[:, columns(j)].astype(F32)) for j in heads]
    fq = [f.astype(BF16) for f in fq32]
    fk = [feature(k_ref[:, columns(j)].astype(F32)).astype(BF16) for j in heads]
    zrows = [head_row(z_ref, step, j) for j in heads]
    v = [v_ref[:, columns(j)] for j in heads]
    weights, inverse = scores_of(fq, fk, zrows, mask)
    num = [dot_nn(weights[j], v[j]) + dot_nn(fq[j], s_ref[j]) for j in heads]
    dnum = [(g_ref[:, columns(j)].astype(F32) * inverse[j]).astype(BF16) for j in heads]
    pair = each(dot_nt, dnum, v)
    shared = [
        jnp.sum(g_ref[:, columns(j)].astype(F32) * num[j], axis=1, keepdims=True) for j in heads
    ]
    dden = [-(s * i) * i for s, i in zip(shared, inverse)]
    mixing = [jnp.where(mask, p + d, 0.0).astype(BF16) for p, d in zip(pair, dden)]
    for j in heads:
        gv_ref[:, columns(j)] = dot_tn(weights[j], dnum[j])
    for j in heads:
        put_head_row(sum_ref, step, j, jnp.sum(dden[j] * fq[j].astype(F32), axis=0, keepdims=True))
    dfq = [
        dot_nn(mixing[j], fk[j]) + dot_nt(dnum[j], s_ref[j]) + dden[j] * zrows[j] for j in heads
    ]
    for j in heads:
        gq_ref[:, columns(j)] = (dfq[j] * jnp.minimum(fq32[j], 1.0)).astype(BF16)
    for j in heads:
        dfk_ref[:, columns(j)] = dot_tn(mixing[j], fq[j])


def key_grad_kernel(step, k_ref, v_ref, dfk_ref, gv_ref, rs_ref, dfk_out_ref, gv_out_ref):
    heads = range(step)
    fk = [feature(k_ref[:, columns(j)].astype(F32)).astype(BF16) for j in heads]
    for j in heads:
        c = columns(j)
        dfk_out_ref[:, c] = dfk_ref[:, c] + dot_nt(v_ref[:, c], rs_ref[j])
    for j in heads:
        c = columns(j)
        gv_out_ref[:, c] = (gv_ref[:, c] + dot_nn(fk[j], rs_ref[j])).astype(BF16)


def key_finish_kernel(step, k_ref, dfk_ref, rz_ref, gk_ref):
    for j in range(step):
        c = columns(j)
        dfk = dfk_ref[:, c] + head_row(rz_ref, step, j)
        gk_ref[:, c] = (dfk * slope(k_ref[:, c].astype(F32))).astype(BF16)


def head_call(kernel, step, kinds_in, kinds_out, arrays, tokens, heads):
    wide = pl.BlockSpec((tokens, step * HD), lambda i: (0, i))
    square = pl.BlockSpec((step, HD, HD), lambda i: (i, 0, 0))
    rows = pl.BlockSpec((heads, HD), lambda i: (0, 0))
    specs = {"w": wide, "f": wide, "s": square, "r": rows}
    shapes = {
        "w": jax.ShapeDtypeStruct((tokens, heads * HD), BF16),
        "f": jax.ShapeDtypeStruct((tokens, heads * HD), F32),
        "s": jax.ShapeDtypeStruct((heads, HD, HD), BF16),
        "r": jax.ShapeDtypeStruct((heads, HD), F32),
    }
    return pl.pallas_call(
        functools.partial(kernel, step),
        grid=(heads // step,),
        in_specs=[specs[t] for t in kinds_in],
        out_specs=[specs[t] for t in kinds_out],
        out_shape=[shapes[t] for t in kinds_out],
        compiler_params=pltpu.CompilerParams(dimension_semantics=("arbitrary",)),
    )(*arrays)


def z_total_kernel(x_ref, tot_ref):
    tot = x_ref[0].astype(F32)
    for z in range(1, x_ref.shape[0]):
        tot = tot + x_ref[z].astype(F32)
    tot_ref[...] = tot


def z_running_kernel(forward, x_ref, base_ref, out_ref):
    n = x_ref.shape[0]
    acc = base_ref[...]
    for s in range(n):
        z = s if forward else n - 1 - s
        out_ref[z] = acc.astype(BF16)
        if s < n - 1:
            acc = acc + x_ref[z].astype(F32)


def z_total(x):
    n, rows, lanes = x.shape
    return pl.pallas_call(
        z_total_kernel,
        grid=(1,),
        in_specs=[pl.BlockSpec((n, rows, lanes), lambda i: (0, i, 0))],
        out_specs=pl.BlockSpec((rows, lanes), lambda i: (i, 0)),
        out_shape=jax.ShapeDtypeStruct((rows, lanes), F32),
    )(x)


def z_running(x, base, forward):
    n, rows, lanes = x.shape
    return pl.pallas_call(
        functools.partial(z_running_kernel, forward),
        grid=(1,),
        in_specs=[
            pl.BlockSpec((n, rows, lanes), lambda i: (0, i, 0)),
            pl.BlockSpec((rows, lanes), lambda i: (i, 0)),
        ],
        out_specs=pl.BlockSpec((n, rows, lanes), lambda i: (0, i, 0)),
        out_shape=jax.ShapeDtypeStruct((n, rows, lanes), BF16),
    )(x, base)


def level(part, total, n, place, hop, forward, wire):
    before = None
    d = 1
    while d < n:
        if total is None:
            got_part, got_total = hop(part.astype(wire), d).astype(F32), None
        elif total is part:
            got_part = got_total = hop(part.astype(wire), d).astype(F32)
        else:
            got = hop(jnp.stack([part, total]).astype(wire), d).astype(F32)
            got_part, got_total = got[0], got[1]
        ok = (place >= d) if forward else (place < n - d)
        masked = jnp.where(ok, got_part, 0.0)
        before = masked if before is None else before + masked
        part, total = part + masked, None if total is None else total + got_total
        d *= 2
    return before, total


def grid_of(ctx):
    side = 1
    while side * side * 2 < ctx:
        side += 1
    return side


def ctx_hop(side, which, forward):
    def hop(value, d):
        d = d if forward else -d
        pairs = []
        for x in range(side):
            for y in range(side):
                for c in range(2):
                    to = (x, (y + d) % side) if which == "y" else ((x + d) % side, y)
                    pairs.append(((x * side + y) * 2 + c, (to[0] * side + to[1]) * 2 + c))
        return lax.ppermute(value, "ctx", pairs)

    return hop


def swap_cores(value, ctx):
    return lax.ppermute(value, "ctx", [(i, i ^ 1) for i in range(ctx)])


def ctx_running(total, ctx, forward, wire, split):
    side = grid_of(ctx)
    place = lax.axis_index("ctx")
    core, y, x = place % 2, (place // 2) % side, place // (2 * side)
    other = swap_cores(total, ctx)
    by_core = jnp.where((core == 1) if forward else (core == 0), other, 0.0)
    chip = total + other
    half = total.shape[0] // 2
    if split:
        chip = jnp.where(core == 0, chip[:half], chip[half:])
    by_y, row = level(chip, chip, side, y, ctx_hop(side, "y", forward), forward, wire)
    by_x, _ = level(row, None, side, x, ctx_hop(side, "x", forward), forward, wire)
    base = by_y + by_x
    if split:
        got = swap_cores(base, ctx)
        base = jnp.concatenate([jnp.where(core == 0, base, got), jnp.where(core == 0, got, base)])
    return by_core + base


def z_gather(x, group):
    return lax.all_to_all(jnp.broadcast_to(x[None], (group, *x.shape)), "head", 0, 0, tiled=True)


def shards(ctx, group, queries, keys, values, out_grad):
    tokens, width = queries.shape
    heads = width // HD
    call = functools.partial(head_call, tokens=tokens, heads=heads)
    owned = heads * HD // group
    place = lax.axis_index("head")

    def to_owners(state):
        return lax.all_to_all(state.reshape(group, owned, HD), "head", 0, 0, tiled=True)

    def from_owners(x):
        return lax.all_to_all(x, "head", 0, 0, tiled=True).reshape(heads, HD, HD)

    ranks = jnp.arange(group)[:, None, None]
    key_state, key_sum = call(key_state_kernel, 16, "ww", "sr", (keys, values))
    sums = z_gather(key_sum, group)
    before = jnp.sum(jnp.where(ranks < place, sums, 0.0), axis=0)
    key_state, before, total = lax.optimization_barrier((key_state, before, jnp.sum(sums, axis=0)))
    key_parts = to_owners(key_state)
    z = before + ctx_running(total, ctx, True, F32, False)
    (query_state,) = call(query_state_kernel, 16, "wwwr", "s", (queries, keys, out_grad, z))
    key_parts, query_state = lax.optimization_barrier((key_parts, query_state))
    query_parts = to_owners(query_state)
    key_total = z_total(key_parts)
    key_base = ctx_running(key_total, ctx, True, BF16, True)
    key_running = z_running(key_parts, key_base, True)
    query_parts, key_running = lax.optimization_barrier((query_parts, key_running))
    prefix = from_owners(key_running)
    query_total = z_total(query_parts)
    query_base = ctx_running(query_total, ctx, False, BF16, True)
    query_running = z_running(query_parts, query_base, False)
    prefix, query_running = lax.optimization_barrier((prefix, query_running))
    suffix = from_owners(query_running)
    grad_queries, dfk, gv, query_sum = call(
        query_grad_kernel, 8, "wwwwrs", "wffr", (queries, keys, values, out_grad, z, prefix)
    )
    later = ctx_running(query_sum, ctx, False, F32, False)
    suffix, both = lax.optimization_barrier((suffix, jnp.stack([query_sum, later])))
    sums = z_gather(both, group)
    dfk, grad_values = call(key_grad_kernel, 16, "wwffs", "fw", (keys, values, dfk, gv, suffix))
    r = jnp.sum(sums[:, 1], axis=0) + jnp.sum(jnp.where(ranks > place, sums[:, 0], 0.0), axis=0)
    (grad_keys,) = call(key_finish_kernel, 16, "wfr", "w", (keys, dfk, r))
    return grad_queries, grad_keys, grad_values


def solution(mesh):
    spec = P(("ctx", "head"), None)
    body = functools.partial(shards, mesh.shape["ctx"], mesh.shape["head"])

    return jax.shard_map(
        body, mesh=mesh, in_specs=(spec,) * 4, out_specs=(spec,) * 3, check_vma=False
    )
```

time: 332 us -> 192 us (0.58)
  the two profiles are of different devices: /device:TPU:1 before, /device:TPU:6 now
where the time goes in v1:
time: 192 us; the launch traced here: 191 us
  waiting for transfers between devices  95.2 us (50%)
  starting transfers between devices  52.1 us (27%)
  Pallas kernels  32.4 us (17%)
  other arithmetic  6.81 us (4%)
  local copies, waits for them, and re-layouts  4.09 us (2%)
    ppermute x16, waiting for transfers between devices, hop(): return lax.ppermute(value, 'ctx', pairs)  57.6 us
    pallas_call x5, Pallas kernels, head_call(): pl.pallas_call(functools.partial(kernel, step), grid=(heads // step,), in...  23.4 us
    ppermute x16, starting transfers between devices, hop(): return lax.ppermute(value, 'ctx', pairs)  21.1 us
    all_to_all x2, starting transfers between devices, z_gather(): lax.all_to_all(jnp.broadcast_to(x[None], (group, *x.shape)), 'head', 0, 0...  15.6 us
    all_to_all x2, waiting for transfers between devices, z_gather(): lax.all_to_all(jnp.broadcast_to(x[None], (group, *x.shape)), 'head', 0, 0...  14.7 us
    ppermute x6, waiting for transfers between devices, swap_cores(): return lax.ppermute(value, 'ctx', [(i, i ^ 1) for i in range(ctx)])  8.69 us
    all_to_all x2, waiting for transfers between devices, to_owners(): lax.all_to_all(state.reshape(group, owned, HD), 'head', 0, 0, tiled=True)  8.56 us
    all_to_all x2, starting transfers between devices, to_owners(): lax.all_to_all(state.reshape(group, owned, HD), 'head', 0, 0, tiled=True)  8 us
  transfers between devices with their start and end apart: 28, of which 25 were waited for; matrix products, arithmetic and copies ran while one was open for 2% of the time, Pallas kernels for 12%

profile of v1, /device:TPU:6, one launch (start us, length us, event | category | flops | bytes accessed | tf_op | source)
XLA Modules:
  0.0 191.5 jit_solution(16016797163635641943)
XLA Ops:
  0.6 3.2 %shard_map.67 = (bf16[32,128,128]{2,1,0:T(8,128)(2,1)}, f32[32,128]{1,0:T(8,128)}) custom-call(bf16[128,4096]{1,0:T(8,128)(2,1)} %k_ref.9, bf16[128,4096]{1,0:T(8,128)(2,1)} %v_ref.5), custom_call_target="tpu_custom_call" | custom-call | tf_op jit(solution)/shard_map/pallas_call | solution.py:146
  3.9 1.4 broadcast_in_dim.65
  5.2 8.5 %all-to-all-start = ((f32[8,32,128]{2,1,0:T(8,128)}), f32[8,32,128]{2,1,0:T(8,128)S(1)}, u32[]{:S(2)}, u32[]{:S(2)}) async-start(f32[8,32,128]{2,1,0:T(8,128)} %broadcast_in_dim.65), calls=%async_computation | async-start | bytes 262144 | tf_op jit(solution)/shard_map/all_to_all | solution.py:262
  13.7 9.1 %all-to-all-done = f32[8,32,128]{2,1,0:T(8,128)S(1)} async-done(((f32[8,32,128]{2,1,0:T(8,128)}), f32[8,32,128]{2,1,0:T(8,128)S(1)}, u32[]{:S(2)}, u32[]{:S(2)}) %all-to-all-start) | async-done | bytes 131104 | tf_op jit(solution)/shard_map/all_to_all | solution.py:262
  22.9 3.6 %all-to-all-start.1 = ((bf16[8,512,128]{2,1,0:T(8,128)(2,1)}), bf16[8,512,128]{2,1,0:T(8,128)(2,1)S(1)}, u32[]{:S(2)}, u32[]{:S(2)}) async-start(bf16[8,512,128]{2,1,0:T(8,128)(2,1)} %bitcast.81), calls=%async_computation.1 | async-start | bytes 2097152 | tf_op jit(solution)/shard_map/all_to_all | solution.py:273
  26.6 1.2 collective-permute-done
  27.7 1.6 collective-permute-start.1
  29.3 3.4 %collective-permute-done.1 = f32[32,128]{1,0:T(8,128)S(1)} collective-permute-done((f32[32,128]{1,0:T(8,128)S(1)}, f32[32,128]{1,0:T(8,128)S(1)}, u32[]{:S(2)}, u32[]{:S(2)}) %collective-permute-start.1) | collective-permute-done | bytes 16416 | tf_op jit(solution)/shard_map/ppermute | solution.py:233
  32.7 2.1 %collective-permute-start.2 = (f32[2,32,128]{2,1,0:T(8,128)S(1)}, f32[2,32,128]{2,1,0:T(8,128)S(1)}, u32[]{:S(2)}, u32[]{:S(2)}) collective-permute-start(f32[2,32,128]{2,1,0:T(8,128)S(1)} %pad_maximum_fusion.2), channel_id=1, source_target_pairs={{0,32},{8,40},{16,48},{24,56},{32,0},{40,8},{48,16},{56,24},{64,96... | collective-permute-start | bytes 98312 | tf_op jit(solution)/shard_map/ppermute | solution.py:233
  34.8 3.4 %collective-permute-done.2 = f32[2,32,128]{2,1,0:T(8,128)S(1)} collective-permute-done((f32[2,32,128]{2,1,0:T(8,128)S(1)}, f32[2,32,128]{2,1,0:T(8,128)S(1)}, u32[]{:S(2)}, u32[]{:S(2)}) %collective-permute-start.2) | collective-permute-done | bytes 32800 | tf_op jit(solution)/shard_map/ppermute | solution.py:233
  38.7 3.3 %collective-permute-done.3 = f32[32,128]{1,0:T(8,128)S(1)} collective-permute-done((f32[32,128]{1,0:T(8,128)S(1)}, f32[32,128]{1,0:T(8,128)S(1)}, u32[]{:S(2)}, u32[]{:S(2)}) %collective-permute-start.3) | collective-permute-done | bytes 16416 | tf_op jit(solution)/shard_map/ppermute | solution.py:233
  41.9 1.4 collective-permute-start.4
  43.4 3.8 %collective-permute-done.4 = f32[32,128]{1,0:T(8,128)S(1)} collective-permute-done((f32[32,128]{1,0:T(8,128)S(1)}, f32[32,128]{1,0:T(8,128)S(1)}, u32[]{:S(2)}, u32[]{:S(2)}) %collective-permute-start.4) | collective-permute-done | bytes 16416 | tf_op jit(solution)/shard_map/ppermute | solution.py:233
  47.2 0.6 fusion.31.z_ref
  47.8 4.5 %shard_map.68 = bf16[32,128,128]{2,1,0:T(8,128)(2,1)} custom-call(bf16[128,4096]{1,0:T(8,128)(2,1)} %q_ref.3, bf16[128,4096]{1,0:T(8,128)(2,1)} %k_ref.9, bf16[128,4096]{1,0:T(8,128)(2,1)} %g_ref.3, f32[32,128]{1,0:T(8,128)} %fusion.31.z_ref), custom_call_target="tpu_custom_call" | custom-call | tf_op jit(solution)/shard_map/pallas_call | solution.py:146
  52.3 1.4 all-to-all-done.1.x_ref
  53.8 1.0 copy-done
  54.7 2.1 %shard_map.69 = f32[512,128]{1,0:T(8,128)} custom-call(bf16[8,512,128]{2,1,0:T(8,128)(2,1)} %copy-done), custom_call_target="tpu_custom_call" | custom-call | tf_op jit(solution)/shard_map/pallas_call | solution.py:175
  56.8 1.7 collective-permute-done.5
  58.5 1.0 add.141
  59.5 1.7 collective-permute-start.6
  61.2 4.4 %all-to-all-start.2 = ((bf16[8,512,128]{2,1,0:T(8,128)(2,1)}), bf16[8,512,128]{2,1,0:T(8,128)(2,1)S(1)}, u32[]{:S(2)}, u32[]{:S(2)}) async-start(bf16[8,512,128]{2,1,0:T(8,128)(2,1)} %bitcast.5), calls=%async_computation.2 | async-start | bytes 2097152 | tf_op jit(solution)/shard_map/all_to_all | solution.py:273
  65.7 3.0 %collective-permute-start.7 = (bf16[2,256,128]{2,1,0:T(8,128)(2,1)S(1)}, bf16[2,256,128]{2,1,0:T(8,128)(2,1)S(1)}, u32[]{:S(2)}, u32[]{:S(2)}) collective-permute-start(bf16[2,256,128]{2,1,0:T(8,128)(2,1)S(1)} %pad_maximum_fusion), channel_id=1, source_target_pairs={{0,32},{8,40},{16,48},{24,56},{32,0},{40,8},{48,16},{56,24},{64,96... | collective-permute-start | bytes 393224 | tf_op jit(solution)/shard_map/ppermute | solution.py:233
  68.7 3.6 %collective-permute-done.7 = bf16[2,256,128]{2,1,0:T(8,128)(2,1)S(1)} collective-permute-done((bf16[2,256,128]{2,1,0:T(8,128)(2,1)S(1)}, bf16[2,256,128]{2,1,0:T(8,128)(2,1)S(1)}, u32[]{:S(2)}, u32[]{:S(2)}) %collective-permute-start.7) | collective-permute-done | bytes 131104 | tf_op jit(solution)/shard_map/ppermute | solution.py:233
  72.3 1.8 collective-permute-start.8
  74.1 2.6 %collective-permute-done.8 = bf16[256,128]{1,0:T(8,128)(2,1)S(1)} collective-permute-done((bf16[256,128]{1,0:T(8,128)(2,1)S(1)}, bf16[256,128]{1,0:T(8,128)(2,1)S(1)}, u32[]{:S(2)}, u32[]{:S(2)}) %collective-permute-start.8) | collective-permute-done | bytes 65568 | tf_op jit(solution)/shard_map/ppermute | solution.py:233
  76.7 1.5 collective-permute-start.9
  78.2 4.4 %collective-permute-done.9 = bf16[256,128]{1,0:T(8,128)(2,1)S(1)} collective-permute-done((bf16[256,128]{1,0:T(8,128)(2,1)S(1)}, bf16[256,128]{1,0:T(8,128)(2,1)S(1)}, u32[]{:S(2)}, u32[]{:S(2)}) %collective-permute-start.9) | collective-permute-done | bytes 65568 | tf_op jit(solution)/shard_map/ppermute | solution.py:233
  82.7 1.3 collective-permute-done.10
  84.1 0.7 maximum_add_fusion.base_ref
  84.8 2.4 %shard_map.70 = bf16[8,512,128]{2,1,0:T(8,128)(2,1)} custom-call(bf16[8,512,128]{2,1,0:T(8,128)(2,1)} %copy-done, f32[512,128]{1,0:T(8,128)} %maximum_add_fusion.base_ref), custom_call_target="tpu_custom_call" | custom-call | tf_op jit(solution)/shard_map/pallas_call | solution.py:186
  87.2 7.1 %all-to-all-done.2.x_ref = bf16[8,512,128]{2,1,0:T(8,128)(2,1)S(1)} async-done(((bf16[8,512,128]{2,1,0:T(8,128)(2,1)}), bf16[8,512,128]{2,1,0:T(8,128)(2,1)S(1)}, u32[]{:S(2)}, u32[]{:S(2)}) %all-to-all-start.2) | async-done | bytes 1048608 | tf_op jit(solution)/shard_map/all_to_all | solution.py:273
  94.4 1.0 copy-done.1
  95.3 2.1 %shard_map.71 = f32[512,128]{1,0:T(8,128)} custom-call(bf16[8,512,128]{2,1,0:T(8,128)(2,1)} %copy-done.1), custom_call_target="tpu_custom_call" | custom-call | tf_op jit(solution)/shard_map/pallas_call | solution.py:175
  97.4 1.7 collective-permute-done.11
  99.2 1.0 add.150
  100.2 2.9 %collective-permute-start.12 = (bf16[256,128]{1,0:T(8,128)(2,1)S(1)}, bf16[256,128]{1,0:T(8,128)(2,1)S(1)}, u32[]{:S(2)}, u32[]{:S(2)}) collective-permute-start(bf16[256,128]{1,0:T(8,128)(2,1)S(1)} %get-tuple-element.43), channel_id=1, source_target_pairs={{0,48},{8,56},{16,0},{24,8},{32,16},{40,24},{48,32},{56,40},{64,11... | collective-permute-start | bytes 196616 | tf_op jit(solution)/shard_map/ppermute | solution.py:233
  103.1 3.6 %all-to-all-start.3 = ((bf16[8,512,128]{2,1,0:T(8,128)(2,1)}), bf16[8,512,128]{2,1,0:T(8,128)(2,1)S(1)}, u32[]{:S(2)}, u32[]{:S(2)}) async-start(bf16[8,512,128]{2,1,0:T(8,128)(2,1)} %shard_map.70), calls=%async_computation.3 | async-start | bytes 2097152 | tf_op jit(solution)/shard_map/all_to_all | solution.py:276
  106.7 1.1 collective-permute-start.13
  107.8 6.0 %collective-permute-done.13 = bf16[2,256,128]{2,1,0:T(8,128)(2,1)S(1)} collective-permute-done((bf16[2,256,128]{2,1,0:T(8,128)(2,1)S(1)}, bf16[2,256,128]{2,1,0:T(8,128)(2,1)S(1)}, u32[]{:S(2)}, u32[]{:S(2)}) %collective-permute-start.13) | collective-permute-done | bytes 131104 | tf_op jit(solution)/shard_map/ppermute | solution.py:233
  113.8 0.9 collective-permute-start.14
  114.7 4.6 %collective-permute-done.14 = bf16[256,128]{1,0:T(8,128)(2,1)S(1)} collective-permute-done((bf16[256,128]{1,0:T(8,128)(2,1)S(1)}, bf16[256,128]{1,0:T(8,128)(2,1)S(1)}, u32[]{:S(2)}, u32[]{:S(2)}) %collective-permute-start.14) | collective-permute-done | bytes 65568 | tf_op jit(solution)/shard_map/ppermute | solution.py:233
  119.7 5.6 %collective-permute-done.15 = bf16[256,128]{1,0:T(8,128)(2,1)S(1)} collective-permute-done((bf16[256,128]{1,0:T(8,128)(2,1)S(1)}, bf16[256,128]{1,0:T(8,128)(2,1)S(1)}, u32[]{:S(2)}, u32[]{:S(2)}) %collective-permute-start.15) | collective-permute-done | bytes 65568 | tf_op jit(solution)/shard_map/ppermute | solution.py:233
  125.4 1.3 collective-permute-done.16
  126.8 0.7 maximum_add_fusion.1.base_ref
  127.5 2.5 %shard_map.72 = bf16[8,512,128]{2,1,0:T(8,128)(2,1)} custom-call(bf16[8,512,128]{2,1,0:T(8,128)(2,1)} %copy-done.1, f32[512,128]{1,0:T(8,128)} %maximum_add_fusion.1.base_ref), custom_call_target="tpu_custom_call" | custom-call | tf_op jit(solution)/shard_map/pallas_call | solution.py:186
  130.0 5.7 %all-to-all-done.3 = bf16[8,512,128]{2,1,0:T(8,128)(2,1)S(1)} async-done(((bf16[8,512,128]{2,1,0:T(8,128)(2,1)}), bf16[8,512,128]{2,1,0:T(8,128)(2,1)S(1)}, u32[]{:S(2)}, u32[]{:S(2)}) %all-to-all-start.3) | async-done | bytes 1048608 | tf_op jit(solution)/shard_map/all_to_all | solution.py:276
  135.7 3.6 %all-to-all-start.4 = ((bf16[8,512,128]{2,1,0:T(8,128)(2,1)}), bf16[8,512,128]{2,1,0:T(8,128)(2,1)S(1)}, u32[]{:S(2)}, u32[]{:S(2)}) async-start(bf16[8,512,128]{2,1,0:T(8,128)(2,1)} %shard_map.72), calls=%async_computation.4 | async-start | bytes 2097152 | tf_op jit(solution)/shard_map/all_to_all | solution.py:276
  139.2 7.9 %shard_map.73 = (bf16[128,4096]{1,0:T(8,128)(2,1)}, f32[128,4096]{1,0:T(8,128)}, f32[128,4096]{1,0:T(8,128)}, f32[32,128]{1,0:T(8,128)}) custom-call(bf16[128,4096]{1,0:T(8,128)(2,1)} %q_ref.3, bf16[128,4096]{1,0:T(8,128)(2,1)} %k_ref.9, bf16[128,4096]{1,0:T(8,128)(2,1)} %v_ref.5, bf16[128,4096]{1,0:T(8,128)(2,1)} %g_ref.3, f32[32,128]{1,0:T(8,128)} %fusion.31.z_ref, ...), custom_call_target="tpu_custom_call" | custom-call | tf_op jit(solution)/shard_map/pallas_call | solution.py:146
  147.1 1.4 collective-permute-done.17
  148.5 0.7 add.159
  149.2 0.6 collective-permute-start.18
  149.8 3.1 %collective-permute-done.18 = f32[32,128]{1,0:T(8,128)S(1)} collective-permute-done((f32[32,128]{1,0:T(8,128)S(1)}, f32[32,128]{1,0:T(8,128)S(1)}, u32[]{:S(2)}, u32[]{:S(2)}) %collective-permute-start.18) | collective-permute-done | bytes 16416 | tf_op jit(solution)/shard_map/ppermute | solution.py:233
  153.0 0.9 collective-permute-start.19
  153.8 4.6 %collective-permute-done.19 = f32[2,32,128]{2,1,0:T(8,128)S(1)} collective-permute-done((f32[2,32,128]{2,1,0:T(8,128)S(1)}, f32[2,32,128]{2,1,0:T(8,128)S(1)}, u32[]{:S(2)}, u32[]{:S(2)}) %collective-permute-start.19) | collective-permute-done | bytes 32800 | tf_op jit(solution)/shard_map/ppermute | solution.py:233
  158.5 0.8 collective-permute-start.20
  159.3 4.1 %collective-permute-done.20 = f32[32,128]{1,0:T(8,128)S(1)} collective-permute-done((f32[32,128]{1,0:T(8,128)S(1)}, f32[32,128]{1,0:T(8,128)S(1)}, u32[]{:S(2)}, u32[]{:S(2)}) %collective-permute-start.20) | collective-permute-done | bytes 16416 | tf_op jit(solution)/shard_map/ppermute | solution.py:233
  163.6 5.1 %collective-permute-done.21 = f32[32,128]{1,0:T(8,128)S(1)} collective-permute-done((f32[32,128]{1,0:T(8,128)S(1)}, f32[32,128]{1,0:T(8,128)S(1)}, u32[]{:S(2)}, u32[]{:S(2)}) %collective-permute-start.21) | collective-permute-done | bytes 16416 | tf_op jit(solution)/shard_map/ppermute | solution.py:233
  168.7 0.7 pad_maximum_fusion.4
  169.4 0.8 broadcast_in_dim.72
  170.2 7.1 %all-to-all-start.5 = ((f32[8,2,32,128]{3,2,1,0:T(8,128)}), f32[8,2,32,128]{3,2,1,0:T(8,128)S(1)}, u32[]{:S(2)}, u32[]{:S(2)}) async-start(f32[8,2,32,128]{3,2,1,0:T(8,128)} %broadcast_in_dim.72), calls=%async_computation.5 | async-start | bytes 524288 | tf_op jit(solution)/shard_map/all_to_all | solution.py:262
  177.3 4.8 %shard_map.74 = (f32[128,4096]{1,0:T(8,128)}, bf16[128,4096]{1,0:T(8,128)(2,1)}) custom-call(bf16[128,4096]{1,0:T(8,128)(2,1)} %k_ref.9, bf16[128,4096]{1,0:T(8,128)(2,1)} %v_ref.5, f32[128,4096]{1,0:T(8,128)} %get-tuple-element.33.dfk_ref, f32[128,4096]{1,0:T(8,128)} %get-tuple-element.34.gv_ref, bf16[32,128,128]{2,1,0:T(8,128)(2,1)} %bitcast.80), custom_call_target="tpu_custom_call" | custom-call | tf_op jit(solution)/shard_map/pallas_call | solution.py:146
  182.1 5.7 %all-to-all-done.5 = f32[8,2,32,128]{3,2,1,0:T(8,128)S(1)} async-done(((f32[8,2,32,128]{3,2,1,0:T(8,128)}), f32[8,2,32,128]{3,2,1,0:T(8,128)S(1)}, u32[]{:S(2)}, u32[]{:S(2)}) %all-to-all-start.5) | async-done | bytes 262176 | tf_op jit(solution)/shard_map/all_to_all | solution.py:262
  188.5 3.0 %shard_map.75 = bf16[128,4096]{1,0:T(8,128)(2,1)} custom-call(bf16[128,4096]{1,0:T(8,128)(2,1)} %k_ref.9, f32[128,4096]{1,0:T(8,128)} %get-tuple-element.38.dfk_ref, f32[32,128]{1,0:T(8,128)} %add.168.rz_ref), custom_call_target="tpu_custom_call" | custom-call | tf_op jit(solution)/shard_map/pallas_call | solution.py:146
  (50 shorter events, 2.6 us)
Async XLA Ops:
  5.2 17.6 %all-to-all-start = ((f32[8,32,128]{2,1,0:T(8,128)}), f32[8,32,128]{2,1,0:T(8,128)S(1)}, u32[]{:S(2)}, u32[]{:S(2)}) async-start(f32[8,32,128]{2,1,0:T(8,128)} %broadcast_in_dim.65), calls=%async_computation | async-start | bytes 262144 | tf_op jit(solution)/shard_map/all_to_all | solution.py:262
  22.9 30.9 %all-to-all-start.1 = ((bf16[8,512,128]{2,1,0:T(8,128)(2,1)}), bf16[8,512,128]{2,1,0:T(8,128)(2,1)S(1)}, u32[]{:S(2)}, u32[]{:S(2)}) async-start(bf16[8,512,128]{2,1,0:T(8,128)(2,1)} %bitcast.81), calls=%async_computation.1 | async-start | bytes 2097152 | tf_op jit(solution)/shard_map/all_to_all | solution.py:273
  26.5 1.3 collective-permute-start
  27.7 4.9 %collective-permute-start.1 = (f32[32,128]{1,0:T(8,128)S(1)}, f32[32,128]{1,0:T(8,128)S(1)}, u32[]{:S(2)}, u32[]{:S(2)}) collective-permute-start(f32[32,128]{1,0:T(8,128)S(1)} %add.131), channel_id=1, source_target_pairs={{0,16},{8,24},{16,32},{24,40},{32,48},{40,56},{48,0},{56,8},{64,80... | collective-permute-start | bytes 49160 | tf_op jit(solution)/shard_map/ppermute | solution.py:233
  32.7 5.5 %collective-permute-start.2 = (f32[2,32,128]{2,1,0:T(8,128)S(1)}, f32[2,32,128]{2,1,0:T(8,128)S(1)}, u32[]{:S(2)}, u32[]{:S(2)}) collective-permute-start(f32[2,32,128]{2,1,0:T(8,128)S(1)} %pad_maximum_fusion.2), channel_id=1, source_target_pairs={{0,32},{8,40},{16,48},{24,56},{32,0},{40,8},{48,16},{56,24},{64,96... | collective-permute-start | bytes 98312 | tf_op jit(solution)/shard_map/ppermute | solution.py:233
  38.2 3.7 %collective-permute-start.3 = (f32[32,128]{1,0:T(8,128)S(1)}, f32[32,128]{1,0:T(8,128)S(1)}, u32[]{:S(2)}, u32[]{:S(2)}) collective-permute-start(f32[32,128]{1,0:T(8,128)S(1)} %fusion.26), channel_id=1, source_target_pairs={{0,64},{8,72},{16,80},{24,88},{32,96},{40,104},{48,112},{56,120},{... | collective-permute-start | bytes 49160 | tf_op jit(solution)/shard_map/ppermute | solution.py:233
  41.9 5.2 %collective-permute-start.4 = (f32[32,128]{1,0:T(8,128)S(1)}, f32[32,128]{1,0:T(8,128)S(1)}, u32[]{:S(2)}, u32[]{:S(2)}) collective-permute-start(f32[32,128]{1,0:T(8,128)S(1)} %select_add_fusion.1), channel_id=1, source_target_pairs={{0,128},{8,136},{16,144},{24,152},{32,160},{40,168},{48,176},{56,1... | collective-permute-start | bytes 49160 | tf_op jit(solution)/shard_map/ppermute | solution.py:233
  53.8 1.0 copy-start
  56.8 1.7 collective-permute-start.5
  59.5 6.1 %collective-permute-start.6 = (bf16[256,128]{1,0:T(8,128)(2,1)S(1)}, bf16[256,128]{1,0:T(8,128)(2,1)S(1)}, u32[]{:S(2)}, u32[]{:S(2)}) collective-permute-start(bf16[256,128]{1,0:T(8,128)(2,1)S(1)} %get-tuple-element.45), channel_id=1, source_target_pairs={{0,16},{8,24},{16,32},{24,40},{32,48},{40,56},{48,0},{56,8},{64,80... | collective-permute-start | bytes 196616 | tf_op jit(solution)/shard_map/ppermute | solution.py:233
  61.2 33.2 %all-to-all-start.2 = ((bf16[8,512,128]{2,1,0:T(8,128)(2,1)}), bf16[8,512,128]{2,1,0:T(8,128)(2,1)S(1)}, u32[]{:S(2)}, u32[]{:S(2)}) async-start(bf16[8,512,128]{2,1,0:T(8,128)(2,1)} %bitcast.5), calls=%async_computation.2 | async-start | bytes 2097152 | tf_op jit(solution)/shard_map/all_to_all | solution.py:273
  65.7 6.6 %collective-permute-start.7 = (bf16[2,256,128]{2,1,0:T(8,128)(2,1)S(1)}, bf16[2,256,128]{2,1,0:T(8,128)(2,1)S(1)}, u32[]{:S(2)}, u32[]{:S(2)}) collective-permute-start(bf16[2,256,128]{2,1,0:T(8,128)(2,1)S(1)} %pad_maximum_fusion), channel_id=1, source_target_pairs={{0,32},{8,40},{16,48},{24,56},{32,0},{40,8},{48,16},{56,24},{64,96... | collective-permute-start | bytes 393224 | tf_op jit(solution)/shard_map/ppermute | solution.py:233
  72.3 4.3 %collective-permute-start.8 = (bf16[256,128]{1,0:T(8,128)(2,1)S(1)}, bf16[256,128]{1,0:T(8,128)(2,1)S(1)}, u32[]{:S(2)}, u32[]{:S(2)}) collective-permute-start(bf16[256,128]{1,0:T(8,128)(2,1)S(1)} %fusion.32), channel_id=1, source_target_pairs={{0,64},{8,72},{16,80},{24,88},{32,96},{40,104},{48,112},{56,120},{... | collective-permute-start | bytes 196616 | tf_op jit(solution)/shard_map/ppermute | solution.py:233
  76.7 5.9 %collective-permute-start.9 = (bf16[256,128]{1,0:T(8,128)(2,1)S(1)}, bf16[256,128]{1,0:T(8,128)(2,1)S(1)}, u32[]{:S(2)}, u32[]{:S(2)}) collective-permute-start(bf16[256,128]{1,0:T(8,128)(2,1)S(1)} %add_convert_fusion.1), channel_id=1, source_target_pairs={{0,128},{8,136},{16,144},{24,152},{32,160},{40,168},{48,176},{56,1... | collective-permute-start | bytes 196616 | tf_op jit(solution)/shard_map/ppermute | solution.py:233
  82.6 1.4 collective-permute-start.10
  94.4 1.0 copy-start.1
  97.4 1.7 collective-permute-start.11
  100.2 6.5 %collective-permute-start.12 = (bf16[256,128]{1,0:T(8,128)(2,1)S(1)}, bf16[256,128]{1,0:T(8,128)(2,1)S(1)}, u32[]{:S(2)}, u32[]{:S(2)}) collective-permute-start(bf16[256,128]{1,0:T(8,128)(2,1)S(1)} %get-tuple-element.43), channel_id=1, source_target_pairs={{0,48},{8,56},{16,0},{24,8},{32,16},{40,24},{48,32},{56,40},{64,11... | collective-permute-start | bytes 196616 | tf_op jit(solution)/shard_map/ppermute | solution.py:233
  103.1 32.6 %all-to-all-start.3 = ((bf16[8,512,128]{2,1,0:T(8,128)(2,1)}), bf16[8,512,128]{2,1,0:T(8,128)(2,1)S(1)}, u32[]{:S(2)}, u32[]{:S(2)}) async-start(bf16[8,512,128]{2,1,0:T(8,128)(2,1)} %shard_map.70), calls=%async_computation.3 | async-start | bytes 2097152 | tf_op jit(solution)/shard_map/all_to_all | solution.py:276
  106.7 7.0 %collective-permute-start.13 = (bf16[2,256,128]{2,1,0:T(8,128)(2,1)S(1)}, bf16[2,256,128]{2,1,0:T(8,128)(2,1)S(1)}, u32[]{:S(2)}, u32[]{:S(2)}) collective-permute-start(bf16[2,256,128]{2,1,0:T(8,128)(2,1)S(1)} %pad_maximum_fusion.1), channel_id=1, source_target_pairs={{0,32},{8,40},{16,48},{24,56},{32,0},{40,8},{48,16},{56,24},{64,96... | collective-permute-start | bytes 393224 | tf_op jit(solution)/shard_map/ppermute | solution.py:233
  113.8 5.6 %collective-permute-start.14 = (bf16[256,128]{1,0:T(8,128)(2,1)S(1)}, bf16[256,128]{1,0:T(8,128)(2,1)S(1)}, u32[]{:S(2)}, u32[]{:S(2)}) collective-permute-start(bf16[256,128]{1,0:T(8,128)(2,1)S(1)} %fusion.33), channel_id=1, source_target_pairs={{0,192},{8,200},{16,208},{24,216},{32,224},{40,232},{48,240},{56,2... | collective-permute-start | bytes 196616 | tf_op jit(solution)/shard_map/ppermute | solution.py:233
  119.4 5.9 %collective-permute-start.15 = (bf16[256,128]{1,0:T(8,128)(2,1)S(1)}, bf16[256,128]{1,0:T(8,128)(2,1)S(1)}, u32[]{:S(2)}, u32[]{:S(2)}) collective-permute-start(bf16[256,128]{1,0:T(8,128)(2,1)S(1)} %add_convert_fusion), channel_id=1, source_target_pairs={{0,128},{8,136},{16,144},{24,152},{32,160},{40,168},{48,176},{56,1... | collective-permute-start | bytes 196616 | tf_op jit(solution)/shard_map/ppermute | solution.py:233
  125.3 1.4 collective-permute-start.16
  135.7 3.6 %copy-start.2 = (bf16[8,512,128]{2,1,0:T(8,128)(2,1)}, bf16[8,512,128]{2,1,0:T(8,128)(2,1)S(1)}, u32[]{:S(2)}) copy-start(bf16[8,512,128]{2,1,0:T(8,128)(2,1)S(1)} %all-to-all-done.3) | copy-start | bytes 3145732
  135.7 33.8 %all-to-all-start.4 = ((bf16[8,512,128]{2,1,0:T(8,128)(2,1)}), bf16[8,512,128]{2,1,0:T(8,128)(2,1)S(1)}, u32[]{:S(2)}, u32[]{:S(2)}) async-start(bf16[8,512,128]{2,1,0:T(8,128)(2,1)} %shard_map.72), calls=%async_computation.4 | async-start | bytes 2097152 | tf_op jit(solution)/shard_map/all_to_all | solution.py:276
  147.1 1.4 collective-permute-start.17
  149.2 3.7 %collective-permute-start.18 = (f32[32,128]{1,0:T(8,128)S(1)}, f32[32,128]{1,0:T(8,128)S(1)}, u32[]{:S(2)}, u32[]{:S(2)}) collective-permute-start(f32[32,128]{1,0:T(8,128)S(1)} %add.159), channel_id=1, source_target_pairs={{0,48},{8,56},{16,0},{24,8},{32,16},{40,24},{48,32},{56,40},{64,11... | collective-permute-start | bytes 49160 | tf_op jit(solution)/shard_map/ppermute | solution.py:233
  153.0 5.5 %collective-permute-start.19 = (f32[2,32,128]{2,1,0:T(8,128)S(1)}, f32[2,32,128]{2,1,0:T(8,128)S(1)}, u32[]{:S(2)}, u32[]{:S(2)}) collective-permute-start(f32[2,32,128]{2,1,0:T(8,128)S(1)} %pad_maximum_fusion.3), channel_id=1, source_target_pairs={{0,32},{8,40},{16,48},{24,56},{32,0},{40,8},{48,16},{56,24},{64,96... | collective-permute-start | bytes 98312 | tf_op jit(solution)/shard_map/ppermute | solution.py:233
  158.5 4.9 %collective-permute-start.20 = (f32[32,128]{1,0:T(8,128)S(1)}, f32[32,128]{1,0:T(8,128)S(1)}, u32[]{:S(2)}, u32[]{:S(2)}) collective-permute-start(f32[32,128]{1,0:T(8,128)S(1)} %fusion.20), channel_id=1, source_target_pairs={{0,192},{8,200},{16,208},{24,216},{32,224},{40,232},{48,240},{56,2... | collective-permute-start | bytes 49160 | tf_op jit(solution)/shard_map/ppermute | solution.py:233
  163.4 5.2 %collective-permute-start.21 = (f32[32,128]{1,0:T(8,128)S(1)}, f32[32,128]{1,0:T(8,128)S(1)}, u32[]{:S(2)}, u32[]{:S(2)}) collective-permute-start(f32[32,128]{1,0:T(8,128)S(1)} %select_add_fusion), channel_id=1, source_target_pairs={{0,128},{8,136},{16,144},{24,152},{32,160},{40,168},{48,176},{56,1... | collective-permute-start | bytes 49160 | tf_op jit(solution)/shard_map/ppermute | solution.py:233
  169.4 7.9 %copy-start.3 = (bf16[8,512,128]{2,1,0:T(8,128)(2,1)}, bf16[8,512,128]{2,1,0:T(8,128)(2,1)S(1)}, u32[]{:S(2)}) copy-start(bf16[8,512,128]{2,1,0:T(8,128)(2,1)S(1)} %all-to-all-done.4) | copy-start | bytes 3145732
  170.2 17.6 %all-to-all-start.5 = ((f32[8,2,32,128]{3,2,1,0:T(8,128)}), f32[8,2,32,128]{3,2,1,0:T(8,128)S(1)}, u32[]{:S(2)}, u32[]{:S(2)}) async-start(f32[8,2,32,128]{3,2,1,0:T(8,128)} %broadcast_in_dim.72), calls=%async_computation.5 | async-start | bytes 524288 | tf_op jit(solution)/shard_map/all_to_all | solution.py:262

commit v2 on v1

--- a/solution.py
+++ b/solution.py
@@ -15,10 +15,6 @@
 
 def feature(real):
     return jnp.where(real > 0, real + 1.0, jnp.exp(jnp.minimum(real, 0.0)))
-
-
-def slope(real):
-    return jnp.where(real > 0, 1.0, jnp.exp(jnp.minimum(real, 0.0)))
 
 
 def dot_nn(a, b):
@@ -84,7 +80,32 @@
         state_ref[j] = states[j].astype(BF16)
 
 
-def query_grad_kernel(step, q_ref, k_ref, v_ref, g_ref, z_ref, s_ref, gq_ref, dfk_ref, gv_ref, sum_ref):
+def num_of(fq, weights, v, s_ref):
+    return [dot_nn(w, x) + dot_nn(f, s_ref[j]) for j, (f, w, x) in enumerate(zip(fq, weights, v))]
+
+
+def dden_of(g_ref, num, inverse):
+    shared = [
+        jnp.sum(g_ref[:, columns(j)].astype(F32) * n, axis=1, keepdims=True)
+        for j, n in enumerate(num)
+    ]
+    return [-(s * i) * i for s, i in zip(shared, inverse)]
+
+
+def query_sum_kernel(step, q_ref, k_ref, v_ref, g_ref, z_ref, s_ref, sum_ref):
+    mask = causal(q_ref.shape[0])
+    heads = range(step)
+    fq = [feature(q_ref[:, columns(j)].astype(F32)).astype(BF16) for j in heads]
+    fk = [feature(k_ref[:, columns(j)].astype(F32)).astype(BF16) for j in heads]
+    weights, inverse = scores_of(fq, fk, [head_row(z_ref, step, j) for j in heads], mask)
+    num = num_of(fq, weights, [v_ref[:, columns(j)] for j in heads], s_ref)
+    dden = dden_of(g_ref, num, inverse)
+    for j in heads:
+        row = jnp.sum(dden[j] * fq[j].astype(F32), axis=0, keepdims=True)
+        put_head_row(sum_ref, step, j, row)
+
+
+def query_grad_kernel(step, q_ref, k_ref, v_ref, g_ref, z_ref, s_ref, gq_ref, dfk_ref, gv_ref):
     mask = causal(q_ref.shape[0])
     heads = range(step)
     fq32 = [feature(q_ref[:, columns(j)].astype(F32)) for j in heads]
@@ -93,18 +114,13 @@
     zrows = [head_row(z_ref, step, j) for j in heads]
     v = [v_ref[:, columns(j)] for j in heads]
     weights, inverse = scores_of(fq, fk, zrows, mask)
-    num = [dot_nn(weights[j], v[j]) + dot_nn(fq[j], s_ref[j]) for j in heads]
+    num = num_of(fq, weights, v, s_ref)
     dnum = [(g_ref[:, columns(j)].astype(F32) * inverse[j]).astype(BF16) for j in heads]
     pair = each(dot_nt, dnum, v)
-    shared = [
-        jnp.sum(g_ref[:, columns(j)].astype(F32) * num[j], axis=1, keepdims=True) for j in heads
-    ]
-    dden = [-(s * i) * i for s, i in zip(shared, inverse)]
+    dden = dden_of(g_ref, num, inverse)
     mixing = [jnp.where(mask, p + d, 0.0).astype(BF16) for p, d in zip(pair, dden)]
     for j in heads:
         gv_ref[:, columns(j)] = dot_tn(weights[j], dnum[j])
-    for j in heads:
-        put_head_row(sum_ref, step, j, jnp.sum(dden[j] * fq[j].astype(F32), axis=0, keepdims=True))
     dfq = [
         dot_nn(mixing[j], fk[j]) + dot_nt(dnum[j], s_ref[j]) + dden[j] * zrows[j] for j in heads
     ]
@@ -114,22 +130,18 @@
         dfk_ref[:, columns(j)] = dot_tn(mixing[j], fq[j])
 
 
-def key_grad_kernel(step, k_ref, v_ref, dfk_ref, gv_ref, rs_ref, dfk_out_ref, gv_out_ref):
-    heads = range(step)
-    fk = [feature(k_ref[:, columns(j)].astype(F32)).astype(BF16) for j in heads]
+def key_grad_kernel(step, k_ref, v_ref, dfk_ref, gv_ref, rs_ref, rz_ref, gk_ref, gv_out_ref):
+    heads = range(step)
+    fk32 = [feature(k_ref[:, columns(j)].astype(F32)) for j in heads]
+    dfk = [dot_nt(v_ref[:, columns(j)], rs_ref[j]) for j in heads]
+    gv = [dot_nn(fk32[j].astype(BF16), rs_ref[j]) for j in heads]
     for j in heads:
         c = columns(j)
-        dfk_out_ref[:, c] = dfk_ref[:, c] + dot_nt(v_ref[:, c], rs_ref[j])
+        whole = dfk[j] + dfk_ref[:, c] + head_row(rz_ref, step, j)
+        gk_ref[:, c] = (whole * jnp.minimum(fk32[j], 1.0)).astype(BF16)
     for j in heads:
         c = columns(j)
-        gv_out_ref[:, c] = (gv_ref[:, c] + dot_nn(fk[j], rs_ref[j])).astype(BF16)
-
-
-def key_finish_kernel(step, k_ref, dfk_ref, rz_ref, gk_ref):
-    for j in range(step):
-        c = columns(j)
-        dfk = dfk_ref[:, c] + head_row(rz_ref, step, j)
-        gk_ref[:, c] = (dfk * slope(k_ref[:, c].astype(F32))).astype(BF16)
+        gv_out_ref[:, c] = (gv[j] + gv_ref[:, c]).astype(BF16)
 
 
 def head_call(kernel, step, kinds_in, kinds_out, arrays, tokens, heads):
@@ -277,13 +289,12 @@
 
     ranks = jnp.arange(group)[:, None, None]
     key_state, key_sum = call(key_state_kernel, 16, "ww", "sr", (keys, values))
-    sums = z_gather(key_sum, group)
-    before = jnp.sum(jnp.where(ranks < place, sums, 0.0), axis=0)
-    key_state, before, total = lax.optimization_barrier((key_state, before, jnp.sum(sums, axis=0)))
     key_parts = to_owners(key_state)
-    z = before + ctx_running(total, ctx, True, F32, False)
+    earlier = ctx_running(key_sum, ctx, True, F32, False)
+    key_parts, both = lax.optimization_barrier((key_parts, jnp.stack([key_sum, earlier])))
+    sums = z_gather(both, group)
+    z = jnp.sum(sums[:, 1], axis=0) + jnp.sum(jnp.where(ranks < place, sums[:, 0], 0.0), axis=0)
     (query_state,) = call(query_state_kernel, 16, "wwwr", "s", (queries, keys, out_grad, z))
-    key_parts, query_state = lax.optimization_barrier((key_parts, query_state))
     query_parts = to_owners(query_state)
     key_total = z_total(key_parts)
     key_base = ctx_running(key_total, ctx, True, BF16, True)
@@ -293,17 +304,17 @@
     query_total = z_total(query_parts)
     query_base = ctx_running(query_total, ctx, False, BF16, True)
     query_running = z_running(query_parts, query_base, False)
-    prefix, query_running = lax.optimization_barrier((prefix, query_running))
+    locals_in = (queries, keys, values, out_grad, z, prefix)
+    (query_sum,) = call(query_sum_kernel, 16, "wwwwrs", "r", locals_in)
+    sums = z_gather(query_sum, group)
+    sums, query_running = lax.optimization_barrier((sums, query_running))
+    grad_queries, dfk, gv = call(query_grad_kernel, 8, "wwwwrs", "wff", locals_in)
     suffix = from_owners(query_running)
-    grad_queries, dfk, gv, query_sum = call(
-        query_grad_kernel, 8, "wwwwrs", "wffr", (queries, keys, values, out_grad, z, prefix)
+    r = ctx_running(jnp.sum(sums, axis=0), ctx, False, F32, False)
+    r = r + jnp.sum(jnp.where(ranks > place, sums, 0.0), axis=0)
+    grad_keys, grad_values = call(
+        key_grad_kernel, 16, "wwffsr", "ww", (keys, values, dfk, gv, suffix, r)
     )
-    later = ctx_running(query_sum, ctx, False, F32, False)
-    suffix, both = lax.optimization_barrier((suffix, jnp.stack([query_sum, later])))
-    sums = z_gather(both, group)
-    dfk, grad_values = call(key_grad_kernel, 16, "wwffs", "fw", (keys, values, dfk, gv, suffix))
-    r = jnp.sum(sums[:, 1], axis=0) + jnp.sum(jnp.where(ranks > place, sums[:, 0], 0.0), axis=0)
-    (grad_keys,) = call(key_finish_kernel, 16, "wfr", "w", (keys, dfk, r))
     return grad_queries, grad_keys, grad_values
 
 

time: 192 us -> 194 us (1.010)
  the two profiles are of different devices: /device:TPU:6 before, /device:TPU:1 now
where the time goes in v2:
time: 194 us
  waiting for transfers between devices  77 us (40%)
  starting transfers between devices  70.9 us (37%)
  Pallas kernels  34.3 us (18%)
  local copies, waits for them, and re-layouts  6.04 us (3%)
  other arithmetic  4.44 us (2%)
    ppermute x16, starting transfers between devices, hop(): return lax.ppermute(value, 'ctx', pairs)  33.5 us
    ppermute x16, waiting for transfers between devices, hop(): return lax.ppermute(value, 'ctx', pairs)  33.4 us
    pallas_call x5, Pallas kernels, head_call(): pl.pallas_call(functools.partial(kernel, step), grid=(heads // step,), in...  25.4 us
    all_to_all x2, waiting for transfers between devices, to_owners(): lax.all_to_all(state.reshape(group, owned, HD), 'head', 0, 0, tiled=True)  16 us
    all_to_all x2, waiting for transfers between devices, z_gather(): lax.all_to_all(jnp.broadcast_to(x[None], (group, *x.shape)), 'head', 0, 0...  14.8 us
    all_to_all x2, starting transfers between devices, to_owners(): lax.all_to_all(state.reshape(group, owned, HD), 'head', 0, 0, tiled=True)  12.7 us
    ppermute x6, starting transfers between devices, swap_cores(): return lax.ppermute(value, 'ctx', [(i, i ^ 1) for i in range(ctx)])  10.9 us
    all_to_all x2, waiting for transfers between devices, from_owners(): return lax.all_to_all(x, 'head', 0, 0, tiled=True).reshape(heads, HD, HD)  9.06 us
  transfers between devices with their start and end apart: 28, of which 24 were waited for; matrix products, arithmetic and copies ran while one was open for 3% of the time, Pallas kernels for 9%

profile of v2, /device:TPU:1, one launch (start us, length us, event | category | flops | bytes accessed | tf_op | source)
XLA Modules:
  0.0 193.6 jit_solution(8632285715953931016)
XLA Ops:
  0.6 3.2 %shard_map.67 = (bf16[32,128,128]{2,1,0:T(8,128)(2,1)}, f32[32,128]{1,0:T(8,128)}) custom-call(bf16[128,4096]{1,0:T(8,128)(2,1)} %k_ref.9, bf16[128,4096]{1,0:T(8,128)(2,1)} %v_ref.7), custom_call_target="tpu_custom_call" | custom-call | tf_op jit(solution)/shard_map/pallas_call | solution.py:158
  3.9 9.1 %all-to-all-start = ((bf16[8,512,128]{2,1,0:T(8,128)(2,1)}), bf16[8,512,128]{2,1,0:T(8,128)(2,1)S(1)}, u32[]{:S(2)}, u32[]{:S(2)}) async-start(bf16[8,512,128]{2,1,0:T(8,128)(2,1)} %bitcast.83), calls=%async_computation | async-start | bytes 2097152 | tf_op jit(solution)/shard_map/all_to_all | solution.py:285
  13.0 1.0 collective-permute-start
  14.9 1.3 collective-permute-start.1
  16.2 2.6 %collective-permute-done.1 = f32[32,128]{1,0:T(8,128)S(1)} collective-permute-done((f32[32,128]{1,0:T(8,128)S(1)}, f32[32,128]{1,0:T(8,128)S(1)}, u32[]{:S(2)}, u32[]{:S(2)}) %collective-permute-start.1) | collective-permute-done | bytes 16416 | tf_op jit(solution)/shard_map/ppermute | solution.py:245
  18.8 2.0 %collective-permute-start.2 = (f32[2,32,128]{2,1,0:T(8,128)S(1)}, f32[2,32,128]{2,1,0:T(8,128)S(1)}, u32[]{:S(2)}, u32[]{:S(2)}) collective-permute-start(f32[2,32,128]{2,1,0:T(8,128)S(1)} %pad_maximum_fusion.2), channel_id=1, source_target_pairs={{0,32},{8,40},{16,48},{24,56},{32,0},{40,8},{48,16},{56,24},{64,96... | collective-permute-start | bytes 98312 | tf_op jit(solution)/shard_map/ppermute | solution.py:245
  20.8 2.6 %collective-permute-done.2 = f32[2,32,128]{2,1,0:T(8,128)S(1)} collective-permute-done((f32[2,32,128]{2,1,0:T(8,128)S(1)}, f32[2,32,128]{2,1,0:T(8,128)S(1)}, u32[]{:S(2)}, u32[]{:S(2)}) %collective-permute-start.2) | collective-permute-done | bytes 32800 | tf_op jit(solution)/shard_map/ppermute | solution.py:245
  23.4 1.2 collective-permute-start.3
  24.6 2.9 %collective-permute-done.3 = f32[32,128]{1,0:T(8,128)S(1)} collective-permute-done((f32[32,128]{1,0:T(8,128)S(1)}, f32[32,128]{1,0:T(8,128)S(1)}, u32[]{:S(2)}, u32[]{:S(2)}) %collective-permute-start.3) | collective-permute-done | bytes 16416 | tf_op jit(solution)/shard_map/ppermute | solution.py:245
  27.5 1.5 collective-permute-start.4
  29.0 2.8 %collective-permute-done.4 = f32[32,128]{1,0:T(8,128)S(1)} collective-permute-done((f32[32,128]{1,0:T(8,128)S(1)}, f32[32,128]{1,0:T(8,128)S(1)}, u32[]{:S(2)}, u32[]{:S(2)}) %collective-permute-start.4) | collective-permute-done | bytes 16416 | tf_op jit(solution)/shard_map/ppermute | solution.py:245
  31.9 10.3 %all-to-all-done.x_ref = bf16[8,512,128]{2,1,0:T(8,128)(2,1)S(1)} async-done(((bf16[8,512,128]{2,1,0:T(8,128)(2,1)}), bf16[8,512,128]{2,1,0:T(8,128)(2,1)S(1)}, u32[]{:S(2)}, u32[]{:S(2)}) %all-to-all-start) | async-done | bytes 1048608 | tf_op jit(solution)/shard_map/all_to_all | solution.py:285
  42.2 1.0 copy-done.1
  43.1 2.1 %shard_map.69 = f32[512,128]{1,0:T(8,128)} custom-call(bf16[8,512,128]{2,1,0:T(8,128)(2,1)} %copy-done.1), custom_call_target="tpu_custom_call" | custom-call | tf_op jit(solution)/shard_map/pallas_call | solution.py:187
  46.4 3.4 %all-to-all-start.1 = ((f32[8,2,32,128]{3,2,1,0:T(8,128)}), f32[8,2,32,128]{3,2,1,0:T(8,128)S(1)}, u32[]{:S(2)}, u32[]{:S(2)}) async-start(f32[8,2,32,128]{3,2,1,0:T(8,128)} %broadcast_in_dim.66), calls=%async_computation.1 | async-start | bytes 524288 | tf_op jit(solution)/shard_map/all_to_all | solution.py:274
  49.9 1.0 add.141
  50.9 1.4 collective-permute-start.6
  52.3 9.9 %all-to-all-done.1 = f32[8,2,32,128]{3,2,1,0:T(8,128)S(1)} async-done(((f32[8,2,32,128]{3,2,1,0:T(8,128)}), f32[8,2,32,128]{3,2,1,0:T(8,128)S(1)}, u32[]{:S(2)}, u32[]{:S(2)}) %all-to-all-start.1) | async-done | bytes 262176 | tf_op jit(solution)/shard_map/all_to_all | solution.py:274
  62.9 4.5 %shard_map.68 = bf16[32,128,128]{2,1,0:T(8,128)(2,1)} custom-call(bf16[128,4096]{1,0:T(8,128)(2,1)} %q_ref.5, bf16[128,4096]{1,0:T(8,128)(2,1)} %k_ref.9, bf16[128,4096]{1,0:T(8,128)(2,1)} %g_ref.5, f32[32,128]{1,0:T(8,128)} %add.140.z_ref), custom_call_target="tpu_custom_call" | custom-call | tf_op jit(solution)/shard_map/pallas_call | solution.py:158
  67.3 3.6 %all-to-all-start.2 = ((bf16[8,512,128]{2,1,0:T(8,128)(2,1)}), bf16[8,512,128]{2,1,0:T(8,128)(2,1)S(1)}, u32[]{:S(2)}, u32[]{:S(2)}) async-start(bf16[8,512,128]{2,1,0:T(8,128)(2,1)} %bitcast.82), calls=%async_computation.2 | async-start | bytes 2097152 | tf_op jit(solution)/shard_map/all_to_all | solution.py:285
  71.0 3.0 %collective-permute-start.7 = (bf16[2,256,128]{2,1,0:T(8,128)(2,1)S(1)}, bf16[2,256,128]{2,1,0:T(8,128)(2,1)S(1)}, u32[]{:S(2)}, u32[]{:S(2)}) collective-permute-start(bf16[2,256,128]{2,1,0:T(8,128)(2,1)S(1)} %pad_maximum_fusion), channel_id=1, source_target_pairs={{0,32},{8,40},{16,48},{24,56},{32,0},{40,8},{48,16},{56,24},{64,96... | collective-permute-start | bytes 393224 | tf_op jit(solution)/shard_map/ppermute | solution.py:245
  74.0 3.2 %collective-permute-done.7 = bf16[2,256,128]{2,1,0:T(8,128)(2,1)S(1)} collective-permute-done((bf16[2,256,128]{2,1,0:T(8,128)(2,1)S(1)}, bf16[2,256,128]{2,1,0:T(8,128)(2,1)S(1)}, u32[]{:S(2)}, u32[]{:S(2)}) %collective-permute-start.7) | collective-permute-done | bytes 131104 | tf_op jit(solution)/shard_map/ppermute | solution.py:245
  77.2 1.3 collective-permute-start.8
  78.5 3.4 %collective-permute-done.8 = bf16[256,128]{1,0:T(8,128)(2,1)S(1)} collective-permute-done((bf16[256,128]{1,0:T(8,128)(2,1)S(1)}, bf16[256,128]{1,0:T(8,128)(2,1)S(1)}, u32[]{:S(2)}, u32[]{:S(2)}) %collective-permute-start.8) | collective-permute-done | bytes 65568 | tf_op jit(solution)/shard_map/ppermute | solution.py:245
  82.0 1.6 collective-permute-start.9
  83.6 3.4 %collective-permute-done.9 = bf16[256,128]{1,0:T(8,128)(2,1)S(1)} collective-permute-done((bf16[256,128]{1,0:T(8,128)(2,1)S(1)}, bf16[256,128]{1,0:T(8,128)(2,1)S(1)}, u32[]{:S(2)}, u32[]{:S(2)}) %collective-permute-start.9) | collective-permute-done | bytes 65568 | tf_op jit(solution)/shard_map/ppermute | solution.py:245
  87.0 3.1 %collective-permute-start.10 = (f32[256,128]{1,0:T(8,128)S(1)}, f32[256,128]{1,0:T(8,128)S(1)}, u32[]{:S(2)}, u32[]{:S(2)}) collective-permute-start(f32[256,128]{1,0:T(8,128)S(1)} %fusion.7), channel_id=1, source_target_pairs={{0,8},{8,0},{16,24},{24,16},{32,40},{40,32},{48,56},{56,48},{64,72... | collective-permute-start | bytes 393224 | tf_op jit(solution)/shard_map/ppermute | solution.py:251
  90.1 1.0 collective-permute-done.10
  91.9 2.4 %shard_map.70 = bf16[8,512,128]{2,1,0:T(8,128)(2,1)} custom-call(bf16[8,512,128]{2,1,0:T(8,128)(2,1)} %copy-done.1, f32[512,128]{1,0:T(8,128)} %maximum_add_fusion.base_ref), custom_call_target="tpu_custom_call" | custom-call | tf_op jit(solution)/shard_map/pallas_call | solution.py:198
  94.3 5.8 %all-to-all-done.2.x_ref = bf16[8,512,128]{2,1,0:T(8,128)(2,1)S(1)} async-done(((bf16[8,512,128]{2,1,0:T(8,128)(2,1)}), bf16[8,512,128]{2,1,0:T(8,128)(2,1)S(1)}, u32[]{:S(2)}, u32[]{:S(2)}) %all-to-all-start.2) | async-done | bytes 1048608 | tf_op jit(solution)/shard_map/all_to_all | solution.py:285
  100.1 1.0 copy-done.2
  101.0 2.1 %shard_map.73 = f32[512,128]{1,0:T(8,128)} custom-call(bf16[8,512,128]{2,1,0:T(8,128)(2,1)} %copy-done.2), custom_call_target="tpu_custom_call" | custom-call | tf_op jit(solution)/shard_map/pallas_call | solution.py:187
  103.6 3.6 %all-to-all-start.3 = ((bf16[8,512,128]{2,1,0:T(8,128)(2,1)}), bf16[8,512,128]{2,1,0:T(8,128)(2,1)S(1)}, u32[]{:S(2)}, u32[]{:S(2)}) async-start(bf16[8,512,128]{2,1,0:T(8,128)(2,1)} %shard_map.70), calls=%async_computation.3 | async-start | bytes 2097152 | tf_op jit(solution)/shard_map/all_to_all | solution.py:288
  107.2 2.8 %collective-permute-start.12 = (bf16[256,128]{1,0:T(8,128)(2,1)S(1)}, bf16[256,128]{1,0:T(8,128)(2,1)S(1)}, u32[]{:S(2)}, u32[]{:S(2)}) collective-permute-start(bf16[256,128]{1,0:T(8,128)(2,1)S(1)} %get-tuple-element.31), channel_id=1, source_target_pairs={{0,48},{8,56},{16,0},{24,8},{32,16},{40,24},{48,32},{56,40},{64,11... | collective-permute-start | bytes 196616 | tf_op jit(solution)/shard_map/ppermute | solution.py:245
  110.0 1.3 collective-permute-done.12
  111.4 2.6 %collective-permute-start.13 = (bf16[2,256,128]{2,1,0:T(8,128)(2,1)S(1)}, bf16[2,256,128]{2,1,0:T(8,128)(2,1)S(1)}, u32[]{:S(2)}, u32[]{:S(2)}) collective-permute-start(bf16[2,256,128]{2,1,0:T(8,128)(2,1)S(1)} %pad_maximum_fusion.1), channel_id=1, source_target_pairs={{0,32},{8,40},{16,48},{24,56},{32,0},{40,8},{48,16},{56,24},{64,96... | collective-permute-start | bytes 393224 | tf_op jit(solution)/shard_map/ppermute | solution.py:245
  114.0 3.3 %collective-permute-done.13 = bf16[2,256,128]{2,1,0:T(8,128)(2,1)S(1)} collective-permute-done((bf16[2,256,128]{2,1,0:T(8,128)(2,1)S(1)}, bf16[2,256,128]{2,1,0:T(8,128)(2,1)S(1)}, u32[]{:S(2)}, u32[]{:S(2)}) %collective-permute-start.13) | collective-permute-done | bytes 131104 | tf_op jit(solution)/shard_map/ppermute | solution.py:245
  117.4 2.6 %collective-permute-start.14 = (bf16[256,128]{1,0:T(8,128)(2,1)S(1)}, bf16[256,128]{1,0:T(8,128)(2,1)S(1)}, u32[]{:S(2)}, u32[]{:S(2)}) collective-permute-start(bf16[256,128]{1,0:T(8,128)(2,1)S(1)} %fusion.33), channel_id=1, source_target_pairs={{0,192},{8,200},{16,208},{24,216},{32,224},{40,232},{48,240},{56,2... | collective-permute-start | bytes 196616 | tf_op jit(solution)/shard_map/ppermute | solution.py:245
  119.9 1.3 collective-permute-done.14
  121.3 2.4 %collective-permute-start.15 = (bf16[256,128]{1,0:T(8,128)(2,1)S(1)}, bf16[256,128]{1,0:T(8,128)(2,1)S(1)}, u32[]{:S(2)}, u32[]{:S(2)}) collective-permute-start(bf16[256,128]{1,0:T(8,128)(2,1)S(1)} %add_convert_fusion), channel_id=1, source_target_pairs={{0,128},{8,136},{16,144},{24,152},{32,160},{40,168},{48,176},{56,1... | collective-permute-start | bytes 196616 | tf_op jit(solution)/shard_map/ppermute | solution.py:245
  123.7 2.4 %collective-permute-done.15 = bf16[256,128]{1,0:T(8,128)(2,1)S(1)} collective-permute-done((bf16[256,128]{1,0:T(8,128)(2,1)S(1)}, bf16[256,128]{1,0:T(8,128)(2,1)S(1)}, u32[]{:S(2)}, u32[]{:S(2)}) %collective-permute-start.15) | collective-permute-done | bytes 65568 | tf_op jit(solution)/shard_map/ppermute | solution.py:245
  126.2 3.8 %collective-permute-start.16 = (f32[256,128]{1,0:T(8,128)S(1)}, f32[256,128]{1,0:T(8,128)S(1)}, u32[]{:S(2)}, u32[]{:S(2)}) collective-permute-start(f32[256,128]{1,0:T(8,128)S(1)} %fusion.5), channel_id=1, source_target_pairs={{0,8},{8,0},{16,24},{24,16},{32,40},{40,32},{48,56},{56,48},{64,72... | collective-permute-start | bytes 393224 | tf_op jit(solution)/shard_map/ppermute | solution.py:251
  130.0 1.0 collective-permute-done.16
  131.0 5.3 %all-to-all-done.3 = bf16[8,512,128]{2,1,0:T(8,128)(2,1)S(1)} async-done(((bf16[8,512,128]{2,1,0:T(8,128)(2,1)}), bf16[8,512,128]{2,1,0:T(8,128)(2,1)S(1)}, u32[]{:S(2)}, u32[]{:S(2)}) %all-to-all-start.3) | async-done | bytes 1048608 | tf_op jit(solution)/shard_map/all_to_all | solution.py:288
  136.3 1.0 copy-done
  137.3 4.8 %shard_map.72 = f32[32,128]{1,0:T(8,128)} custom-call(bf16[128,4096]{1,0:T(8,128)(2,1)} %q_ref.5, bf16[128,4096]{1,0:T(8,128)(2,1)} %k_ref.9, bf16[128,4096]{1,0:T(8,128)(2,1)} %v_ref.7, bf16[128,4096]{1,0:T(8,128)(2,1)} %g_ref.5, f32[32,128]{1,0:T(8,128)} %add.140.z_ref, bf16[32,128,128]{2,1,0:T(8,128)(2,1)} %bitcast.79), custom_call_target="tpu_custom_call" | custom-call | tf_op jit(solution)/shard_map/pallas_call | solution.py:158
  142.1 1.4 broadcast_in_dim.72
  143.5 3.4 %all-to-all-start.4 = ((f32[8,32,128]{2,1,0:T(8,128)}), f32[8,32,128]{2,1,0:T(8,128)S(1)}, u32[]{:S(2)}, u32[]{:S(2)}) async-start(f32[8,32,128]{2,1,0:T(8,128)} %broadcast_in_dim.72), calls=%async_computation.4 | async-start | bytes 262144 | tf_op jit(solution)/shard_map/all_to_all | solution.py:274
  147.6 2.4 %shard_map.74 = bf16[8,512,128]{2,1,0:T(8,128)(2,1)} custom-call(bf16[8,512,128]{2,1,0:T(8,128)(2,1)} %copy-done.2, f32[512,128]{1,0:T(8,128)} %maximum_add_fusion.1.base_ref), custom_call_target="tpu_custom_call" | custom-call | tf_op jit(solution)/shard_map/pallas_call | solution.py:198
  150.0 4.9 %all-to-all-done.4 = f32[8,32,128]{2,1,0:T(8,128)S(1)} async-done(((f32[8,32,128]{2,1,0:T(8,128)}), f32[8,32,128]{2,1,0:T(8,128)S(1)}, u32[]{:S(2)}, u32[]{:S(2)}) %all-to-all-start.4) | async-done | bytes 131104 | tf_op jit(solution)/shard_map/all_to_all | solution.py:274
  155.0 3.6 %all-to-all-start.5 = ((bf16[8,512,128]{2,1,0:T(8,128)(2,1)}), bf16[8,512,128]{2,1,0:T(8,128)(2,1)S(1)}, u32[]{:S(2)}, u32[]{:S(2)}) async-start(bf16[8,512,128]{2,1,0:T(8,128)(2,1)} %shard_map.74), calls=%async_computation.5 | async-start | bytes 2097152 | tf_op jit(solution)/shard_map/all_to_all | solution.py:288
  158.6 1.9 collective-permute-start.17
  160.6 0.8 collective-permute-done.17
  161.4 2.7 %collective-permute-start.18 = (f32[32,128]{1,0:T(8,128)S(1)}, f32[32,128]{1,0:T(8,128)S(1)}, u32[]{:S(2)}, u32[]{:S(2)}) collective-permute-start(f32[32,128]{1,0:T(8,128)S(1)} %add.159), channel_id=1, source_target_pairs={{0,48},{8,56},{16,0},{24,8},{32,16},{40,24},{48,32},{56,40},{64,11... | collective-permute-start | bytes 49160 | tf_op jit(solution)/shard_map/ppermute | solution.py:245
  164.2 0.9 collective-permute-done.18
  165.0 2.3 %collective-permute-start.19 = (f32[2,32,128]{2,1,0:T(8,128)S(1)}, f32[2,32,128]{2,1,0:T(8,128)S(1)}, u32[]{:S(2)}, u32[]{:S(2)}) collective-permute-start(f32[2,32,128]{2,1,0:T(8,128)S(1)} %pad_maximum_fusion.4), channel_id=1, source_target_pairs={{0,32},{8,40},{16,48},{24,56},{32,0},{40,8},{48,16},{56,24},{64,96... | collective-permute-start | bytes 98312 | tf_op jit(solution)/shard_map/ppermute | solution.py:245
  167.3 2.4 %collective-permute-done.19 = f32[2,32,128]{2,1,0:T(8,128)S(1)} collective-permute-done((f32[2,32,128]{2,1,0:T(8,128)S(1)}, f32[2,32,128]{2,1,0:T(8,128)S(1)}, u32[]{:S(2)}, u32[]{:S(2)}) %collective-permute-start.19) | collective-permute-done | bytes 32800 | tf_op jit(solution)/shard_map/ppermute | solution.py:245
  169.7 2.5 %collective-permute-start.20 = (f32[32,128]{1,0:T(8,128)S(1)}, f32[32,128]{1,0:T(8,128)S(1)}, u32[]{:S(2)}, u32[]{:S(2)}) collective-permute-start(f32[32,128]{1,0:T(8,128)S(1)} %fusion.20), channel_id=1, source_target_pairs={{0,192},{8,200},{16,208},{24,216},{32,224},{40,232},{48,240},{56,2... | collective-permute-start | bytes 49160 | tf_op jit(solution)/shard_map/ppermute | solution.py:245
  172.2 0.9 collective-permute-done.20
  173.1 2.3 %collective-permute-start.21 = (f32[32,128]{1,0:T(8,128)S(1)}, f32[32,128]{1,0:T(8,128)S(1)}, u32[]{:S(2)}, u32[]{:S(2)}) collective-permute-start(f32[32,128]{1,0:T(8,128)S(1)} %select_add_fusion), channel_id=1, source_target_pairs={{0,128},{8,136},{16,144},{24,152},{32,160},{40,168},{48,176},{56,1... | collective-permute-start | bytes 49160 | tf_op jit(solution)/shard_map/ppermute | solution.py:245
  175.3 7.9 %shard_map.71 = (bf16[128,4096]{1,0:T(8,128)(2,1)}, f32[128,4096]{1,0:T(8,128)}, f32[128,4096]{1,0:T(8,128)}) custom-call(bf16[128,4096]{1,0:T(8,128)(2,1)} %q_ref.5, bf16[128,4096]{1,0:T(8,128)(2,1)} %k_ref.9, bf16[128,4096]{1,0:T(8,128)(2,1)} %v_ref.7, bf16[128,4096]{1,0:T(8,128)(2,1)} %g_ref.5, f32[32,128]{1,0:T(8,128)} %add.140.z_ref, ...), custom_call_target="tpu_custom_call" | custom-call | tf_op jit(solution)/shard_map/pallas_call | solution.py:158
  183.9 3.8 %all-to-all-done.5 = bf16[8,512,128]{2,1,0:T(8,128)(2,1)S(1)} async-done(((bf16[8,512,128]{2,1,0:T(8,128)(2,1)}), bf16[8,512,128]{2,1,0:T(8,128)(2,1)S(1)}, u32[]{:S(2)}, u32[]{:S(2)}) %all-to-all-start.5) | async-done | bytes 1048608 | tf_op jit(solution)/shard_map/all_to_all | solution.py:288
  187.6 1.0 copy-done.3
  188.7 4.9 %shard_map.75 = (bf16[128,4096]{1,0:T(8,128)(2,1)}, bf16[128,4096]{1,0:T(8,128)(2,1)}) custom-call(bf16[128,4096]{1,0:T(8,128)(2,1)} %k_ref.9, bf16[128,4096]{1,0:T(8,128)(2,1)} %v_ref.7, f32[128,4096]{1,0:T(8,128)} %get-tuple-element.22.dfk_ref, f32[128,4096]{1,0:T(8,128)} %get-tuple-element.23.gv_ref, bf16[32,128,128]{2,1,0:T(8,128)(2,1)} %bitcast.81, ...), custom_call_target="tpu_custom_call" | custom-call | tf_op jit(solution)/shard_map/pallas_call | solution.py:158
  (54 shorter events, 6.0 us)
Async XLA Ops:
  3.9 9.1 %copy-start.5 = (f32[32,128]{1,0:T(8,128)S(1)}, f32[32,128]{1,0:T(8,128)}, u32[]{:S(2)}) copy-start(f32[32,128]{1,0:T(8,128)} %get-tuple-element.17) | copy-start | bytes 49156
  3.9 38.3 %all-to-all-start = ((bf16[8,512,128]{2,1,0:T(8,128)(2,1)}), bf16[8,512,128]{2,1,0:T(8,128)(2,1)S(1)}, u32[]{:S(2)}, u32[]{:S(2)}) async-start(bf16[8,512,128]{2,1,0:T(8,128)(2,1)} %bitcast.83), calls=%async_computation | async-start | bytes 2097152 | tf_op jit(solution)/shard_map/all_to_all | solution.py:285
  13.0 1.9 collective-permute-start
  14.9 3.9 %collective-permute-start.1 = (f32[32,128]{1,0:T(8,128)S(1)}, f32[32,128]{1,0:T(8,128)S(1)}, u32[]{:S(2)}, u32[]{:S(2)}) collective-permute-start(f32[32,128]{1,0:T(8,128)S(1)} %add.131), channel_id=1, source_target_pairs={{0,16},{8,24},{16,32},{24,40},{32,48},{40,56},{48,0},{56,8},{64,80... | collective-permute-start | bytes 49160 | tf_op jit(solution)/shard_map/ppermute | solution.py:245
  18.8 4.7 %collective-permute-start.2 = (f32[2,32,128]{2,1,0:T(8,128)S(1)}, f32[2,32,128]{2,1,0:T(8,128)S(1)}, u32[]{:S(2)}, u32[]{:S(2)}) collective-permute-start(f32[2,32,128]{2,1,0:T(8,128)S(1)} %pad_maximum_fusion.2), channel_id=1, source_target_pairs={{0,32},{8,40},{16,48},{24,56},{32,0},{40,8},{48,16},{56,24},{64,96... | collective-permute-start | bytes 98312 | tf_op jit(solution)/shard_map/ppermute | solution.py:245
  23.4 4.1 %collective-permute-start.3 = (f32[32,128]{1,0:T(8,128)S(1)}, f32[32,128]{1,0:T(8,128)S(1)}, u32[]{:S(2)}, u32[]{:S(2)}) collective-permute-start(f32[32,128]{1,0:T(8,128)S(1)} %fusion.26), channel_id=1, source_target_pairs={{0,64},{8,72},{16,80},{24,88},{32,96},{40,104},{48,112},{56,120},{... | collective-permute-start | bytes 49160 | tf_op jit(solution)/shard_map/ppermute | solution.py:245
  27.5 4.4 %collective-permute-start.4 = (f32[32,128]{1,0:T(8,128)S(1)}, f32[32,128]{1,0:T(8,128)S(1)}, u32[]{:S(2)}, u32[]{:S(2)}) collective-permute-start(f32[32,128]{1,0:T(8,128)S(1)} %select_add_fusion.1), channel_id=1, source_target_pairs={{0,128},{8,136},{16,144},{24,152},{32,160},{40,168},{48,176},{56,1... | collective-permute-start | bytes 49160 | tf_op jit(solution)/shard_map/ppermute | solution.py:245
  42.2 1.0 copy-start.1
  45.2 4.7 %collective-permute-start.5 = (f32[512,128]{1,0:T(8,128)}, f32[512,128]{1,0:T(8,128)S(1)}, u32[]{:S(2)}, u32[]{:S(2)}) collective-permute-start(f32[512,128]{1,0:T(8,128)} %shard_map.69), channel_id=1, source_target_pairs={{0,8},{8,0},{16,24},{24,16},{32,40},{40,32},{48,56},{56,48},{64,72... | collective-permute-start | bytes 786440 | tf_op jit(solution)/shard_map/ppermute | solution.py:251
  46.4 15.7 %all-to-all-start.1 = ((f32[8,2,32,128]{3,2,1,0:T(8,128)}), f32[8,2,32,128]{3,2,1,0:T(8,128)S(1)}, u32[]{:S(2)}, u32[]{:S(2)}) async-start(f32[8,2,32,128]{3,2,1,0:T(8,128)} %broadcast_in_dim.66), calls=%async_computation.1 | async-start | bytes 524288 | tf_op jit(solution)/shard_map/all_to_all | solution.py:274
  50.9 20.0 %collective-permute-start.6 = (bf16[256,128]{1,0:T(8,128)(2,1)S(1)}, bf16[256,128]{1,0:T(8,128)(2,1)S(1)}, u32[]{:S(2)}, u32[]{:S(2)}) collective-permute-start(bf16[256,128]{1,0:T(8,128)(2,1)S(1)} %get-tuple-element.33), channel_id=1, source_target_pairs={{0,16},{8,24},{16,32},{24,40},{32,48},{40,56},{48,0},{56,8},{64,80... | collective-permute-start | bytes 196616 | tf_op jit(solution)/shard_map/ppermute | solution.py:245
  67.3 32.7 %all-to-all-start.2 = ((bf16[8,512,128]{2,1,0:T(8,128)(2,1)}), bf16[8,512,128]{2,1,0:T(8,128)(2,1)S(1)}, u32[]{:S(2)}, u32[]{:S(2)}) async-start(bf16[8,512,128]{2,1,0:T(8,128)(2,1)} %bitcast.82), calls=%async_computation.2 | async-start | bytes 2097152 | tf_op jit(solution)/shard_map/all_to_all | solution.py:285
  71.0 6.2 %collective-permute-start.7 = (bf16[2,256,128]{2,1,0:T(8,128)(2,1)S(1)}, bf16[2,256,128]{2,1,0:T(8,128)(2,1)S(1)}, u32[]{:S(2)}, u32[]{:S(2)}) collective-permute-start(bf16[2,256,128]{2,1,0:T(8,128)(2,1)S(1)} %pad_maximum_fusion), channel_id=1, source_target_pairs={{0,32},{8,40},{16,48},{24,56},{32,0},{40,8},{48,16},{56,24},{64,96... | collective-permute-start | bytes 393224 | tf_op jit(solution)/shard_map/ppermute | solution.py:245
  77.2 4.7 %collective-permute-start.8 = (bf16[256,128]{1,0:T(8,128)(2,1)S(1)}, bf16[256,128]{1,0:T(8,128)(2,1)S(1)}, u32[]{:S(2)}, u32[]{:S(2)}) collective-permute-start(bf16[256,128]{1,0:T(8,128)(2,1)S(1)} %fusion.32), channel_id=1, source_target_pairs={{0,64},{8,72},{16,80},{24,88},{32,96},{40,104},{48,112},{56,120},{... | collective-permute-start | bytes 196616 | tf_op jit(solution)/shard_map/ppermute | solution.py:245
  82.0 5.0 %collective-permute-start.9 = (bf16[256,128]{1,0:T(8,128)(2,1)S(1)}, bf16[256,128]{1,0:T(8,128)(2,1)S(1)}, u32[]{:S(2)}, u32[]{:S(2)}) collective-permute-start(bf16[256,128]{1,0:T(8,128)(2,1)S(1)} %add_convert_fusion.1), channel_id=1, source_target_pairs={{0,128},{8,136},{16,144},{24,152},{32,160},{40,168},{48,176},{56,1... | collective-permute-start | bytes 196616 | tf_op jit(solution)/shard_map/ppermute | solution.py:245
  87.0 4.1 %collective-permute-start.10 = (f32[256,128]{1,0:T(8,128)S(1)}, f32[256,128]{1,0:T(8,128)S(1)}, u32[]{:S(2)}, u32[]{:S(2)}) collective-permute-start(f32[256,128]{1,0:T(8,128)S(1)} %fusion.7), channel_id=1, source_target_pairs={{0,8},{8,0},{16,24},{24,16},{32,40},{40,32},{48,56},{56,48},{64,72... | collective-permute-start | bytes 393224 | tf_op jit(solution)/shard_map/ppermute | solution.py:251
  100.1 1.0 copy-start.2
  103.1 4.1 %copy-start.4 = (f32[512,128]{1,0:T(8,128)S(1)}, f32[512,128]{1,0:T(8,128)}, u32[]{:S(2)}) copy-start(f32[512,128]{1,0:T(8,128)} %shard_map.73) | copy-start | bytes 786436
  103.1 4.1 %collective-permute-start.11 = (f32[512,128]{1,0:T(8,128)}, f32[512,128]{1,0:T(8,128)S(1)}, u32[]{:S(2)}, u32[]{:S(2)}) collective-permute-start(f32[512,128]{1,0:T(8,128)} %shard_map.73), channel_id=1, source_target_pairs={{0,8},{8,0},{16,24},{24,16},{32,40},{40,32},{48,56},{56,48},{64,72... | collective-permute-start | bytes 786440 | tf_op jit(solution)/shard_map/ppermute | solution.py:251
  103.6 32.8 %all-to-all-start.3 = ((bf16[8,512,128]{2,1,0:T(8,128)(2,1)}), bf16[8,512,128]{2,1,0:T(8,128)(2,1)S(1)}, u32[]{:S(2)}, u32[]{:S(2)}) async-start(bf16[8,512,128]{2,1,0:T(8,128)(2,1)} %shard_map.70), calls=%async_computation.3 | async-start | bytes 2097152 | tf_op jit(solution)/shard_map/all_to_all | solution.py:288
  107.2 4.1 %collective-permute-start.12 = (bf16[256,128]{1,0:T(8,128)(2,1)S(1)}, bf16[256,128]{1,0:T(8,128)(2,1)S(1)}, u32[]{:S(2)}, u32[]{:S(2)}) collective-permute-start(bf16[256,128]{1,0:T(8,128)(2,1)S(1)} %get-tuple-element.31), channel_id=1, source_target_pairs={{0,48},{8,56},{16,0},{24,8},{32,16},{40,24},{48,32},{56,40},{64,11... | collective-permute-start | bytes 196616 | tf_op jit(solution)/shard_map/ppermute | solution.py:245
  111.4 5.9 %collective-permute-start.13 = (bf16[2,256,128]{2,1,0:T(8,128)(2,1)S(1)}, bf16[2,256,128]{2,1,0:T(8,128)(2,1)S(1)}, u32[]{:S(2)}, u32[]{:S(2)}) collective-permute-start(bf16[2,256,128]{2,1,0:T(8,128)(2,1)S(1)} %pad_maximum_fusion.1), channel_id=1, source_target_pairs={{0,32},{8,40},{16,48},{24,56},{32,0},{40,8},{48,16},{56,24},{64,96... | collective-permute-start | bytes 393224 | tf_op jit(solution)/shard_map/ppermute | solution.py:245
  117.4 3.9 %collective-permute-start.14 = (bf16[256,128]{1,0:T(8,128)(2,1)S(1)}, bf16[256,128]{1,0:T(8,128)(2,1)S(1)}, u32[]{:S(2)}, u32[]{:S(2)}) collective-permute-start(bf16[256,128]{1,0:T(8,128)(2,1)S(1)} %fusion.33), channel_id=1, source_target_pairs={{0,192},{8,200},{16,208},{24,216},{32,224},{40,232},{48,240},{56,2... | collective-permute-start | bytes 196616 | tf_op jit(solution)/shard_map/ppermute | solution.py:245
  121.3 4.8 %collective-permute-start.15 = (bf16[256,128]{1,0:T(8,128)(2,1)S(1)}, bf16[256,128]{1,0:T(8,128)(2,1)S(1)}, u32[]{:S(2)}, u32[]{:S(2)}) collective-permute-start(bf16[256,128]{1,0:T(8,128)(2,1)S(1)} %add_convert_fusion), channel_id=1, source_target_pairs={{0,128},{8,136},{16,144},{24,152},{32,160},{40,168},{48,176},{56,1... | collective-permute-start | bytes 196616 | tf_op jit(solution)/shard_map/ppermute | solution.py:245
  126.2 4.8 %collective-permute-start.16 = (f32[256,128]{1,0:T(8,128)S(1)}, f32[256,128]{1,0:T(8,128)S(1)}, u32[]{:S(2)}, u32[]{:S(2)}) collective-permute-start(f32[256,128]{1,0:T(8,128)S(1)} %fusion.5), channel_id=1, source_target_pairs={{0,8},{8,0},{16,24},{24,16},{32,40},{40,32},{48,56},{56,48},{64,72... | collective-permute-start | bytes 393224 | tf_op jit(solution)/shard_map/ppermute | solution.py:251
  136.3 1.0 copy-start
  143.5 11.5 %all-to-all-start.4 = ((f32[8,32,128]{2,1,0:T(8,128)}), f32[8,32,128]{2,1,0:T(8,128)S(1)}, u32[]{:S(2)}, u32[]{:S(2)}) async-start(f32[8,32,128]{2,1,0:T(8,128)} %broadcast_in_dim.72), calls=%async_computation.4 | async-start | bytes 262144 | tf_op jit(solution)/shard_map/all_to_all | solution.py:274
  155.0 32.7 %all-to-all-start.5 = ((bf16[8,512,128]{2,1,0:T(8,128)(2,1)}), bf16[8,512,128]{2,1,0:T(8,128)(2,1)S(1)}, u32[]{:S(2)}, u32[]{:S(2)}) async-start(bf16[8,512,128]{2,1,0:T(8,128)(2,1)} %shard_map.74), calls=%async_computation.5 | async-start | bytes 2097152 | tf_op jit(solution)/shard_map/all_to_all | solution.py:288
  158.6 2.8 %collective-permute-start.17 = (f32[32,128]{1,0:T(8,128)S(1)}, f32[32,128]{1,0:T(8,128)S(1)}, u32[]{:S(2)}, u32[]{:S(2)}) collective-permute-start(f32[32,128]{1,0:T(8,128)S(1)} %get-tuple-element.29), channel_id=1, source_target_pairs={{0,8},{8,0},{16,24},{24,16},{32,40},{40,32},{48,56},{56,48},{64,72... | collective-permute-start | bytes 49160 | tf_op jit(solution)/shard_map/ppermute | solution.py:251
  161.4 3.6 %collective-permute-start.18 = (f32[32,128]{1,0:T(8,128)S(1)}, f32[32,128]{1,0:T(8,128)S(1)}, u32[]{:S(2)}, u32[]{:S(2)}) collective-permute-start(f32[32,128]{1,0:T(8,128)S(1)} %add.159), channel_id=1, source_target_pairs={{0,48},{8,56},{16,0},{24,8},{32,16},{40,24},{48,32},{56,40},{64,11... | collective-permute-start | bytes 49160 | tf_op jit(solution)/shard_map/ppermute | solution.py:245
  165.0 4.6 %collective-permute-start.19 = (f32[2,32,128]{2,1,0:T(8,128)S(1)}, f32[2,32,128]{2,1,0:T(8,128)S(1)}, u32[]{:S(2)}, u32[]{:S(2)}) collective-permute-start(f32[2,32,128]{2,1,0:T(8,128)S(1)} %pad_maximum_fusion.4), channel_id=1, source_target_pairs={{0,32},{8,40},{16,48},{24,56},{32,0},{40,8},{48,16},{56,24},{64,96... | collective-permute-start | bytes 98312 | tf_op jit(solution)/shard_map/ppermute | solution.py:245
  169.7 3.4 %collective-permute-start.20 = (f32[32,128]{1,0:T(8,128)S(1)}, f32[32,128]{1,0:T(8,128)S(1)}, u32[]{:S(2)}, u32[]{:S(2)}) collective-permute-start(f32[32,128]{1,0:T(8,128)S(1)} %fusion.20), channel_id=1, source_target_pairs={{0,192},{8,200},{16,208},{24,216},{32,224},{40,232},{48,240},{56,2... | collective-permute-start | bytes 49160 | tf_op jit(solution)/shard_map/ppermute | solution.py:245
  173.1 10.2 %collective-permute-start.21 = (f32[32,128]{1,0:T(8,128)S(1)}, f32[32,128]{1,0:T(8,128)S(1)}, u32[]{:S(2)}, u32[]{:S(2)}) collective-permute-start(f32[32,128]{1,0:T(8,128)S(1)} %select_add_fusion), channel_id=1, source_target_pairs={{0,128},{8,136},{16,144},{24,152},{32,160},{40,168},{48,176},{56,1... | collective-permute-start | bytes 49160 | tf_op jit(solution)/shard_map/ppermute | solution.py:245
  187.6 1.0 copy-start.3

commit v3 on v2

--- a/solution.py
+++ b/solution.py
@@ -41,8 +41,10 @@
     return ref[pl.ds(pl.program_id(0) * step + j, 1), :]
 
 
-def put_head_row(ref, step, j, row):
-    ref[pl.ds(pl.program_id(0) * step + j, 1), :] = row
+def put_rows(ref, step, j, row):
+    at = pl.ds(pl.program_id(0) * step + j, 1)
+    for member in range(ref.shape[0]):
+        ref[member, at, :] = row
 
 
 def each(fn, *lists):
@@ -54,7 +56,8 @@
     fk = [feature(k_ref[:, columns(j)].astype(F32)).astype(BF16) for j in heads]
     states = [dot_tn(fk[j], v_ref[:, columns(j)]) for j in heads]
     for j in heads:
-        put_head_row(sum_ref, step, j, jnp.sum(fk[j].astype(F32), axis=0, keepdims=True))
+        row = jnp.sum(fk[j].astype(F32), axis=0, keepdims=True)
+        put_rows(sum_ref, step, j, row)
     for j in heads:
         state_ref[j] = states[j].astype(BF16)
 
@@ -92,20 +95,7 @@
     return [-(s * i) * i for s, i in zip(shared, inverse)]
 
 
-def query_sum_kernel(step, q_ref, k_ref, v_ref, g_ref, z_ref, s_ref, sum_ref):
-    mask = causal(q_ref.shape[0])
-    heads = range(step)
-    fq = [feature(q_ref[:, columns(j)].astype(F32)).astype(BF16) for j in heads]
-    fk = [feature(k_ref[:, columns(j)].astype(F32)).astype(BF16) for j in heads]
-    weights, inverse = scores_of(fq, fk, [head_row(z_ref, step, j) for j in heads], mask)
-    num = num_of(fq, weights, [v_ref[:, columns(j)] for j in heads], s_ref)
-    dden = dden_of(g_ref, num, inverse)
-    for j in heads:
-        row = jnp.sum(dden[j] * fq[j].astype(F32), axis=0, keepdims=True)
-        put_head_row(sum_ref, step, j, row)
-
-
-def query_grad_kernel(step, q_ref, k_ref, v_ref, g_ref, z_ref, s_ref, gq_ref, dfk_ref, gv_ref):
+def query_grad_kernel(step, q_ref, k_ref, v_ref, g_ref, z_ref, s_ref, gq_ref, dfk_ref, gv_ref, sum_ref):
     mask = causal(q_ref.shape[0])
     heads = range(step)
     fq32 = [feature(q_ref[:, columns(j)].astype(F32)) for j in heads]
@@ -120,6 +110,9 @@
     dden = dden_of(g_ref, num, inverse)
     mixing = [jnp.where(mask, p + d, 0.0).astype(BF16) for p, d in zip(pair, dden)]
     for j in heads:
+        row = jnp.sum(dden[j] * fq[j].astype(F32), axis=0, keepdims=True)
+        put_rows(sum_ref, step, j, row)
+    for j in heads:
         gv_ref[:, columns(j)] = dot_tn(weights[j], dnum[j])
     dfq = [
         dot_nn(mixing[j], fk[j]) + dot_nt(dnum[j], s_ref[j]) + dden[j] * zrows[j] for j in heads
@@ -130,26 +123,47 @@
         dfk_ref[:, columns(j)] = dot_tn(mixing[j], fq[j])
 
 
-def key_grad_kernel(step, k_ref, v_ref, dfk_ref, gv_ref, rs_ref, rz_ref, gk_ref, gv_out_ref):
-    heads = range(step)
-    fk32 = [feature(k_ref[:, columns(j)].astype(F32)) for j in heads]
-    dfk = [dot_nt(v_ref[:, columns(j)], rs_ref[j]) for j in heads]
-    gv = [dot_nn(fk32[j].astype(BF16), rs_ref[j]) for j in heads]
-    for j in heads:
-        c = columns(j)
-        whole = dfk[j] + dfk_ref[:, c] + head_row(rz_ref, step, j)
-        gk_ref[:, c] = (whole * jnp.minimum(fk32[j], 1.0)).astype(BF16)
-    for j in heads:
-        c = columns(j)
-        gv_out_ref[:, c] = (gv[j] + gv_ref[:, c]).astype(BF16)
-
-
-def head_call(kernel, step, kinds_in, kinds_out, arrays, tokens, heads):
+def key_grad_kernel(
+    place_ref, k_ref, v_ref, dfk_ref, gv_ref, rz_ref, *refs
+):
+    pieces, (gk_ref, gv_out_ref) = refs[:-2], refs[-2:]
+    group = len(pieces)
+    per = pieces[0].shape[0] // HD
+    for first in range(0, group, 2):
+        work = []
+        for d in (first, first + 1):
+            owner = lax.rem(place_ref[0] + group - d, group)
+            for j in range(per):
+                at = pl.ds(pl.multiple_of(owner * per * HD, per * HD) + j * HD, HD)
+                work.append((pieces[d][j * HD : (j + 1) * HD, :], at, owner * per + j))
+        fk32 = [feature(k_ref[:, at].astype(F32)) for _, at, _ in work]
+        dfk = [dot_nt(v_ref[:, at], state) for state, at, _ in work]
+        gv = [dot_nn(f.astype(BF16), state) for f, (state, _, _) in zip(fk32, work)]
+        for f, whole, (_, at, head) in zip(fk32, dfk, work):
+            whole = whole + dfk_ref[:, at] + rz_ref[pl.ds(head, 1), :]
+            gk_ref[:, at] = (whole * jnp.minimum(f, 1.0)).astype(BF16)
+        for part, (_, at, _) in zip(gv, work):
+            gv_out_ref[:, at] = (part + gv_ref[:, at]).astype(BF16)
+
+
+def key_grad(place, arrays, pieces, tokens, width):
+    return pl.pallas_call(
+        key_grad_kernel,
+        in_specs=[pl.BlockSpec(memory_space=pltpu.SMEM)]
+        + [pl.BlockSpec(memory_space=pltpu.VMEM)] * (len(arrays) + len(pieces)),
+        out_specs=[pl.BlockSpec(memory_space=pltpu.VMEM)] * 2,
+        out_shape=[jax.ShapeDtypeStruct((tokens, width), BF16)] * 2,
+    )(place, *arrays, *pieces)
+
+
+def head_call(kernel, step, kinds_in, kinds_out, arrays, tokens, heads, group):
     wide = pl.BlockSpec((tokens, step * HD), lambda i: (0, i))
     square = pl.BlockSpec((step, HD, HD), lambda i: (i, 0, 0))
     rows = pl.BlockSpec((heads, HD), lambda i: (0, 0))
-    specs = {"w": wide, "f": wide, "s": square, "r": rows}
+    copies = pl.BlockSpec((group, heads, HD), lambda i: (0, 0, 0))
+    specs = {"g": copies, "w": wide, "f": wide, "s": square, "r": rows}
     shapes = {
+        "g": jax.ShapeDtypeStruct((group, heads, HD), F32),
         "w": jax.ShapeDtypeStruct((tokens, heads * HD), BF16),
         "f": jax.ShapeDtypeStruct((tokens, heads * HD), F32),
         "s": jax.ShapeDtypeStruct((heads, HD, HD), BF16),
@@ -193,37 +207,45 @@
     )(x)
 
 
+def z_spread_kernel(place_ref, x_ref, base_ref, *refs):
+    outs, held = refs[:-1], refs[-1]
+    z_running_kernel(False, x_ref, base_ref, held)
+    for d, out in enumerate(outs):
+        out[...] = held[lax.rem(place_ref[0] + d, len(outs))]
+
+
 def z_running(x, base, forward):
     n, rows, lanes = x.shape
+    whole = pl.BlockSpec(memory_space=pltpu.VMEM)
     return pl.pallas_call(
         functools.partial(z_running_kernel, forward),
-        grid=(1,),
-        in_specs=[
-            pl.BlockSpec((n, rows, lanes), lambda i: (0, i, 0)),
-            pl.BlockSpec((rows, lanes), lambda i: (i, 0)),
-        ],
-        out_specs=pl.BlockSpec((n, rows, lanes), lambda i: (0, i, 0)),
+        in_specs=[whole, whole],
+        out_specs=whole,
         out_shape=jax.ShapeDtypeStruct((n, rows, lanes), BF16),
     )(x, base)
 
 
-def level(part, total, n, place, hop, forward, wire):
-    before = None
-    d = 1
-    while d < n:
-        if total is None:
-            got_part, got_total = hop(part.astype(wire), d).astype(F32), None
-        elif total is part:
-            got_part = got_total = hop(part.astype(wire), d).astype(F32)
-        else:
-            got = hop(jnp.stack([part, total]).astype(wire), d).astype(F32)
-            got_part, got_total = got[0], got[1]
-        ok = (place >= d) if forward else (place < n - d)
-        masked = jnp.where(ok, got_part, 0.0)
-        before = masked if before is None else before + masked
-        part, total = part + masked, None if total is None else total + got_total
-        d *= 2
-    return before, total
+def z_spread(place, x, base):
+    n, rows, lanes = x.shape
+    whole = pl.BlockSpec(memory_space=pltpu.VMEM)
+    return pl.pallas_call(
+        z_spread_kernel,
+        in_specs=[pl.BlockSpec(memory_space=pltpu.SMEM), whole, whole],
+        out_specs=[whole] * n,
+        out_shape=[jax.ShapeDtypeStruct((rows, lanes), BF16)] * n,
+        scratch_shapes=[pltpu.VMEM((n, rows, lanes), BF16)],
+    )(place, x, base)
+
+
+def level(value, n, place, hop, forward, wire, need_total):
+    sent = value.astype(wire)
+    got = [hop(sent, d, need_total).astype(F32) for d in range(1, n)]
+    if not need_total:
+        return sum(got[1:], got[0]), None
+    before = sum(
+        jnp.where((place >= d) if forward else (place < n - d), g, 0.0) for d, g in enumerate(got, 1)
+    )
+    return before, sum(got, value)
 
 
 def grid_of(ctx):
@@ -234,14 +256,16 @@
 
 
 def ctx_hop(side, which, forward):
-    def hop(value, d):
+    def hop(value, d, wrap):
         d = d if forward else -d
         pairs = []
         for x in range(side):
             for y in range(side):
-                for c in range(2):
-                    to = (x, (y + d) % side) if which == "y" else ((x + d) % side, y)
-                    pairs.append(((x * side + y) * 2 + c, (to[0] * side + to[1]) * 2 + c))
+                to = (x, y + d) if which == "y" else (x + d, y)
+                if not wrap and not all(0 <= t < side for t in to):
+                    continue
+                at = (to[0] % side) * side + to[1] % side
+                pairs += [((x * side + y) * 2 + c, at * 2 + c) for c in range(2)]
         return lax.ppermute(value, "ctx", pairs)
 
     return hop
@@ -261,8 +285,8 @@
     half = total.shape[0] // 2
     if split:
         chip = jnp.where(core == 0, chip[:half], chip[half:])
-    by_y, row = level(chip, chip, side, y, ctx_hop(side, "y", forward), forward, wire)
-    by_x, _ = level(row, None, side, x, ctx_hop(side, "x", forward), forward, wire)
+    by_y, row = level(chip, side, y, ctx_hop(side, "y", forward), forward, wire, True)
+    by_x, _ = level(row, side, x, ctx_hop(side, "x", forward), forward, wire, False)
     base = by_y + by_x
     if split:
         got = swap_cores(base, ctx)
@@ -270,14 +294,14 @@
     return by_core + base
 
 
-def z_gather(x, group):
-    return lax.all_to_all(jnp.broadcast_to(x[None], (group, *x.shape)), "head", 0, 0, tiled=True)
+def z_gather(copies):
+    return lax.all_to_all(copies, "head", 0, 0, tiled=True)
 
 
 def shards(ctx, group, queries, keys, values, out_grad):
     tokens, width = queries.shape
     heads = width // HD
-    call = functools.partial(head_call, tokens=tokens, heads=heads)
+    call = functools.partial(head_call, tokens=tokens, heads=heads, group=group)
     owned = heads * HD // group
     place = lax.axis_index("head")
 
@@ -288,13 +312,16 @@
         return lax.all_to_all(x, "head", 0, 0, tiled=True).reshape(heads, HD, HD)
 
     ranks = jnp.arange(group)[:, None, None]
-    key_state, key_sum = call(key_state_kernel, 16, "ww", "sr", (keys, values))
+    where = jnp.full((1,), place, jnp.int32)
+    key_state, key_sum = call(key_state_kernel, 16, "ww", "sg", (keys, values))
+    sums = z_gather(key_sum)
+    before = jnp.sum(jnp.where(ranks < place, sums, 0.0), axis=0)
+    total = jnp.sum(sums, axis=0)
+    key_state, before, total = lax.optimization_barrier((key_state, before, total))
     key_parts = to_owners(key_state)
-    earlier = ctx_running(key_sum, ctx, True, F32, False)
-    key_parts, both = lax.optimization_barrier((key_parts, jnp.stack([key_sum, earlier])))
-    sums = z_gather(both, group)
-    z = jnp.sum(sums[:, 1], axis=0) + jnp.sum(jnp.where(ranks < place, sums[:, 0], 0.0), axis=0)
+    z = before + ctx_running(total, ctx, True, F32, False)
     (query_state,) = call(query_state_kernel, 16, "wwwr", "s", (queries, keys, out_grad, z))
+    key_parts, query_state = lax.optimization_barrier((key_parts, query_state))
     query_parts = to_owners(query_state)
     key_total = z_total(key_parts)
     key_base = ctx_running(key_total, ctx, True, BF16, True)
@@ -303,17 +330,19 @@
     prefix = from_owners(key_running)
     query_total = z_total(query_parts)
     query_base = ctx_running(query_total, ctx, False, BF16, True)
-    query_running = z_running(query_parts, query_base, False)
-    locals_in = (queries, keys, values, out_grad, z, prefix)
-    (query_sum,) = call(query_sum_kernel, 16, "wwwwrs", "r", locals_in)
-    sums = z_gather(query_sum, group)
-    sums, query_running = lax.optimization_barrier((sums, query_running))
-    grad_queries, dfk, gv = call(query_grad_kernel, 8, "wwwwrs", "wff", locals_in)
-    suffix = from_owners(query_running)
+    spread = z_spread(where, query_parts, query_base)
+    grad_queries, dfk, gv, query_sum = call(
+        query_grad_kernel, 8, "wwwwrs", "wffg", (queries, keys, values, out_grad, z, prefix)
+    )
+    sums = z_gather(query_sum)
+    pieces = [spread[0]] + [None] * (group - 1)
+    for d in sorted(range(1, group), key=lambda d: -min(d, group - d)):
+        pairs = [(i, (i + d) % group) for i in range(group)]
+        pieces[d] = lax.ppermute(spread[d], "head", pairs)
     r = ctx_running(jnp.sum(sums, axis=0), ctx, False, F32, False)
     r = r + jnp.sum(jnp.where(ranks > place, sums, 0.0), axis=0)
-    grad_keys, grad_values = call(
-        key_grad_kernel, 16, "wwffsr", "ww", (keys, values, dfk, gv, suffix, r)
+    grad_keys, grad_values = key_grad(
+        where, (keys, values, dfk, gv, r), pieces, tokens, width
     )
     return grad_queries, grad_keys, grad_values
 

time: 194 us -> 197 us (1.015)
  the two profiles are of different devices: /device:TPU:1 before, /device:TPU:2 now
where the time goes in v3:
time: 197 us; the launch traced here: 196 us
  starting transfers between devices  82.2 us (42%)
  waiting for transfers between devices  75.4 us (38%)
  Pallas kernels  30.5 us (15%)
  other arithmetic  5.15 us (3%)
    ppermute x24, starting transfers between devices, hop(): return lax.ppermute(value, 'ctx', pairs)  38.2 us
    ppermute x24, waiting for transfers between devices, hop(): return lax.ppermute(value, 'ctx', pairs)  20 us
    all_to_all x2, waiting for transfers between devices, z_gather(): return lax.all_to_all(copies, 'head', 0, 0, tiled=True)  18.3 us
    ppermute x7, waiting for transfers between devices, shards(): pieces[d] = lax.ppermute(spread[d], 'head', pairs)  16.1 us
    pallas_call x3, Pallas kernels, head_call(): pl.pallas_call(functools.partial(kernel, step), grid=(heads // step,), in...  15.6 us
    ppermute x7, starting transfers between devices, shards(): pieces[d] = lax.ppermute(spread[d], 'head', pairs)  15.3 us
    all_to_all x1, waiting for transfers between devices, from_owners(): return lax.all_to_all(x, 'head', 0, 0, tiled=True).reshape(heads, HD, HD)  12.4 us
    all_to_all x2, starting transfers between devices, z_gather(): return lax.all_to_all(copies, 'head', 0, 0, tiled=True)  11.8 us
  transfers between devices with their start and end apart: 42, of which 22 were waited for; matrix products, arithmetic and copies ran while one was open for 3% of the time, Pallas kernels for 11%

profile of v3, /device:TPU:2, one launch (start us, length us, event | category | flops | bytes accessed | tf_op | source)
XLA Modules:
  0.0 195.8 jit_solution(10231417671327791068)
XLA Ops:
  0.6 3.2 %shard_map.67 = (bf16[32,128,128]{2,1,0:T(8,128)(2,1)}, f32[8,32,128]{2,1,0:T(8,128)}) custom-call(bf16[128,4096]{1,0:T(8,128)(2,1)} %k_ref.7, bf16[128,4096]{1,0:T(8,128)(2,1)} %v_ref.5), custom_call_target="tpu_custom_call" | custom-call | tf_op jit(solution)/shard_map/pallas_call | solution.py:172
  3.8 8.5 %all-to-all-start = ((f32[8,32,128]{2,1,0:T(8,128)}), f32[8,32,128]{2,1,0:T(8,128)S(1)}, u32[]{:S(2)}, u32[]{:S(2)}) async-start(f32[8,32,128]{2,1,0:T(8,128)} %get-tuple-element.27), calls=%async_computation | async-start | bytes 262144 | tf_op jit(solution)/shard_map/all_to_all | solution.py:298
  12.3 9.1 %all-to-all-done = f32[8,32,128]{2,1,0:T(8,128)S(1)} async-done(((f32[8,32,128]{2,1,0:T(8,128)}), f32[8,32,128]{2,1,0:T(8,128)S(1)}, u32[]{:S(2)}, u32[]{:S(2)}) %all-to-all-start) | async-done | bytes 131104 | tf_op jit(solution)/shard_map/all_to_all | solution.py:298
  21.5 3.6 %all-to-all-start.1 = ((bf16[8,512,128]{2,1,0:T(8,128)(2,1)}), bf16[8,512,128]{2,1,0:T(8,128)(2,1)S(1)}, u32[]{:S(2)}, u32[]{:S(2)}) async-start(bf16[8,512,128]{2,1,0:T(8,128)(2,1)} %bitcast.6), calls=%async_computation.1 | async-start | bytes 2097152 | tf_op jit(solution)/shard_map/all_to_all | solution.py:309
  25.2 1.2 collective-permute-done
  26.3 3.0 %collective-permute-start.3 = (f32[32,128]{1,0:T(8,128)S(1)}, f32[32,128]{1,0:T(8,128)S(1)}, u32[]{:S(2)}, u32[]{:S(2)}) collective-permute-start(f32[32,128]{1,0:T(8,128)S(1)} %add.142), channel_id=1, source_target_pairs={{0,48},{8,56},{16,0},{24,8},{32,16},{40,24},{48,32},{56,40},{64,11... | collective-permute-start | bytes 49160 | tf_op jit(solution)/shard_map/ppermute | solution.py:269
  29.4 0.6 collective-permute-start.2
  30.0 1.0 collective-permute-start.1
  31.0 3.6 %collective-permute-done.2 = f32[32,128]{1,0:T(8,128)S(1)} collective-permute-done((f32[32,128]{1,0:T(8,128)S(1)}, f32[32,128]{1,0:T(8,128)S(1)}, u32[]{:S(2)}, u32[]{:S(2)}) %collective-permute-start.2) | collective-permute-done | bytes 16416 | tf_op jit(solution)/shard_map/ppermute | solution.py:269
  34.9 0.7 collective-permute-start.6
  35.6 4.7 %collective-permute-start.5 = (f32[32,128]{1,0:T(8,128)S(1)}, f32[32,128]{1,0:T(8,128)S(1)}, u32[]{:S(2)}, u32[]{:S(2)}) collective-permute-start(f32[32,128]{1,0:T(8,128)S(1)} %add_add_fusion.3), channel_id=1, source_target_pairs={{0,128},{8,136},{16,144},{24,152},{32,160},{40,168},{48,176},{56,1... | collective-permute-start | bytes 49160 | tf_op jit(solution)/shard_map/ppermute | solution.py:269
  40.3 1.9 collective-permute-start.4
  42.3 3.6 %collective-permute-done.4 = f32[32,128]{1,0:T(8,128)S(1)} collective-permute-done((f32[32,128]{1,0:T(8,128)S(1)}, f32[32,128]{1,0:T(8,128)S(1)}, u32[]{:S(2)}, u32[]{:S(2)}) %collective-permute-start.4) | collective-permute-done | bytes 16416 | tf_op jit(solution)/shard_map/ppermute | solution.py:269
  46.5 4.5 %shard_map.68 = bf16[32,128,128]{2,1,0:T(8,128)(2,1)} custom-call(bf16[128,4096]{1,0:T(8,128)(2,1)} %q_ref.3, bf16[128,4096]{1,0:T(8,128)(2,1)} %k_ref.7, bf16[128,4096]{1,0:T(8,128)(2,1)} %g_ref.3, f32[32,128]{1,0:T(8,128)} %add_add_fusion.2.z_ref), custom_call_target="tpu_custom_call" | custom-call | tf_op jit(solution)/shard_map/pallas_call | solution.py:172
  51.0 1.3 all-to-all-done.1.x_ref
  52.4 5.7 %all-to-all-start.2 = ((bf16[8,512,128]{2,1,0:T(8,128)(2,1)}), bf16[8,512,128]{2,1,0:T(8,128)(2,1)S(1)}, u32[]{:S(2)}, u32[]{:S(2)}) async-start(bf16[8,512,128]{2,1,0:T(8,128)(2,1)} %bitcast.5), calls=%async_computation.2 | async-start | bytes 2097152 | tf_op jit(solution)/shard_map/all_to_all | solution.py:309
  58.1 2.1 %shard_map.69 = f32[512,128]{1,0:T(8,128)} custom-call(bf16[8,512,128]{2,1,0:T(8,128)(2,1)} %copy-done.1), custom_call_target="tpu_custom_call" | custom-call | tf_op jit(solution)/shard_map/pallas_call | solution.py:201
  60.2 1.7 collective-permute-done.7
  61.9 1.0 add.153
  62.9 1.0 collective-permute-start.10
  63.9 0.9 collective-permute-start.9
  64.8 1.3 collective-permute-start.8
  66.1 1.8 collective-permute-done.10
  67.9 2.1 %collective-permute-done.9 = bf16[256,128]{1,0:T(8,128)(2,1)S(1)} collective-permute-done((bf16[256,128]{1,0:T(8,128)(2,1)S(1)}, bf16[256,128]{1,0:T(8,128)(2,1)S(1)}, u32[]{:S(2)}, u32[]{:S(2)}) %collective-permute-start.9) | collective-permute-done | bytes 65568 | tf_op jit(solution)/shard_map/ppermute | solution.py:269
  70.0 0.6 collective-permute-done.8
  70.7 0.7 collective-permute-start.13
  71.4 4.7 %collective-permute-start.12 = (bf16[256,128]{1,0:T(8,128)(2,1)S(1)}, bf16[256,128]{1,0:T(8,128)(2,1)S(1)}, u32[]{:S(2)}, u32[]{:S(2)}) collective-permute-start(bf16[256,128]{1,0:T(8,128)(2,1)S(1)} %fusion.3), channel_id=1, source_target_pairs={{0,128},{8,136},{16,144},{24,152},{32,160},{40,168},{48,176},{56,1... | collective-permute-start | bytes 196616 | tf_op jit(solution)/shard_map/ppermute | solution.py:269
  76.0 1.9 collective-permute-start.11
  78.0 4.2 %collective-permute-done.11 = bf16[256,128]{1,0:T(8,128)(2,1)S(1)} collective-permute-done((bf16[256,128]{1,0:T(8,128)(2,1)S(1)}, bf16[256,128]{1,0:T(8,128)(2,1)S(1)}, u32[]{:S(2)}, u32[]{:S(2)}) %collective-permute-start.11) | collective-permute-done | bytes 65568 | tf_op jit(solution)/shard_map/ppermute | solution.py:269
  82.3 1.3 collective-permute-done.14
  83.7 0.7 maximum_add_fusion.base_ref
  84.4 2.4 %shard_map.70 = bf16[8,512,128]{2,1,0:T(8,128)(2,1)} custom-call(bf16[8,512,128]{2,1,0:T(8,128)(2,1)} %copy-done.1, f32[512,128]{1,0:T(8,128)} %maximum_add_fusion.base_ref), custom_call_target="tpu_custom_call" | custom-call | tf_op jit(solution)/shard_map/pallas_call | solution.py:220
  86.8 7.1 %all-to-all-start.3 = ((bf16[8,512,128]{2,1,0:T(8,128)(2,1)}), bf16[8,512,128]{2,1,0:T(8,128)(2,1)S(1)}, u32[]{:S(2)}, u32[]{:S(2)}) async-start(bf16[8,512,128]{2,1,0:T(8,128)(2,1)} %shard_map.70), calls=%async_computation.3 | async-start | bytes 2097152 | tf_op jit(solution)/shard_map/all_to_all | solution.py:312
  94.0 2.1 %shard_map.72 = f32[512,128]{1,0:T(8,128)} custom-call(bf16[8,512,128]{2,1,0:T(8,128)(2,1)} %copy-done), custom_call_target="tpu_custom_call" | custom-call | tf_op jit(solution)/shard_map/pallas_call | solution.py:201
  96.0 1.7 collective-permute-done.22
  97.8 1.0 add.174
  98.9 2.0 %collective-permute-start.24 = (bf16[256,128]{1,0:T(8,128)(2,1)S(1)}, bf16[256,128]{1,0:T(8,128)(2,1)S(1)}, u32[]{:S(2)}, u32[]{:S(2)}) collective-permute-start(bf16[256,128]{1,0:T(8,128)(2,1)S(1)} %fusion.9), channel_id=1, source_target_pairs={{0,32},{8,40},{16,48},{24,56},{32,0},{40,8},{48,16},{56,24},{64,96... | collective-permute-start | bytes 196616 | tf_op jit(solution)/shard_map/ppermute | solution.py:269
  100.9 1.6 collective-permute-start.23
  102.5 3.1 %collective-permute-done.25 = bf16[256,128]{1,0:T(8,128)(2,1)S(1)} collective-permute-done((bf16[256,128]{1,0:T(8,128)(2,1)S(1)}, bf16[256,128]{1,0:T(8,128)(2,1)S(1)}, u32[]{:S(2)}, u32[]{:S(2)}) %collective-permute-start.25) | collective-permute-done | bytes 65568 | tf_op jit(solution)/shard_map/ppermute | solution.py:269
  106.2 0.8 collective-permute-start.28
  107.1 1.3 collective-permute-start.27
  108.4 2.2 %collective-permute-start.26 = (bf16[256,128]{1,0:T(8,128)(2,1)S(1)}, bf16[256,128]{1,0:T(8,128)(2,1)S(1)}, u32[]{:S(2)}, u32[]{:S(2)}) collective-permute-start(bf16[256,128]{1,0:T(8,128)(2,1)S(1)} %fusion.7), channel_id=1, source_target_pairs={{64,0},{72,8},{80,16},{88,24},{96,32},{104,40},{112,48},{120,56},{... | collective-permute-start | bytes 196616 | tf_op jit(solution)/shard_map/ppermute | solution.py:269
  110.6 12.4 %all-to-all-done.3 = bf16[8,512,128]{2,1,0:T(8,128)(2,1)S(1)} async-done(((bf16[8,512,128]{2,1,0:T(8,128)(2,1)}), bf16[8,512,128]{2,1,0:T(8,128)(2,1)S(1)}, u32[]{:S(2)}, u32[]{:S(2)}) %all-to-all-start.3) | async-done | bytes 1048608 | tf_op jit(solution)/shard_map/all_to_all | solution.py:312
  123.0 1.0 copy-done.2
  124.0 7.9 %shard_map.71 = (bf16[128,4096]{1,0:T(8,128)(2,1)}, f32[128,4096]{1,0:T(8,128)}, f32[128,4096]{1,0:T(8,128)}, f32[8,32,128]{2,1,0:T(8,128)}) custom-call(bf16[128,4096]{1,0:T(8,128)(2,1)} %q_ref.3, bf16[128,4096]{1,0:T(8,128)(2,1)} %k_ref.7, bf16[128,4096]{1,0:T(8,128)(2,1)} %v_ref.5, bf16[128,4096]{1,0:T(8,128)(2,1)} %g_ref.3, ...), custom_call_target="tpu_custom_call" | custom-call | tf_op jit(solution)/shard_map/pallas_call | solution.py:172
  131.9 3.4 %all-to-all-start.4 = ((f32[8,32,128]{2,1,0:T(8,128)}), f32[8,32,128]{2,1,0:T(8,128)S(1)}, u32[]{:S(2)}, u32[]{:S(2)}) async-start(f32[8,32,128]{2,1,0:T(8,128)} %get-tuple-element.37), calls=%async_computation.4 | async-start | bytes 262144 | tf_op jit(solution)/shard_map/all_to_all | solution.py:298
  135.5 9.2 %all-to-all-done.4 = f32[8,32,128]{2,1,0:T(8,128)S(1)} async-done(((f32[8,32,128]{2,1,0:T(8,128)}), f32[8,32,128]{2,1,0:T(8,128)S(1)}, u32[]{:S(2)}, u32[]{:S(2)}) %all-to-all-start.4) | async-done | bytes 131104 | tf_op jit(solution)/shard_map/all_to_all | solution.py:298
  144.9 1.1 collective-permute-done.15
  146.1 2.0 %collective-permute-start.17 = (f32[32,128]{1,0:T(8,128)S(1)}, f32[32,128]{1,0:T(8,128)S(1)}, u32[]{:S(2)}, u32[]{:S(2)}) collective-permute-start(f32[32,128]{1,0:T(8,128)S(1)} %add.163), channel_id=1, source_target_pairs={{0,32},{8,40},{16,48},{24,56},{32,0},{40,8},{48,16},{56,24},{64,96... | collective-permute-start | bytes 49160 | tf_op jit(solution)/shard_map/ppermute | solution.py:269
  148.1 1.7 collective-permute-start.16
  149.7 0.7 maximum_add_fusion.1.base_ref
  150.5 2.4 %shard_map.73 = (bf16[512,128]{1,0:T(8,128)(2,1)}, bf16[512,128]{1,0:T(8,128)(2,1)}, bf16[512,128]{1,0:T(8,128)(2,1)}, bf16[512,128]{1,0:T(8,128)(2,1)}, bf16[51...) custom-call(s32[1]{0:T(128)} %bitcast.3.place_ref, ...), custom_call_target="tpu_custom_call" | custom-call | tf_op jit(solution)/shard_map/pallas_call | solution.py:231
  153.9 0.7 collective-permute-start.21
  154.6 1.3 collective-permute-start.20
  155.9 2.2 %collective-permute-start.19 = (f32[32,128]{1,0:T(8,128)S(1)}, f32[32,128]{1,0:T(8,128)S(1)}, u32[]{:S(2)}, u32[]{:S(2)}) collective-permute-start(f32[32,128]{1,0:T(8,128)S(1)} %add_add_fusion.1), channel_id=1, source_target_pairs={{64,0},{72,8},{80,16},{88,24},{96,32},{104,40},{112,48},{120,56},{... | collective-permute-start | bytes 49160 | tf_op jit(solution)/shard_map/ppermute | solution.py:269
  158.1 5.2 %collective-permute-done.30.refs_1_ = bf16[512,128]{1,0:T(8,128)(2,1)S(1)} collective-permute-done((bf16[512,128]{1,0:T(8,128)(2,1)}, bf16[512,128]{1,0:T(8,128)(2,1)S(1)}, u32[]{:S(2)}, u32[]{:S(2)}) %collective-permute-start.30) | collective-permute-done | bytes 131104 | tf_op jit(solution)/shard_map/ppermute | solution.py:341
  163.3 2.8 %collective-permute-start.33 = (bf16[512,128]{1,0:T(8,128)(2,1)}, bf16[512,128]{1,0:T(8,128)(2,1)S(1)}, u32[]{:S(2)}, u32[]{:S(2)}) collective-permute-start(bf16[512,128]{1,0:T(8,128)(2,1)} %get-tuple-element.43), channel_id=1, source_target_pairs={{0,4},{1,5},{2,6},{3,7},{4,0},{5,1},{6,2},{7,3},{8,12},{9,13},{10,... | collective-permute-start | bytes 393224 | tf_op jit(solution)/shard_map/ppermute | solution.py:341
  166.0 10.9 %collective-permute-start.34 = (bf16[512,128]{1,0:T(8,128)(2,1)}, bf16[512,128]{1,0:T(8,128)(2,1)S(1)}, u32[]{:S(2)}, u32[]{:S(2)}) collective-permute-start(bf16[512,128]{1,0:T(8,128)(2,1)} %get-tuple-element.44), channel_id=1, source_target_pairs={{0,5},{1,6},{2,7},{3,0},{4,1},{5,2},{6,3},{7,4},{8,13},{9,14},{10,... | collective-permute-start | bytes 393224 | tf_op jit(solution)/shard_map/ppermute | solution.py:341
  177.0 0.6 collective-permute-start.36
  177.6 0.6 add_add_fusion.rz_ref
  178.3 5.8 %collective-permute-done.34.refs_5_ = bf16[512,128]{1,0:T(8,128)(2,1)S(1)} collective-permute-done((bf16[512,128]{1,0:T(8,128)(2,1)}, bf16[512,128]{1,0:T(8,128)(2,1)S(1)}, u32[]{:S(2)}, u32[]{:S(2)}) %collective-permute-start.34) | collective-permute-done | bytes 131104 | tf_op jit(solution)/shard_map/ppermute | solution.py:341
  184.0 4.6 %collective-permute-done.35.refs_6_ = bf16[512,128]{1,0:T(8,128)(2,1)S(1)} collective-permute-done((bf16[512,128]{1,0:T(8,128)(2,1)}, bf16[512,128]{1,0:T(8,128)(2,1)S(1)}, u32[]{:S(2)}, u32[]{:S(2)}) %collective-permute-start.35) | collective-permute-done | bytes 131104 | tf_op jit(solution)/shard_map/ppermute | solution.py:341
  188.6 0.6 collective-permute-done.36.refs_7_
  189.9 5.9 %shard_map.74 = (bf16[128,4096]{1,0:T(8,128)(2,1)}, bf16[128,4096]{1,0:T(8,128)(2,1)}) custom-call(s32[1]{0:T(128)} %bitcast.3.place_ref, bf16[128,4096]{1,0:T(8,128)(2,1)} %k_ref.7, bf16[128,4096]{1,0:T(8,128)(2,1)} %v_ref.5, f32[128,4096]{1,0:T(8,128)} %get-tuple-element.35.dfk_ref, f32[128,4096]{1,0:T(8,128)} %get-tuple-element.36.gv_ref, ...), custom_call_target="tpu_custom_call" | custom-call | tf_op jit(solution)/shard_map/pallas_call | solution.py:150
  (70 shorter events, 4.2 us)
Async XLA Ops:
  3.8 17.6 %all-to-all-start = ((f32[8,32,128]{2,1,0:T(8,128)}), f32[8,32,128]{2,1,0:T(8,128)S(1)}, u32[]{:S(2)}, u32[]{:S(2)}) async-start(f32[8,32,128]{2,1,0:T(8,128)} %get-tuple-element.27), calls=%async_computation | async-start | bytes 262144 | tf_op jit(solution)/shard_map/all_to_all | solution.py:298
  21.5 30.9 %all-to-all-start.1 = ((bf16[8,512,128]{2,1,0:T(8,128)(2,1)}), bf16[8,512,128]{2,1,0:T(8,128)(2,1)S(1)}, u32[]{:S(2)}, u32[]{:S(2)}) async-start(bf16[8,512,128]{2,1,0:T(8,128)(2,1)} %bitcast.6), calls=%async_computation.1 | async-start | bytes 2097152 | tf_op jit(solution)/shard_map/all_to_all | solution.py:309
  25.1 1.3 collective-permute-start
  26.3 4.6 %collective-permute-start.3 = (f32[32,128]{1,0:T(8,128)S(1)}, f32[32,128]{1,0:T(8,128)S(1)}, u32[]{:S(2)}, u32[]{:S(2)}) collective-permute-start(f32[32,128]{1,0:T(8,128)S(1)} %add.142), channel_id=1, source_target_pairs={{0,48},{8,56},{16,0},{24,8},{32,16},{40,24},{48,32},{56,40},{64,11... | collective-permute-start | bytes 49160 | tf_op jit(solution)/shard_map/ppermute | solution.py:269
  29.4 5.2 %collective-permute-start.2 = (f32[32,128]{1,0:T(8,128)S(1)}, f32[32,128]{1,0:T(8,128)S(1)}, u32[]{:S(2)}, u32[]{:S(2)}) collective-permute-start(f32[32,128]{1,0:T(8,128)S(1)} %add.142), channel_id=1, source_target_pairs={{0,32},{8,40},{16,48},{24,56},{32,0},{40,8},{48,16},{56,24},{64,96... | collective-permute-start | bytes 49160 | tf_op jit(solution)/shard_map/ppermute | solution.py:269
  30.0 4.9 %collective-permute-start.1 = (f32[32,128]{1,0:T(8,128)S(1)}, f32[32,128]{1,0:T(8,128)S(1)}, u32[]{:S(2)}, u32[]{:S(2)}) collective-permute-start(f32[32,128]{1,0:T(8,128)S(1)} %add.142), channel_id=1, source_target_pairs={{0,16},{8,24},{16,32},{24,40},{32,48},{40,56},{48,0},{56,8},{64,80... | collective-permute-start | bytes 49160 | tf_op jit(solution)/shard_map/ppermute | solution.py:269
  34.9 7.3 %collective-permute-start.6 = (f32[32,128]{1,0:T(8,128)S(1)}, f32[32,128]{1,0:T(8,128)S(1)}, u32[]{:S(2)}, u32[]{:S(2)}) collective-permute-start(f32[32,128]{1,0:T(8,128)S(1)} %add_add_fusion.3), channel_id=1, source_target_pairs={{0,192},{8,200},{16,208},{24,216},{32,224},{40,232},{48,240},{56,2... | collective-permute-start | bytes 49160 | tf_op jit(solution)/shard_map/ppermute | solution.py:269
  35.6 6.7 %collective-permute-start.5 = (f32[32,128]{1,0:T(8,128)S(1)}, f32[32,128]{1,0:T(8,128)S(1)}, u32[]{:S(2)}, u32[]{:S(2)}) collective-permute-start(f32[32,128]{1,0:T(8,128)S(1)} %add_add_fusion.3), channel_id=1, source_target_pairs={{0,128},{8,136},{16,144},{24,152},{32,160},{40,168},{48,176},{56,1... | collective-permute-start | bytes 49160 | tf_op jit(solution)/shard_map/ppermute | solution.py:269
  40.3 5.6 %collective-permute-start.4 = (f32[32,128]{1,0:T(8,128)S(1)}, f32[32,128]{1,0:T(8,128)S(1)}, u32[]{:S(2)}, u32[]{:S(2)}) collective-permute-start(f32[32,128]{1,0:T(8,128)S(1)} %add_add_fusion.3), channel_id=1, source_target_pairs={{0,64},{8,72},{16,80},{24,88},{32,96},{40,104},{48,112},{56,120},{... | collective-permute-start | bytes 49160 | tf_op jit(solution)/shard_map/ppermute | solution.py:269
  52.4 5.7 %copy-start.1 = (bf16[8,512,128]{2,1,0:T(8,128)(2,1)}, bf16[8,512,128]{2,1,0:T(8,128)(2,1)S(1)}, u32[]{:S(2)}) copy-start(bf16[8,512,128]{2,1,0:T(8,128)(2,1)S(1)} %all-to-all-done.1.x_ref) | copy-start | bytes 3145732
  52.4 34.5 %all-to-all-start.2 = ((bf16[8,512,128]{2,1,0:T(8,128)(2,1)}), bf16[8,512,128]{2,1,0:T(8,128)(2,1)S(1)}, u32[]{:S(2)}, u32[]{:S(2)}) async-start(bf16[8,512,128]{2,1,0:T(8,128)(2,1)} %bitcast.5), calls=%async_computation.2 | async-start | bytes 2097152 | tf_op jit(solution)/shard_map/all_to_all | solution.py:309
  60.2 1.7 collective-permute-start.7
  62.9 5.0 %collective-permute-start.10 = (bf16[256,128]{1,0:T(8,128)(2,1)S(1)}, bf16[256,128]{1,0:T(8,128)(2,1)S(1)}, u32[]{:S(2)}, u32[]{:S(2)}) collective-permute-start(bf16[256,128]{1,0:T(8,128)(2,1)S(1)} %fusion.8), channel_id=1, source_target_pairs={{0,48},{8,56},{16,0},{24,8},{32,16},{40,24},{48,32},{56,40},{64,11... | collective-permute-start | bytes 196616 | tf_op jit(solution)/shard_map/ppermute | solution.py:269
  63.9 6.1 %collective-permute-start.9 = (bf16[256,128]{1,0:T(8,128)(2,1)S(1)}, bf16[256,128]{1,0:T(8,128)(2,1)S(1)}, u32[]{:S(2)}, u32[]{:S(2)}) collective-permute-start(bf16[256,128]{1,0:T(8,128)(2,1)S(1)} %fusion.8), channel_id=1, source_target_pairs={{0,32},{8,40},{16,48},{24,56},{32,0},{40,8},{48,16},{56,24},{64,96... | collective-permute-start | bytes 196616 | tf_op jit(solution)/shard_map/ppermute | solution.py:269
  64.8 5.8 %collective-permute-start.8 = (bf16[256,128]{1,0:T(8,128)(2,1)S(1)}, bf16[256,128]{1,0:T(8,128)(2,1)S(1)}, u32[]{:S(2)}, u32[]{:S(2)}) collective-permute-start(bf16[256,128]{1,0:T(8,128)(2,1)S(1)} %fusion.8), channel_id=1, source_target_pairs={{0,16},{8,24},{16,32},{24,40},{32,48},{40,56},{48,0},{56,8},{64,80... | collective-permute-start | bytes 196616 | tf_op jit(solution)/shard_map/ppermute | solution.py:269
  70.7 7.3 %collective-permute-start.13 = (bf16[256,128]{1,0:T(8,128)(2,1)S(1)}, bf16[256,128]{1,0:T(8,128)(2,1)S(1)}, u32[]{:S(2)}, u32[]{:S(2)}) collective-permute-start(bf16[256,128]{1,0:T(8,128)(2,1)S(1)} %fusion.3), channel_id=1, source_target_pairs={{0,192},{8,200},{16,208},{24,216},{32,224},{40,232},{48,240},{56,2... | collective-permute-start | bytes 196616 | tf_op jit(solution)/shard_map/ppermute | solution.py:269
  71.4 6.6 %collective-permute-start.12 = (bf16[256,128]{1,0:T(8,128)(2,1)S(1)}, bf16[256,128]{1,0:T(8,128)(2,1)S(1)}, u32[]{:S(2)}, u32[]{:S(2)}) collective-permute-start(bf16[256,128]{1,0:T(8,128)(2,1)S(1)} %fusion.3), channel_id=1, source_target_pairs={{0,128},{8,136},{16,144},{24,152},{32,160},{40,168},{48,176},{56,1... | collective-permute-start | bytes 196616 | tf_op jit(solution)/shard_map/ppermute | solution.py:269
  76.0 6.2 %collective-permute-start.11 = (bf16[256,128]{1,0:T(8,128)(2,1)S(1)}, bf16[256,128]{1,0:T(8,128)(2,1)S(1)}, u32[]{:S(2)}, u32[]{:S(2)}) collective-permute-start(bf16[256,128]{1,0:T(8,128)(2,1)S(1)} %fusion.3), channel_id=1, source_target_pairs={{0,64},{8,72},{16,80},{24,88},{32,96},{40,104},{48,112},{56,120},{... | collective-permute-start | bytes 196616 | tf_op jit(solution)/shard_map/ppermute | solution.py:269
  82.2 1.4 collective-permute-start.14
  86.8 7.1 %copy-start = (bf16[8,512,128]{2,1,0:T(8,128)(2,1)}, bf16[8,512,128]{2,1,0:T(8,128)(2,1)S(1)}, u32[]{:S(2)}) copy-start(bf16[8,512,128]{2,1,0:T(8,128)(2,1)S(1)} %all-to-all-done.2.x_ref) | copy-start | bytes 3145732
  86.8 36.2 %all-to-all-start.3 = ((bf16[8,512,128]{2,1,0:T(8,128)(2,1)}), bf16[8,512,128]{2,1,0:T(8,128)(2,1)S(1)}, u32[]{:S(2)}, u32[]{:S(2)}) async-start(bf16[8,512,128]{2,1,0:T(8,128)(2,1)} %shard_map.70), calls=%async_computation.3 | async-start | bytes 2097152 | tf_op jit(solution)/shard_map/all_to_all | solution.py:312
  96.0 1.7 collective-permute-start.22
  98.8 6.8 %collective-permute-start.25 = (bf16[256,128]{1,0:T(8,128)(2,1)S(1)}, bf16[256,128]{1,0:T(8,128)(2,1)S(1)}, u32[]{:S(2)}, u32[]{:S(2)}) collective-permute-start(bf16[256,128]{1,0:T(8,128)(2,1)S(1)} %fusion.9), channel_id=1, source_target_pairs={{0,16},{8,24},{16,32},{24,40},{32,48},{40,56},{48,0},{56,8},{64,80... | collective-permute-start | bytes 196616 | tf_op jit(solution)/shard_map/ppermute | solution.py:269
  98.9 6.7 %collective-permute-start.24 = (bf16[256,128]{1,0:T(8,128)(2,1)S(1)}, bf16[256,128]{1,0:T(8,128)(2,1)S(1)}, u32[]{:S(2)}, u32[]{:S(2)}) collective-permute-start(bf16[256,128]{1,0:T(8,128)(2,1)S(1)} %fusion.9), channel_id=1, source_target_pairs={{0,32},{8,40},{16,48},{24,56},{32,0},{40,8},{48,16},{56,24},{64,96... | collective-permute-start | bytes 196616 | tf_op jit(solution)/shard_map/ppermute | solution.py:269
  100.9 5.3 %collective-permute-start.23 = (bf16[256,128]{1,0:T(8,128)(2,1)S(1)}, bf16[256,128]{1,0:T(8,128)(2,1)S(1)}, u32[]{:S(2)}, u32[]{:S(2)}) collective-permute-start(bf16[256,128]{1,0:T(8,128)(2,1)S(1)} %fusion.9), channel_id=1, source_target_pairs={{0,48},{8,56},{16,0},{24,8},{32,16},{40,24},{48,32},{56,40},{64,11... | collective-permute-start | bytes 196616 | tf_op jit(solution)/shard_map/ppermute | solution.py:269
  106.2 29.0 %collective-permute-start.28 = (bf16[256,128]{1,0:T(8,128)(2,1)S(1)}, bf16[256,128]{1,0:T(8,128)(2,1)S(1)}, u32[]{:S(2)}, u32[]{:S(2)}) collective-permute-start(bf16[256,128]{1,0:T(8,128)(2,1)S(1)} %fusion.7), channel_id=1, source_target_pairs={{192,0},{200,8},{208,16},{216,24},{224,32},{232,40},{240,48},{248,... | collective-permute-start | bytes 196616 | tf_op jit(solution)/shard_map/ppermute | solution.py:269
  107.1 28.2 %collective-permute-start.27 = (bf16[256,128]{1,0:T(8,128)(2,1)S(1)}, bf16[256,128]{1,0:T(8,128)(2,1)S(1)}, u32[]{:S(2)}, u32[]{:S(2)}) collective-permute-start(bf16[256,128]{1,0:T(8,128)(2,1)S(1)} %fusion.7), channel_id=1, source_target_pairs={{128,0},{136,8},{144,16},{152,24},{160,32},{168,40},{176,48},{184,... | collective-permute-start | bytes 196616 | tf_op jit(solution)/shard_map/ppermute | solution.py:269
  108.4 26.9 %collective-permute-start.26 = (bf16[256,128]{1,0:T(8,128)(2,1)S(1)}, bf16[256,128]{1,0:T(8,128)(2,1)S(1)}, u32[]{:S(2)}, u32[]{:S(2)}) collective-permute-start(bf16[256,128]{1,0:T(8,128)(2,1)S(1)} %fusion.7), channel_id=1, source_target_pairs={{64,0},{72,8},{80,16},{88,24},{96,32},{104,40},{112,48},{120,56},{... | collective-permute-start | bytes 196616 | tf_op jit(solution)/shard_map/ppermute | solution.py:269
  123.0 1.0 copy-start.2
  131.9 12.8 %all-to-all-start.4 = ((f32[8,32,128]{2,1,0:T(8,128)}), f32[8,32,128]{2,1,0:T(8,128)S(1)}, u32[]{:S(2)}, u32[]{:S(2)}) async-start(f32[8,32,128]{2,1,0:T(8,128)} %get-tuple-element.37), calls=%async_computation.4 | async-start | bytes 262144 | tf_op jit(solution)/shard_map/all_to_all | solution.py:298
  135.4 9.5 %collective-permute-start.29 = (f32[256,128]{1,0:T(8,128)S(1)}, f32[256,128]{1,0:T(8,128)S(1)}, u32[]{:S(2)}, u32[]{:S(2)}) collective-permute-start(f32[256,128]{1,0:T(8,128)S(1)} %fusion.6), channel_id=1, source_target_pairs={{0,8},{8,0},{16,24},{24,16},{32,40},{40,32},{48,56},{56,48},{64,72... | collective-permute-start | bytes 393224 | tf_op jit(solution)/shard_map/ppermute | solution.py:275
  144.8 1.3 collective-permute-start.15
  146.1 7.8 %collective-permute-start.18 = (f32[32,128]{1,0:T(8,128)S(1)}, f32[32,128]{1,0:T(8,128)S(1)}, u32[]{:S(2)}, u32[]{:S(2)}) collective-permute-start(f32[32,128]{1,0:T(8,128)S(1)} %add.163), channel_id=1, source_target_pairs={{0,16},{8,24},{16,32},{24,40},{32,48},{40,56},{48,0},{56,8},{64,80... | collective-permute-start | bytes 49160 | tf_op jit(solution)/shard_map/ppermute | solution.py:269
  146.1 7.8 %collective-permute-start.17 = (f32[32,128]{1,0:T(8,128)S(1)}, f32[32,128]{1,0:T(8,128)S(1)}, u32[]{:S(2)}, u32[]{:S(2)}) collective-permute-start(f32[32,128]{1,0:T(8,128)S(1)} %add.163), channel_id=1, source_target_pairs={{0,32},{8,40},{16,48},{24,56},{32,0},{40,8},{48,16},{56,24},{64,96... | collective-permute-start | bytes 49160 | tf_op jit(solution)/shard_map/ppermute | solution.py:269
  148.1 5.8 %collective-permute-start.16 = (f32[32,128]{1,0:T(8,128)S(1)}, f32[32,128]{1,0:T(8,128)S(1)}, u32[]{:S(2)}, u32[]{:S(2)}) collective-permute-start(f32[32,128]{1,0:T(8,128)S(1)} %add.163), channel_id=1, source_target_pairs={{0,48},{8,56},{16,0},{24,8},{32,16},{40,24},{48,32},{56,40},{64,11... | collective-permute-start | bytes 49160 | tf_op jit(solution)/shard_map/ppermute | solution.py:269
  152.9 10.4 %collective-permute-start.30 = (bf16[512,128]{1,0:T(8,128)(2,1)}, bf16[512,128]{1,0:T(8,128)(2,1)S(1)}, u32[]{:S(2)}, u32[]{:S(2)}) collective-permute-start(bf16[512,128]{1,0:T(8,128)(2,1)} %get-tuple-element.40), channel_id=1, source_target_pairs={{0,1},{1,2},{2,3},{3,4},{4,5},{5,6},{6,7},{7,0},{8,9},{9,10},{10,1... | collective-permute-start | bytes 393224 | tf_op jit(solution)/shard_map/ppermute | solution.py:341
  153.5 9.8 %collective-permute-start.31 = (bf16[512,128]{1,0:T(8,128)(2,1)}, bf16[512,128]{1,0:T(8,128)(2,1)S(1)}, u32[]{:S(2)}, u32[]{:S(2)}) collective-permute-start(bf16[512,128]{1,0:T(8,128)(2,1)} %get-tuple-element.41), channel_id=1, source_target_pairs={{0,2},{1,3},{2,4},{3,5},{4,6},{5,7},{6,0},{7,1},{8,10},{9,11},{10,... | collective-permute-start | bytes 393224 | tf_op jit(solution)/shard_map/ppermute | solution.py:341
  153.9 12.1 %collective-permute-start.21 = (f32[32,128]{1,0:T(8,128)S(1)}, f32[32,128]{1,0:T(8,128)S(1)}, u32[]{:S(2)}, u32[]{:S(2)}) collective-permute-start(f32[32,128]{1,0:T(8,128)S(1)} %add_add_fusion.1), channel_id=1, source_target_pairs={{192,0},{200,8},{208,16},{216,24},{224,32},{232,40},{240,48},{248,... | collective-permute-start | bytes 49160 | tf_op jit(solution)/shard_map/ppermute | solution.py:269
  154.6 22.4 %collective-permute-start.20 = (f32[32,128]{1,0:T(8,128)S(1)}, f32[32,128]{1,0:T(8,128)S(1)}, u32[]{:S(2)}, u32[]{:S(2)}) collective-permute-start(f32[32,128]{1,0:T(8,128)S(1)} %add_add_fusion.1), channel_id=1, source_target_pairs={{128,0},{136,8},{144,16},{152,24},{160,32},{168,40},{176,48},{184,... | collective-permute-start | bytes 49160 | tf_op jit(solution)/shard_map/ppermute | solution.py:269
  155.9 21.1 %collective-permute-start.19 = (f32[32,128]{1,0:T(8,128)S(1)}, f32[32,128]{1,0:T(8,128)S(1)}, u32[]{:S(2)}, u32[]{:S(2)}) collective-permute-start(f32[32,128]{1,0:T(8,128)S(1)} %add_add_fusion.1), channel_id=1, source_target_pairs={{64,0},{72,8},{80,16},{88,24},{96,32},{104,40},{112,48},{120,56},{... | collective-permute-start | bytes 49160 | tf_op jit(solution)/shard_map/ppermute | solution.py:269
  163.3 26.0 %copy-start.3 = (bf16[512,128]{1,0:T(8,128)(2,1)}, bf16[512,128]{1,0:T(8,128)(2,1)S(1)}, u32[]{:S(2)}) copy-start(bf16[512,128]{1,0:T(8,128)(2,1)S(1)} %collective-permute-done.30.refs_1_) | copy-start | bytes 393220
  163.3 15.0 %collective-permute-start.32 = (bf16[512,128]{1,0:T(8,128)(2,1)}, bf16[512,128]{1,0:T(8,128)(2,1)S(1)}, u32[]{:S(2)}, u32[]{:S(2)}) collective-permute-start(bf16[512,128]{1,0:T(8,128)(2,1)} %get-tuple-element.42), channel_id=1, source_target_pairs={{0,3},{1,4},{2,5},{3,6},{4,7},{5,0},{6,1},{7,2},{8,11},{9,12},{10,... | collective-permute-start | bytes 393224 | tf_op jit(solution)/shard_map/ppermute | solution.py:341
  163.3 26.0 %copy-start.4 = (bf16[512,128]{1,0:T(8,128)(2,1)}, bf16[512,128]{1,0:T(8,128)(2,1)S(1)}, u32[]{:S(2)}) copy-start(bf16[512,128]{1,0:T(8,128)(2,1)S(1)} %collective-permute-done.31.refs_2_) | copy-start | bytes 393220
  163.3 15.0 %collective-permute-start.33 = (bf16[512,128]{1,0:T(8,128)(2,1)}, bf16[512,128]{1,0:T(8,128)(2,1)S(1)}, u32[]{:S(2)}, u32[]{:S(2)}) collective-permute-start(bf16[512,128]{1,0:T(8,128)(2,1)} %get-tuple-element.43), channel_id=1, source_target_pairs={{0,4},{1,5},{2,6},{3,7},{4,0},{5,1},{6,2},{7,3},{8,12},{9,13},{10,... | collective-permute-start | bytes 393224 | tf_op jit(solution)/shard_map/ppermute | solution.py:341
  166.0 18.0 %collective-permute-start.34 = (bf16[512,128]{1,0:T(8,128)(2,1)}, bf16[512,128]{1,0:T(8,128)(2,1)S(1)}, u32[]{:S(2)}, u32[]{:S(2)}) collective-permute-start(bf16[512,128]{1,0:T(8,128)(2,1)} %get-tuple-element.44), channel_id=1, source_target_pairs={{0,5},{1,6},{2,7},{3,0},{4,1},{5,2},{6,3},{7,4},{8,13},{9,14},{10,... | collective-permute-start | bytes 393224 | tf_op jit(solution)/shard_map/ppermute | solution.py:341
  177.0 11.6 %collective-permute-start.35 = (bf16[512,128]{1,0:T(8,128)(2,1)}, bf16[512,128]{1,0:T(8,128)(2,1)S(1)}, u32[]{:S(2)}, u32[]{:S(2)}) collective-permute-start(bf16[512,128]{1,0:T(8,128)(2,1)} %get-tuple-element.45), channel_id=1, source_target_pairs={{0,6},{1,7},{2,0},{3,1},{4,2},{5,3},{6,4},{7,5},{8,14},{9,15},{10,... | collective-permute-start | bytes 393224 | tf_op jit(solution)/shard_map/ppermute | solution.py:341
  177.0 12.2 %collective-permute-start.36 = (bf16[512,128]{1,0:T(8,128)(2,1)}, bf16[512,128]{1,0:T(8,128)(2,1)S(1)}, u32[]{:S(2)}, u32[]{:S(2)}) collective-permute-start(bf16[512,128]{1,0:T(8,128)(2,1)} %get-tuple-element.46), channel_id=1, source_target_pairs={{0,7},{1,0},{2,1},{3,2},{4,3},{5,4},{6,5},{7,6},{8,15},{9,8},{10,9... | collective-permute-start | bytes 393224 | tf_op jit(solution)/shard_map/ppermute | solution.py:341
  178.2 11.0 %copy-start.5 = (bf16[512,128]{1,0:T(8,128)(2,1)}, bf16[512,128]{1,0:T(8,128)(2,1)S(1)}, u32[]{:S(2)}) copy-start(bf16[512,128]{1,0:T(8,128)(2,1)S(1)} %collective-permute-done.32.refs_3_) | copy-start | bytes 393220
  178.2 11.0 %copy-start.6 = (bf16[512,128]{1,0:T(8,128)(2,1)}, bf16[512,128]{1,0:T(8,128)(2,1)S(1)}, u32[]{:S(2)}) copy-start(bf16[512,128]{1,0:T(8,128)(2,1)S(1)} %collective-permute-done.33.refs_4_) | copy-start | bytes 393220
  184.0 5.2 %copy-start.7 = (bf16[512,128]{1,0:T(8,128)(2,1)}, bf16[512,128]{1,0:T(8,128)(2,1)S(1)}, u32[]{:S(2)}) copy-start(bf16[512,128]{1,0:T(8,128)(2,1)S(1)} %collective-permute-done.34.refs_5_) | copy-start | bytes 393220
  188.6 0.7 copy-start.8
  189.2 0.7 copy-start.9

commit v4 on v3

--- a/solution.py
+++ b/solution.py
@@ -123,37 +123,54 @@
         dfk_ref[:, columns(j)] = dot_tn(mixing[j], fq[j])
 
 
-def key_grad_kernel(
-    place_ref, k_ref, v_ref, dfk_ref, gv_ref, rz_ref, *refs
-):
-    pieces, (gk_ref, gv_out_ref) = refs[:-2], refs[-2:]
-    group = len(pieces)
-    per = pieces[0].shape[0] // HD
+def key_grad_kernel(place_ref, k_hbm, v_hbm, dfk_hbm, gv_hbm, rz_ref, *refs):
+    group = len(refs) - 7
+    pieces, (gk_ref, gv_out_ref), loaded, sems = refs[:group], refs[group : group + 2], refs[-5:-1], refs[-1]
+    rows = pieces[0].shape[0]
+    owners = [lax.rem(place_ref[0] + group - d, group) for d in range(group)]
+    ats = [pl.multiple_of(owner * rows, rows) for owner in owners]
+    copies = [
+        [
+            pltpu.make_async_copy(src.at[:, pl.ds(at, rows)], dst.at[d], sems.at[n, d])
+            for n, (src, dst) in enumerate(zip((k_hbm, v_hbm, dfk_hbm, gv_hbm), loaded))
+        ]
+        for d, at in enumerate(ats)
+    ]
+    for some in copies:
+        for copy in some:
+            copy.start()
+    k, v, dfk_in, gv_in = loaded
     for first in range(0, group, 2):
         work = []
         for d in (first, first + 1):
-            owner = lax.rem(place_ref[0] + group - d, group)
-            for j in range(per):
-                at = pl.ds(pl.multiple_of(owner * per * HD, per * HD) + j * HD, HD)
-                work.append((pieces[d][j * HD : (j + 1) * HD, :], at, owner * per + j))
-        fk32 = [feature(k_ref[:, at].astype(F32)) for _, at, _ in work]
-        dfk = [dot_nt(v_ref[:, at], state) for state, at, _ in work]
-        gv = [dot_nn(f.astype(BF16), state) for f, (state, _, _) in zip(fk32, work)]
-        for f, whole, (_, at, head) in zip(fk32, dfk, work):
-            whole = whole + dfk_ref[:, at] + rz_ref[pl.ds(head, 1), :]
-            gk_ref[:, at] = (whole * jnp.minimum(f, 1.0)).astype(BF16)
-        for part, (_, at, _) in zip(gv, work):
-            gv_out_ref[:, at] = (part + gv_ref[:, at]).astype(BF16)
-
-
-def key_grad(place, arrays, pieces, tokens, width):
+            for copy in copies[d]:
+                copy.wait()
+            work += [(d, j) for j in range(rows // HD)]
+        states = [pieces[d][columns(j), :] for d, j in work]
+        fk32 = [feature(k[d, :, columns(j)].astype(F32)) for d, j in work]
+        dfk = [dot_nt(v[d, :, columns(j)], state) for (d, j), state in zip(work, states)]
+        gv = [dot_nn(f.astype(BF16), state) for f, state in zip(fk32, states)]
+        for f, whole, (d, j) in zip(fk32, dfk, work):
+            row = rz_ref[pl.ds(owners[d] * (rows // HD) + j, 1), :]
+            whole = whole + dfk_in[d, :, columns(j)] + row
+            gk_ref[:, pl.ds(ats[d] + j * HD, HD)] = (whole * jnp.minimum(f, 1.0)).astype(BF16)
+        for part, (d, j) in zip(gv, work):
+            part = part + gv_in[d, :, columns(j)]
+            gv_out_ref[:, pl.ds(ats[d] + j * HD, HD)] = part.astype(BF16)
+
+
+def key_grad(place, k, v, dfk, gv, r, pieces):
+    tokens, width = k.shape
+    group, rows = len(pieces), pieces[0].shape[0]
+    whole, away = pl.BlockSpec(memory_space=pltpu.VMEM), pl.BlockSpec(memory_space=pl.ANY)
     return pl.pallas_call(
         key_grad_kernel,
-        in_specs=[pl.BlockSpec(memory_space=pltpu.SMEM)]
-        + [pl.BlockSpec(memory_space=pltpu.VMEM)] * (len(arrays) + len(pieces)),
-        out_specs=[pl.BlockSpec(memory_space=pltpu.VMEM)] * 2,
+        in_specs=[pl.BlockSpec(memory_space=pltpu.SMEM)] + [away] * 4 + [whole] * (1 + group),
+        out_specs=[whole] * 2,
         out_shape=[jax.ShapeDtypeStruct((tokens, width), BF16)] * 2,
-    )(place, *arrays, *pieces)
+        scratch_shapes=[pltpu.VMEM((group, tokens, rows), x.dtype) for x in (k, v, dfk, gv)]
+        + [pltpu.SemaphoreType.DMA((4, group))],
+    )(place, k, v, dfk, gv, r, *pieces)
 
 
 def head_call(kernel, step, kinds_in, kinds_out, arrays, tokens, heads, group):
@@ -179,13 +196,6 @@
     )(*arrays)
 
 
-def z_total_kernel(x_ref, tot_ref):
-    tot = x_ref[0].astype(F32)
-    for z in range(1, x_ref.shape[0]):
-        tot = tot + x_ref[z].astype(F32)
-    tot_ref[...] = tot
-
-
 def z_running_kernel(forward, x_ref, base_ref, out_ref):
     n = x_ref.shape[0]
     acc = base_ref[...]
@@ -197,14 +207,7 @@
 
 
 def z_total(x):
-    n, rows, lanes = x.shape
-    return pl.pallas_call(
-        z_total_kernel,
-        grid=(1,),
-        in_specs=[pl.BlockSpec((n, rows, lanes), lambda i: (0, i, 0))],
-        out_specs=pl.BlockSpec((rows, lanes), lambda i: (i, 0)),
-        out_shape=jax.ShapeDtypeStruct((rows, lanes), F32),
-    )(x)
+    return jnp.sum(x.astype(F32), axis=0)
 
 
 def z_spread_kernel(place_ref, x_ref, base_ref, *refs):
@@ -341,9 +344,7 @@
         pieces[d] = lax.ppermute(spread[d], "head", pairs)
     r = ctx_running(jnp.sum(sums, axis=0), ctx, False, F32, False)
     r = r + jnp.sum(jnp.where(ranks > place, sums, 0.0), axis=0)
-    grad_keys, grad_values = key_grad(
-        where, (keys, values, dfk, gv, r), pieces, tokens, width
-    )
+    grad_keys, grad_values = key_grad(where, keys, values, dfk, gv, r, pieces)
     return grad_queries, grad_keys, grad_values
 
 

time: 197 us -> 194 us (0.985)
  the two profiles are of different devices: /device:TPU:2 before, /device:TPU:1 now
where the time goes in v4:
time: 194 us; the launch traced here: 191 us
  starting transfers between devices  82.4 us (42%)
  waiting for transfers between devices  75.6 us (39%)
  Pallas kernels  26.7 us (14%)
  other arithmetic  3.55 us (2%)
    ppermute x24, starting transfers between devices, hop(): return lax.ppermute(value, 'ctx', pairs)  37.5 us
    ppermute x7, waiting for transfers between devices, shards(): pieces[d] = lax.ppermute(spread[d], 'head', pairs)  18.8 us
    all_to_all x1, waiting for transfers between devices, from_owners(): return lax.all_to_all(x, 'head', 0, 0, tiled=True).reshape(heads, HD, HD)  16.7 us
    pallas_call x3, Pallas kernels, head_call(): pl.pallas_call(functools.partial(kernel, step), grid=(heads // step,), in...  15.7 us
    all_to_all x2, waiting for transfers between devices, z_gather(): return lax.all_to_all(copies, 'head', 0, 0, tiled=True)  15.1 us
    ppermute x24, waiting for transfers between devices, hop(): return lax.ppermute(value, 'ctx', pairs)  13.8 us
    all_to_all x2, starting transfers between devices, z_gather(): return lax.all_to_all(copies, 'head', 0, 0, tiled=True)  12.4 us
    ppermute x7, starting transfers between devices, shards(): pieces[d] = lax.ppermute(spread[d], 'head', pairs)  10.5 us
  transfers between devices with their start and end apart: 42, of which 24 were waited for; matrix products, arithmetic and copies ran while one was open for 2% of the time, Pallas kernels for 9%

profile of v4, /device:TPU:1, one launch (start us, length us, event | category | flops | bytes accessed | tf_op | source)
XLA Modules:
  0.0 191.0 jit_solution(1050196494403744279)
XLA Ops:
  0.6 3.2 %shard_map.67 = (bf16[32,128,128]{2,1,0:T(8,128)(2,1)}, f32[8,32,128]{2,1,0:T(8,128)}) custom-call(bf16[128,4096]{1,0:T(8,128)(2,1)} %k_hbm.1, bf16[128,4096]{1,0:T(8,128)(2,1)} %v_hbm.1), custom_call_target="tpu_custom_call" | custom-call | tf_op jit(solution)/shard_map/pallas_call | solution.py:189
  3.9 9.0 %all-to-all-start = ((f32[8,32,128]{2,1,0:T(8,128)}), f32[8,32,128]{2,1,0:T(8,128)S(1)}, u32[]{:S(2)}, u32[]{:S(2)}) async-start(f32[8,32,128]{2,1,0:T(8,128)} %get-tuple-element.27), calls=%async_computation | async-start | bytes 262144 | tf_op jit(solution)/shard_map/all_to_all | solution.py:301
  12.9 7.7 %all-to-all-done = f32[8,32,128]{2,1,0:T(8,128)S(1)} async-done(((f32[8,32,128]{2,1,0:T(8,128)}), f32[8,32,128]{2,1,0:T(8,128)S(1)}, u32[]{:S(2)}, u32[]{:S(2)}) %all-to-all-start) | async-done | bytes 131104 | tf_op jit(solution)/shard_map/all_to_all | solution.py:301
  20.7 3.6 %all-to-all-start.1 = ((bf16[8,512,128]{2,1,0:T(8,128)(2,1)}), bf16[8,512,128]{2,1,0:T(8,128)(2,1)S(1)}, u32[]{:S(2)}, u32[]{:S(2)}) async-start(bf16[8,512,128]{2,1,0:T(8,128)(2,1)} %bitcast.6), calls=%async_computation.1 | async-start | bytes 2097152 | tf_op jit(solution)/shard_map/all_to_all | solution.py:312
  24.3 2.4 %collective-permute-start = (f32[32,128]{1,0:T(8,128)S(1)}, f32[32,128]{1,0:T(8,128)S(1)}, u32[]{:S(2)}, u32[]{:S(2)}) collective-permute-start(f32[32,128]{1,0:T(8,128)S(1)} %get-tuple-element.29), channel_id=1, source_target_pairs={{0,8},{8,0},{16,24},{24,16},{32,40},{40,32},{48,56},{56,48},{64,72... | collective-permute-start | bytes 49160 | tf_op jit(solution)/shard_map/ppermute | solution.py:278
  26.7 0.8 collective-permute-done
  27.5 2.7 %collective-permute-start.3 = (f32[32,128]{1,0:T(8,128)S(1)}, f32[32,128]{1,0:T(8,128)S(1)}, u32[]{:S(2)}, u32[]{:S(2)}) collective-permute-start(f32[32,128]{1,0:T(8,128)S(1)} %add.142), channel_id=1, source_target_pairs={{0,48},{8,56},{16,0},{24,8},{32,16},{40,24},{48,32},{56,40},{64,11... | collective-permute-start | bytes 49160 | tf_op jit(solution)/shard_map/ppermute | solution.py:272
  30.6 0.7 collective-permute-start.1
  31.3 3.3 %collective-permute-done.2 = f32[32,128]{1,0:T(8,128)S(1)} collective-permute-done((f32[32,128]{1,0:T(8,128)S(1)}, f32[32,128]{1,0:T(8,128)S(1)}, u32[]{:S(2)}, u32[]{:S(2)}) %collective-permute-start.2) | collective-permute-done | bytes 16416 | tf_op jit(solution)/shard_map/ppermute | solution.py:272
  34.8 4.4 %collective-permute-start.6 = (f32[32,128]{1,0:T(8,128)S(1)}, f32[32,128]{1,0:T(8,128)S(1)}, u32[]{:S(2)}, u32[]{:S(2)}) collective-permute-start(f32[32,128]{1,0:T(8,128)S(1)} %add_add_fusion.3), channel_id=1, source_target_pairs={{0,192},{8,200},{16,208},{24,216},{32,224},{40,232},{48,240},{56,2... | collective-permute-start | bytes 49160 | tf_op jit(solution)/shard_map/ppermute | solution.py:272
  39.2 1.3 collective-permute-start.5
  40.5 2.5 %collective-permute-start.4 = (f32[32,128]{1,0:T(8,128)S(1)}, f32[32,128]{1,0:T(8,128)S(1)}, u32[]{:S(2)}, u32[]{:S(2)}) collective-permute-start(f32[32,128]{1,0:T(8,128)S(1)} %add_add_fusion.3), channel_id=1, source_target_pairs={{0,64},{8,72},{16,80},{24,88},{32,96},{40,104},{48,112},{56,120},{... | collective-permute-start | bytes 49160 | tf_op jit(solution)/shard_map/ppermute | solution.py:272
  43.0 0.8 collective-permute-done.4
  44.4 4.5 %shard_map.68 = bf16[32,128,128]{2,1,0:T(8,128)(2,1)} custom-call(bf16[128,4096]{1,0:T(8,128)(2,1)} %q_ref.3, bf16[128,4096]{1,0:T(8,128)(2,1)} %k_hbm.1, bf16[128,4096]{1,0:T(8,128)(2,1)} %g_ref.3, f32[32,128]{1,0:T(8,128)} %add_add_fusion.2.z_ref), custom_call_target="tpu_custom_call" | custom-call | tf_op jit(solution)/shard_map/pallas_call | solution.py:189
  49.0 4.3 %all-to-all-done.1.x_ref = bf16[8,512,128]{2,1,0:T(8,128)(2,1)S(1)} async-done(((bf16[8,512,128]{2,1,0:T(8,128)(2,1)}), bf16[8,512,128]{2,1,0:T(8,128)(2,1)S(1)}, u32[]{:S(2)}, u32[]{:S(2)}) %all-to-all-start.1) | async-done | bytes 1048608 | tf_op jit(solution)/shard_map/all_to_all | solution.py:312
  53.3 3.6 %all-to-all-start.2 = ((bf16[8,512,128]{2,1,0:T(8,128)(2,1)}), bf16[8,512,128]{2,1,0:T(8,128)(2,1)S(1)}, u32[]{:S(2)}, u32[]{:S(2)}) async-start(bf16[8,512,128]{2,1,0:T(8,128)(2,1)} %bitcast.5), calls=%async_computation.2 | async-start | bytes 2097152 | tf_op jit(solution)/shard_map/all_to_all | solution.py:312
  57.0 2.0 %collective-permute-start.7 = (f32[512,128]{1,0:T(8,128)S(1)}, f32[512,128]{1,0:T(8,128)S(1)}, u32[]{:S(2)}, u32[]{:S(2)}) collective-permute-start(f32[512,128]{1,0:T(8,128)S(1)} %convert_reduce_fusion.1), channel_id=1, source_target_pairs={{0,8},{8,0},{16,24},{24,16},{32,40},{40,32},{48,56},{56,48},{64,72... | collective-permute-start | bytes 786440 | tf_op jit(solution)/shard_map/ppermute | solution.py:278
  59.0 1.2 collective-permute-done.7
  60.3 1.5 collective-permute-start.10
  62.1 0.7 collective-permute-start.8
  62.8 1.0 collective-permute-done.10
  63.8 2.9 %collective-permute-done.9 = bf16[256,128]{1,0:T(8,128)(2,1)S(1)} collective-permute-done((bf16[256,128]{1,0:T(8,128)(2,1)S(1)}, bf16[256,128]{1,0:T(8,128)(2,1)S(1)}, u32[]{:S(2)}, u32[]{:S(2)}) %collective-permute-start.9) | collective-permute-done | bytes 65568 | tf_op jit(solution)/shard_map/ppermute | solution.py:272
  66.6 1.5 collective-permute-done.8
  68.2 4.4 %collective-permute-start.13 = (bf16[256,128]{1,0:T(8,128)(2,1)S(1)}, bf16[256,128]{1,0:T(8,128)(2,1)S(1)}, u32[]{:S(2)}, u32[]{:S(2)}) collective-permute-start(bf16[256,128]{1,0:T(8,128)(2,1)S(1)} %fusion.3), channel_id=1, source_target_pairs={{0,192},{8,200},{16,208},{24,216},{32,224},{40,232},{48,240},{56,2... | collective-permute-start | bytes 196616 | tf_op jit(solution)/shard_map/ppermute | solution.py:272
  72.6 1.3 collective-permute-start.12
  73.9 2.5 %collective-permute-start.11 = (bf16[256,128]{1,0:T(8,128)(2,1)S(1)}, bf16[256,128]{1,0:T(8,128)(2,1)S(1)}, u32[]{:S(2)}, u32[]{:S(2)}) collective-permute-start(bf16[256,128]{1,0:T(8,128)(2,1)S(1)} %fusion.3), channel_id=1, source_target_pairs={{0,64},{8,72},{16,80},{24,88},{32,96},{40,104},{48,112},{56,120},{... | collective-permute-start | bytes 196616 | tf_op jit(solution)/shard_map/ppermute | solution.py:272
  76.4 1.3 collective-permute-done.11
  77.8 2.2 %collective-permute-start.14 = (f32[256,128]{1,0:T(8,128)S(1)}, f32[256,128]{1,0:T(8,128)S(1)}, u32[]{:S(2)}, u32[]{:S(2)}) collective-permute-start(f32[256,128]{1,0:T(8,128)S(1)} %fusion.2), channel_id=1, source_target_pairs={{0,8},{8,0},{16,24},{24,16},{32,40},{40,32},{48,56},{56,48},{64,72... | collective-permute-start | bytes 393224 | tf_op jit(solution)/shard_map/ppermute | solution.py:278
  80.0 1.0 collective-permute-done.14
  81.0 0.8 maximum_add_fusion.base_ref
  81.7 2.4 %shard_map.69 = bf16[8,512,128]{2,1,0:T(8,128)(2,1)} custom-call(bf16[8,512,128]{2,1,0:T(8,128)(2,1)} %copy-done.1, f32[512,128]{1,0:T(8,128)} %maximum_add_fusion.base_ref), custom_call_target="tpu_custom_call" | custom-call | tf_op jit(solution)/shard_map/pallas_call | solution.py:223
  84.1 1.8 all-to-all-done.2.x_ref
  86.0 5.0 %all-to-all-start.3 = ((bf16[8,512,128]{2,1,0:T(8,128)(2,1)}), bf16[8,512,128]{2,1,0:T(8,128)(2,1)S(1)}, u32[]{:S(2)}, u32[]{:S(2)}) async-start(bf16[8,512,128]{2,1,0:T(8,128)(2,1)} %shard_map.69), calls=%async_computation.3 | async-start | bytes 2097152 | tf_op jit(solution)/shard_map/all_to_all | solution.py:315
  91.1 0.7 collective-permute-start.22
  91.9 1.2 collective-permute-done.22
  93.2 2.4 %collective-permute-start.24 = (bf16[256,128]{1,0:T(8,128)(2,1)S(1)}, bf16[256,128]{1,0:T(8,128)(2,1)S(1)}, u32[]{:S(2)}, u32[]{:S(2)}) collective-permute-start(bf16[256,128]{1,0:T(8,128)(2,1)S(1)} %fusion.9), channel_id=1, source_target_pairs={{0,32},{8,40},{16,48},{24,56},{32,0},{40,8},{48,16},{56,24},{64,96... | collective-permute-start | bytes 196616 | tf_op jit(solution)/shard_map/ppermute | solution.py:272
  95.5 1.1 collective-permute-start.23
  96.6 1.9 collective-permute-done.25
  98.5 0.8 collective-permute-done.23
  99.4 1.5 collective-permute-start.28
  100.9 1.3 collective-permute-start.27
  102.2 1.3 collective-permute-start.26
  103.5 16.7 %all-to-all-done.3 = bf16[8,512,128]{2,1,0:T(8,128)(2,1)S(1)} async-done(((bf16[8,512,128]{2,1,0:T(8,128)(2,1)}), bf16[8,512,128]{2,1,0:T(8,128)(2,1)S(1)}, u32[]{:S(2)}, u32[]{:S(2)}) %all-to-all-start.3) | async-done | bytes 1048608 | tf_op jit(solution)/shard_map/all_to_all | solution.py:315
  120.2 1.0 copy-done.2
  121.2 8.0 %shard_map.70 = (bf16[128,4096]{1,0:T(8,128)(2,1)}, f32[128,4096]{1,0:T(8,128)}, f32[128,4096]{1,0:T(8,128)}, f32[8,32,128]{2,1,0:T(8,128)}) custom-call(bf16[128,4096]{1,0:T(8,128)(2,1)} %q_ref.3, bf16[128,4096]{1,0:T(8,128)(2,1)} %k_hbm.1, bf16[128,4096]{1,0:T(8,128)(2,1)} %v_hbm.1, bf16[128,4096]{1,0:T(8,128)(2,1)} %g_ref.3, ...), custom_call_target="tpu_custom_call" | custom-call | tf_op jit(solution)/shard_map/pallas_call | solution.py:189
  129.1 3.4 %all-to-all-start.4 = ((f32[8,32,128]{2,1,0:T(8,128)}), f32[8,32,128]{2,1,0:T(8,128)S(1)}, u32[]{:S(2)}, u32[]{:S(2)}) async-start(f32[8,32,128]{2,1,0:T(8,128)} %get-tuple-element.37), calls=%async_computation.4 | async-start | bytes 262144 | tf_op jit(solution)/shard_map/all_to_all | solution.py:301
  133.2 7.3 %all-to-all-done.4 = f32[8,32,128]{2,1,0:T(8,128)S(1)} async-done(((f32[8,32,128]{2,1,0:T(8,128)}), f32[8,32,128]{2,1,0:T(8,128)S(1)}, u32[]{:S(2)}, u32[]{:S(2)}) %all-to-all-start.4) | async-done | bytes 131104 | tf_op jit(solution)/shard_map/all_to_all | solution.py:301
  140.6 2.0 %collective-permute-start.15 = (f32[32,128]{1,0:T(8,128)S(1)}, f32[32,128]{1,0:T(8,128)S(1)}, u32[]{:S(2)}, u32[]{:S(2)}) collective-permute-start(f32[32,128]{1,0:T(8,128)S(1)} %get-tuple-element.49), channel_id=1, source_target_pairs={{0,8},{8,0},{16,24},{24,16},{32,40},{40,32},{48,56},{56,48},{64,72... | collective-permute-start | bytes 49160 | tf_op jit(solution)/shard_map/ppermute | solution.py:278
  142.6 0.8 collective-permute-done.15
  143.5 2.4 %collective-permute-start.17 = (f32[32,128]{1,0:T(8,128)S(1)}, f32[32,128]{1,0:T(8,128)S(1)}, u32[]{:S(2)}, u32[]{:S(2)}) collective-permute-start(f32[32,128]{1,0:T(8,128)S(1)} %add.163), channel_id=1, source_target_pairs={{0,32},{8,40},{16,48},{24,56},{32,0},{40,8},{48,16},{56,24},{64,96... | collective-permute-start | bytes 49160 | tf_op jit(solution)/shard_map/ppermute | solution.py:272
  145.9 1.1 collective-permute-start.16
  147.0 0.7 maximum_add_fusion.1.base_ref
  147.7 2.5 %shard_map.71 = (bf16[512,128]{1,0:T(8,128)(2,1)}, bf16[512,128]{1,0:T(8,128)(2,1)}, bf16[512,128]{1,0:T(8,128)(2,1)}, bf16[512,128]{1,0:T(8,128)(2,1)}, bf16[51...) custom-call(s32[1]{0:T(128)} %bitcast.3.place_ref, ...), custom_call_target="tpu_custom_call" | custom-call | tf_op jit(solution)/shard_map/pallas_call | solution.py:234
  150.6 1.3 collective-permute-start.21
  151.9 1.3 collective-permute-start.20
  153.2 1.3 collective-permute-start.19
  154.5 2.7 %collective-permute-done.30.refs_1_ = bf16[512,128]{1,0:T(8,128)(2,1)S(1)} collective-permute-done((bf16[512,128]{1,0:T(8,128)(2,1)}, bf16[512,128]{1,0:T(8,128)(2,1)S(1)}, u32[]{:S(2)}, u32[]{:S(2)}) %collective-permute-start.30) | collective-permute-done | bytes 131104 | tf_op jit(solution)/shard_map/ppermute | solution.py:344
  157.2 2.7 %collective-permute-start.33 = (bf16[512,128]{1,0:T(8,128)(2,1)}, bf16[512,128]{1,0:T(8,128)(2,1)S(1)}, u32[]{:S(2)}, u32[]{:S(2)}) collective-permute-start(bf16[512,128]{1,0:T(8,128)(2,1)} %get-tuple-element.43), channel_id=1, source_target_pairs={{0,4},{1,5},{2,6},{3,7},{4,0},{5,1},{6,2},{7,3},{8,12},{9,13},{10,... | collective-permute-start | bytes 393224 | tf_op jit(solution)/shard_map/ppermute | solution.py:344
  159.9 7.0 %collective-permute-start.34 = (bf16[512,128]{1,0:T(8,128)(2,1)}, bf16[512,128]{1,0:T(8,128)(2,1)S(1)}, u32[]{:S(2)}, u32[]{:S(2)}) collective-permute-start(bf16[512,128]{1,0:T(8,128)(2,1)} %get-tuple-element.44), channel_id=1, source_target_pairs={{0,5},{1,6},{2,7},{3,0},{4,1},{5,2},{6,3},{7,4},{8,13},{9,14},{10,... | collective-permute-start | bytes 393224 | tf_op jit(solution)/shard_map/ppermute | solution.py:344
  167.3 0.6 add_add_fusion.rz_ref
  167.9 4.0 %collective-permute-done.32.refs_3_ = bf16[512,128]{1,0:T(8,128)(2,1)S(1)} collective-permute-done((bf16[512,128]{1,0:T(8,128)(2,1)}, bf16[512,128]{1,0:T(8,128)(2,1)S(1)}, u32[]{:S(2)}, u32[]{:S(2)}) %collective-permute-start.32) | collective-permute-done | bytes 131104 | tf_op jit(solution)/shard_map/ppermute | solution.py:344
  171.8 2.2 %collective-permute-done.34.refs_5_ = bf16[512,128]{1,0:T(8,128)(2,1)S(1)} collective-permute-done((bf16[512,128]{1,0:T(8,128)(2,1)}, bf16[512,128]{1,0:T(8,128)(2,1)S(1)}, u32[]{:S(2)}, u32[]{:S(2)}) %collective-permute-start.34) | collective-permute-done | bytes 131104 | tf_op jit(solution)/shard_map/ppermute | solution.py:344
  174.0 9.9 %collective-permute-done.35.refs_6_ = bf16[512,128]{1,0:T(8,128)(2,1)S(1)} collective-permute-done((bf16[512,128]{1,0:T(8,128)(2,1)}, bf16[512,128]{1,0:T(8,128)(2,1)S(1)}, u32[]{:S(2)}, u32[]{:S(2)}) %collective-permute-start.35) | collective-permute-done | bytes 131104 | tf_op jit(solution)/shard_map/ppermute | solution.py:344
  184.7 6.1 %shard_map.72 = (bf16[128,4096]{1,0:T(8,128)(2,1)}, bf16[128,4096]{1,0:T(8,128)(2,1)}) custom-call(s32[1]{0:T(128)} %bitcast.3.place_ref, bf16[128,4096]{1,0:T(8,128)(2,1)} %k_hbm.1, bf16[128,4096]{1,0:T(8,128)(2,1)} %v_hbm.1, f32[128,4096]{1,0:T(8,128)} %get-tuple-element.35.dfk_hbm, f32[128,4096]{1,0:T(8,128)} %get-tuple-element.36.gv_hbm, ...), custom_call_target="tpu_custom_call" | custom-call | tf_op jit(solution)/shard_map/pallas_call | solution.py:166
  (70 shorter events, 4.6 us)
Async XLA Ops:
  3.9 16.8 %all-to-all-start = ((f32[8,32,128]{2,1,0:T(8,128)}), f32[8,32,128]{2,1,0:T(8,128)S(1)}, u32[]{:S(2)}, u32[]{:S(2)}) async-start(f32[8,32,128]{2,1,0:T(8,128)} %get-tuple-element.27), calls=%async_computation | async-start | bytes 262144 | tf_op jit(solution)/shard_map/all_to_all | solution.py:301
  20.7 32.6 %all-to-all-start.1 = ((bf16[8,512,128]{2,1,0:T(8,128)(2,1)}), bf16[8,512,128]{2,1,0:T(8,128)(2,1)S(1)}, u32[]{:S(2)}, u32[]{:S(2)}) async-start(bf16[8,512,128]{2,1,0:T(8,128)(2,1)} %bitcast.6), calls=%async_computation.1 | async-start | bytes 2097152 | tf_op jit(solution)/shard_map/all_to_all | solution.py:312
  24.3 3.2 %collective-permute-start = (f32[32,128]{1,0:T(8,128)S(1)}, f32[32,128]{1,0:T(8,128)S(1)}, u32[]{:S(2)}, u32[]{:S(2)}) collective-permute-start(f32[32,128]{1,0:T(8,128)S(1)} %get-tuple-element.29), channel_id=1, source_target_pairs={{0,8},{8,0},{16,24},{24,16},{32,40},{40,32},{48,56},{56,48},{64,72... | collective-permute-start | bytes 49160 | tf_op jit(solution)/shard_map/ppermute | solution.py:278
  27.5 3.8 %collective-permute-start.3 = (f32[32,128]{1,0:T(8,128)S(1)}, f32[32,128]{1,0:T(8,128)S(1)}, u32[]{:S(2)}, u32[]{:S(2)}) collective-permute-start(f32[32,128]{1,0:T(8,128)S(1)} %add.142), channel_id=1, source_target_pairs={{0,48},{8,56},{16,0},{24,8},{32,16},{40,24},{48,32},{56,40},{64,11... | collective-permute-start | bytes 49160 | tf_op jit(solution)/shard_map/ppermute | solution.py:272
  30.2 4.4 %collective-permute-start.2 = (f32[32,128]{1,0:T(8,128)S(1)}, f32[32,128]{1,0:T(8,128)S(1)}, u32[]{:S(2)}, u32[]{:S(2)}) collective-permute-start(f32[32,128]{1,0:T(8,128)S(1)} %add.142), channel_id=1, source_target_pairs={{0,32},{8,40},{16,48},{24,56},{32,0},{40,8},{48,16},{56,24},{64,96... | collective-permute-start | bytes 49160 | tf_op jit(solution)/shard_map/ppermute | solution.py:272
  30.6 4.2 %collective-permute-start.1 = (f32[32,128]{1,0:T(8,128)S(1)}, f32[32,128]{1,0:T(8,128)S(1)}, u32[]{:S(2)}, u32[]{:S(2)}) collective-permute-start(f32[32,128]{1,0:T(8,128)S(1)} %add.142), channel_id=1, source_target_pairs={{0,16},{8,24},{16,32},{24,40},{32,48},{40,56},{48,0},{56,8},{64,80... | collective-permute-start | bytes 49160 | tf_op jit(solution)/shard_map/ppermute | solution.py:272
  34.8 8.2 %collective-permute-start.6 = (f32[32,128]{1,0:T(8,128)S(1)}, f32[32,128]{1,0:T(8,128)S(1)}, u32[]{:S(2)}, u32[]{:S(2)}) collective-permute-start(f32[32,128]{1,0:T(8,128)S(1)} %add_add_fusion.3), channel_id=1, source_target_pairs={{0,192},{8,200},{16,208},{24,216},{32,224},{40,232},{48,240},{56,2... | collective-permute-start | bytes 49160 | tf_op jit(solution)/shard_map/ppermute | solution.py:272
  39.2 3.8 %collective-permute-start.5 = (f32[32,128]{1,0:T(8,128)S(1)}, f32[32,128]{1,0:T(8,128)S(1)}, u32[]{:S(2)}, u32[]{:S(2)}) collective-permute-start(f32[32,128]{1,0:T(8,128)S(1)} %add_add_fusion.3), channel_id=1, source_target_pairs={{0,128},{8,136},{16,144},{24,152},{32,160},{40,168},{48,176},{56,1... | collective-permute-start | bytes 49160 | tf_op jit(solution)/shard_map/ppermute | solution.py:272
  40.5 3.3 %collective-permute-start.4 = (f32[32,128]{1,0:T(8,128)S(1)}, f32[32,128]{1,0:T(8,128)S(1)}, u32[]{:S(2)}, u32[]{:S(2)}) collective-permute-start(f32[32,128]{1,0:T(8,128)S(1)} %add_add_fusion.3), channel_id=1, source_target_pairs={{0,64},{8,72},{16,80},{24,88},{32,96},{40,104},{48,112},{56,120},{... | collective-permute-start | bytes 49160 | tf_op jit(solution)/shard_map/ppermute | solution.py:272
  53.3 6.9 %copy-start.1 = (bf16[8,512,128]{2,1,0:T(8,128)(2,1)}, bf16[8,512,128]{2,1,0:T(8,128)(2,1)S(1)}, u32[]{:S(2)}) copy-start(bf16[8,512,128]{2,1,0:T(8,128)(2,1)S(1)} %all-to-all-done.1.x_ref) | copy-start | bytes 3145732
  53.3 32.7 %all-to-all-start.2 = ((bf16[8,512,128]{2,1,0:T(8,128)(2,1)}), bf16[8,512,128]{2,1,0:T(8,128)(2,1)S(1)}, u32[]{:S(2)}, u32[]{:S(2)}) async-start(bf16[8,512,128]{2,1,0:T(8,128)(2,1)} %bitcast.5), calls=%async_computation.2 | async-start | bytes 2097152 | tf_op jit(solution)/shard_map/all_to_all | solution.py:312
  57.0 3.2 %collective-permute-start.7 = (f32[512,128]{1,0:T(8,128)S(1)}, f32[512,128]{1,0:T(8,128)S(1)}, u32[]{:S(2)}, u32[]{:S(2)}) collective-permute-start(f32[512,128]{1,0:T(8,128)S(1)} %convert_reduce_fusion.1), channel_id=1, source_target_pairs={{0,8},{8,0},{16,24},{24,16},{32,40},{40,32},{48,56},{56,48},{64,72... | collective-permute-start | bytes 786440 | tf_op jit(solution)/shard_map/ppermute | solution.py:278
  60.3 3.5 %collective-permute-start.10 = (bf16[256,128]{1,0:T(8,128)(2,1)S(1)}, bf16[256,128]{1,0:T(8,128)(2,1)S(1)}, u32[]{:S(2)}, u32[]{:S(2)}) collective-permute-start(bf16[256,128]{1,0:T(8,128)(2,1)S(1)} %fusion.8), channel_id=1, source_target_pairs={{0,48},{8,56},{16,0},{24,8},{32,16},{40,24},{48,32},{56,40},{64,11... | collective-permute-start | bytes 196616 | tf_op jit(solution)/shard_map/ppermute | solution.py:272
  61.7 4.9 %collective-permute-start.9 = (bf16[256,128]{1,0:T(8,128)(2,1)S(1)}, bf16[256,128]{1,0:T(8,128)(2,1)S(1)}, u32[]{:S(2)}, u32[]{:S(2)}) collective-permute-start(bf16[256,128]{1,0:T(8,128)(2,1)S(1)} %fusion.8), channel_id=1, source_target_pairs={{0,32},{8,40},{16,48},{24,56},{32,0},{40,8},{48,16},{56,24},{64,96... | collective-permute-start | bytes 196616 | tf_op jit(solution)/shard_map/ppermute | solution.py:272
  62.1 6.1 %collective-permute-start.8 = (bf16[256,128]{1,0:T(8,128)(2,1)S(1)}, bf16[256,128]{1,0:T(8,128)(2,1)S(1)}, u32[]{:S(2)}, u32[]{:S(2)}) collective-permute-start(bf16[256,128]{1,0:T(8,128)(2,1)S(1)} %fusion.8), channel_id=1, source_target_pairs={{0,16},{8,24},{16,32},{24,40},{32,48},{40,56},{48,0},{56,8},{64,80... | collective-permute-start | bytes 196616 | tf_op jit(solution)/shard_map/ppermute | solution.py:272
  68.2 8.2 %collective-permute-start.13 = (bf16[256,128]{1,0:T(8,128)(2,1)S(1)}, bf16[256,128]{1,0:T(8,128)(2,1)S(1)}, u32[]{:S(2)}, u32[]{:S(2)}) collective-permute-start(bf16[256,128]{1,0:T(8,128)(2,1)S(1)} %fusion.3), channel_id=1, source_target_pairs={{0,192},{8,200},{16,208},{24,216},{32,224},{40,232},{48,240},{56,2... | collective-permute-start | bytes 196616 | tf_op jit(solution)/shard_map/ppermute | solution.py:272
  72.6 3.8 %collective-permute-start.12 = (bf16[256,128]{1,0:T(8,128)(2,1)S(1)}, bf16[256,128]{1,0:T(8,128)(2,1)S(1)}, u32[]{:S(2)}, u32[]{:S(2)}) collective-permute-start(bf16[256,128]{1,0:T(8,128)(2,1)S(1)} %fusion.3), channel_id=1, source_target_pairs={{0,128},{8,136},{16,144},{24,152},{32,160},{40,168},{48,176},{56,1... | collective-permute-start | bytes 196616 | tf_op jit(solution)/shard_map/ppermute | solution.py:272
  73.9 3.8 %collective-permute-start.11 = (bf16[256,128]{1,0:T(8,128)(2,1)S(1)}, bf16[256,128]{1,0:T(8,128)(2,1)S(1)}, u32[]{:S(2)}, u32[]{:S(2)}) collective-permute-start(bf16[256,128]{1,0:T(8,128)(2,1)S(1)} %fusion.3), channel_id=1, source_target_pairs={{0,64},{8,72},{16,80},{24,88},{32,96},{40,104},{48,112},{56,120},{... | collective-permute-start | bytes 196616 | tf_op jit(solution)/shard_map/ppermute | solution.py:272
  77.8 3.2 %collective-permute-start.14 = (f32[256,128]{1,0:T(8,128)S(1)}, f32[256,128]{1,0:T(8,128)S(1)}, u32[]{:S(2)}, u32[]{:S(2)}) collective-permute-start(f32[256,128]{1,0:T(8,128)S(1)} %fusion.2), channel_id=1, source_target_pairs={{0,8},{8,0},{16,24},{24,16},{32,40},{40,32},{48,56},{56,48},{64,72... | collective-permute-start | bytes 393224 | tf_op jit(solution)/shard_map/ppermute | solution.py:278
  86.0 7.1 %copy-start = (bf16[8,512,128]{2,1,0:T(8,128)(2,1)}, bf16[8,512,128]{2,1,0:T(8,128)(2,1)S(1)}, u32[]{:S(2)}) copy-start(bf16[8,512,128]{2,1,0:T(8,128)(2,1)S(1)} %all-to-all-done.2.x_ref) | copy-start | bytes 3145732
  86.0 34.2 %all-to-all-start.3 = ((bf16[8,512,128]{2,1,0:T(8,128)(2,1)}), bf16[8,512,128]{2,1,0:T(8,128)(2,1)S(1)}, u32[]{:S(2)}, u32[]{:S(2)}) async-start(bf16[8,512,128]{2,1,0:T(8,128)(2,1)} %shard_map.69), calls=%async_computation.3 | async-start | bytes 2097152 | tf_op jit(solution)/shard_map/all_to_all | solution.py:315
  91.1 1.9 collective-permute-start.22
  93.1 5.4 %collective-permute-start.25 = (bf16[256,128]{1,0:T(8,128)(2,1)S(1)}, bf16[256,128]{1,0:T(8,128)(2,1)S(1)}, u32[]{:S(2)}, u32[]{:S(2)}) collective-permute-start(bf16[256,128]{1,0:T(8,128)(2,1)S(1)} %fusion.9), channel_id=1, source_target_pairs={{0,16},{8,24},{16,32},{24,40},{32,48},{40,56},{48,0},{56,8},{64,80... | collective-permute-start | bytes 196616 | tf_op jit(solution)/shard_map/ppermute | solution.py:272
  93.2 5.3 %collective-permute-start.24 = (bf16[256,128]{1,0:T(8,128)(2,1)S(1)}, bf16[256,128]{1,0:T(8,128)(2,1)S(1)}, u32[]{:S(2)}, u32[]{:S(2)}) collective-permute-start(bf16[256,128]{1,0:T(8,128)(2,1)S(1)} %fusion.9), channel_id=1, source_target_pairs={{0,32},{8,40},{16,48},{24,56},{32,0},{40,8},{48,16},{56,24},{64,96... | collective-permute-start | bytes 196616 | tf_op jit(solution)/shard_map/ppermute | solution.py:272
  95.5 3.8 %collective-permute-start.23 = (bf16[256,128]{1,0:T(8,128)(2,1)S(1)}, bf16[256,128]{1,0:T(8,128)(2,1)S(1)}, u32[]{:S(2)}, u32[]{:S(2)}) collective-permute-start(bf16[256,128]{1,0:T(8,128)(2,1)S(1)} %fusion.9), channel_id=1, source_target_pairs={{0,48},{8,56},{16,0},{24,8},{32,16},{40,24},{48,32},{56,40},{64,11... | collective-permute-start | bytes 196616 | tf_op jit(solution)/shard_map/ppermute | solution.py:272
  99.4 33.1 %collective-permute-start.28 = (bf16[256,128]{1,0:T(8,128)(2,1)S(1)}, bf16[256,128]{1,0:T(8,128)(2,1)S(1)}, u32[]{:S(2)}, u32[]{:S(2)}) collective-permute-start(bf16[256,128]{1,0:T(8,128)(2,1)S(1)} %fusion.7), channel_id=1, source_target_pairs={{192,0},{200,8},{208,16},{216,24},{224,32},{232,40},{240,48},{248,... | collective-permute-start | bytes 196616 | tf_op jit(solution)/shard_map/ppermute | solution.py:272
  100.9 31.7 %collective-permute-start.27 = (bf16[256,128]{1,0:T(8,128)(2,1)S(1)}, bf16[256,128]{1,0:T(8,128)(2,1)S(1)}, u32[]{:S(2)}, u32[]{:S(2)}) collective-permute-start(bf16[256,128]{1,0:T(8,128)(2,1)S(1)} %fusion.7), channel_id=1, source_target_pairs={{128,0},{136,8},{144,16},{152,24},{160,32},{168,40},{176,48},{184,... | collective-permute-start | bytes 196616 | tf_op jit(solution)/shard_map/ppermute | solution.py:272
  102.2 30.4 %collective-permute-start.26 = (bf16[256,128]{1,0:T(8,128)(2,1)S(1)}, bf16[256,128]{1,0:T(8,128)(2,1)S(1)}, u32[]{:S(2)}, u32[]{:S(2)}) collective-permute-start(bf16[256,128]{1,0:T(8,128)(2,1)S(1)} %fusion.7), channel_id=1, source_target_pairs={{64,0},{72,8},{80,16},{88,24},{96,32},{104,40},{112,48},{120,56},{... | collective-permute-start | bytes 196616 | tf_op jit(solution)/shard_map/ppermute | solution.py:272
  120.2 1.0 copy-start.2
  129.1 11.4 %all-to-all-start.4 = ((f32[8,32,128]{2,1,0:T(8,128)}), f32[8,32,128]{2,1,0:T(8,128)S(1)}, u32[]{:S(2)}, u32[]{:S(2)}) async-start(f32[8,32,128]{2,1,0:T(8,128)} %get-tuple-element.37), calls=%async_computation.4 | async-start | bytes 262144 | tf_op jit(solution)/shard_map/all_to_all | solution.py:301
  132.6 10.0 %collective-permute-start.29 = (f32[256,128]{1,0:T(8,128)S(1)}, f32[256,128]{1,0:T(8,128)S(1)}, u32[]{:S(2)}, u32[]{:S(2)}) collective-permute-start(f32[256,128]{1,0:T(8,128)S(1)} %fusion.6), channel_id=1, source_target_pairs={{0,8},{8,0},{16,24},{24,16},{32,40},{40,32},{48,56},{56,48},{64,72... | collective-permute-start | bytes 393224 | tf_op jit(solution)/shard_map/ppermute | solution.py:278
  140.6 2.8 %collective-permute-start.15 = (f32[32,128]{1,0:T(8,128)S(1)}, f32[32,128]{1,0:T(8,128)S(1)}, u32[]{:S(2)}, u32[]{:S(2)}) collective-permute-start(f32[32,128]{1,0:T(8,128)S(1)} %get-tuple-element.49), channel_id=1, source_target_pairs={{0,8},{8,0},{16,24},{24,16},{32,40},{40,32},{48,56},{56,48},{64,72... | collective-permute-start | bytes 49160 | tf_op jit(solution)/shard_map/ppermute | solution.py:278
  143.5 7.1 %collective-permute-start.18 = (f32[32,128]{1,0:T(8,128)S(1)}, f32[32,128]{1,0:T(8,128)S(1)}, u32[]{:S(2)}, u32[]{:S(2)}) collective-permute-start(f32[32,128]{1,0:T(8,128)S(1)} %add.163), channel_id=1, source_target_pairs={{0,16},{8,24},{16,32},{24,40},{32,48},{40,56},{48,0},{56,8},{64,80... | collective-permute-start | bytes 49160 | tf_op jit(solution)/shard_map/ppermute | solution.py:272
  143.5 7.1 %collective-permute-start.17 = (f32[32,128]{1,0:T(8,128)S(1)}, f32[32,128]{1,0:T(8,128)S(1)}, u32[]{:S(2)}, u32[]{:S(2)}) collective-permute-start(f32[32,128]{1,0:T(8,128)S(1)} %add.163), channel_id=1, source_target_pairs={{0,32},{8,40},{16,48},{24,56},{32,0},{40,8},{48,16},{56,24},{64,96... | collective-permute-start | bytes 49160 | tf_op jit(solution)/shard_map/ppermute | solution.py:272
  145.9 4.7 %collective-permute-start.16 = (f32[32,128]{1,0:T(8,128)S(1)}, f32[32,128]{1,0:T(8,128)S(1)}, u32[]{:S(2)}, u32[]{:S(2)}) collective-permute-start(f32[32,128]{1,0:T(8,128)S(1)} %add.163), channel_id=1, source_target_pairs={{0,48},{8,56},{16,0},{24,8},{32,16},{40,24},{48,32},{56,40},{64,11... | collective-permute-start | bytes 49160 | tf_op jit(solution)/shard_map/ppermute | solution.py:272
  150.2 7.0 %collective-permute-start.30 = (bf16[512,128]{1,0:T(8,128)(2,1)}, bf16[512,128]{1,0:T(8,128)(2,1)S(1)}, u32[]{:S(2)}, u32[]{:S(2)}) collective-permute-start(bf16[512,128]{1,0:T(8,128)(2,1)} %get-tuple-element.40), channel_id=1, source_target_pairs={{0,1},{1,2},{2,3},{3,4},{4,5},{5,6},{6,7},{7,0},{8,9},{9,10},{10,1... | collective-permute-start | bytes 393224 | tf_op jit(solution)/shard_map/ppermute | solution.py:344
  150.5 6.7 %collective-permute-start.31 = (bf16[512,128]{1,0:T(8,128)(2,1)}, bf16[512,128]{1,0:T(8,128)(2,1)S(1)}, u32[]{:S(2)}, u32[]{:S(2)}) collective-permute-start(bf16[512,128]{1,0:T(8,128)(2,1)} %get-tuple-element.41), channel_id=1, source_target_pairs={{0,2},{1,3},{2,4},{3,5},{4,6},{5,7},{6,0},{7,1},{8,10},{9,11},{10,... | collective-permute-start | bytes 393224 | tf_op jit(solution)/shard_map/ppermute | solution.py:344
  150.6 9.3 %collective-permute-start.21 = (f32[32,128]{1,0:T(8,128)S(1)}, f32[32,128]{1,0:T(8,128)S(1)}, u32[]{:S(2)}, u32[]{:S(2)}) collective-permute-start(f32[32,128]{1,0:T(8,128)S(1)} %add_add_fusion.1), channel_id=1, source_target_pairs={{192,0},{200,8},{208,16},{216,24},{224,32},{232,40},{240,48},{248,... | collective-permute-start | bytes 49160 | tf_op jit(solution)/shard_map/ppermute | solution.py:272
  151.9 15.0 %collective-permute-start.20 = (f32[32,128]{1,0:T(8,128)S(1)}, f32[32,128]{1,0:T(8,128)S(1)}, u32[]{:S(2)}, u32[]{:S(2)}) collective-permute-start(f32[32,128]{1,0:T(8,128)S(1)} %add_add_fusion.1), channel_id=1, source_target_pairs={{128,0},{136,8},{144,16},{152,24},{160,32},{168,40},{176,48},{184,... | collective-permute-start | bytes 49160 | tf_op jit(solution)/shard_map/ppermute | solution.py:272
  153.2 13.7 %collective-permute-start.19 = (f32[32,128]{1,0:T(8,128)S(1)}, f32[32,128]{1,0:T(8,128)S(1)}, u32[]{:S(2)}, u32[]{:S(2)}) collective-permute-start(f32[32,128]{1,0:T(8,128)S(1)} %add_add_fusion.1), channel_id=1, source_target_pairs={{64,0},{72,8},{80,16},{88,24},{96,32},{104,40},{112,48},{120,56},{... | collective-permute-start | bytes 49160 | tf_op jit(solution)/shard_map/ppermute | solution.py:272
  157.2 26.9 %copy-start.3 = (bf16[512,128]{1,0:T(8,128)(2,1)}, bf16[512,128]{1,0:T(8,128)(2,1)S(1)}, u32[]{:S(2)}) copy-start(bf16[512,128]{1,0:T(8,128)(2,1)S(1)} %collective-permute-done.30.refs_1_) | copy-start | bytes 393220
  157.2 14.7 %collective-permute-start.32 = (bf16[512,128]{1,0:T(8,128)(2,1)}, bf16[512,128]{1,0:T(8,128)(2,1)S(1)}, u32[]{:S(2)}, u32[]{:S(2)}) collective-permute-start(bf16[512,128]{1,0:T(8,128)(2,1)} %get-tuple-element.42), channel_id=1, source_target_pairs={{0,3},{1,4},{2,5},{3,6},{4,7},{5,0},{6,1},{7,2},{8,11},{9,12},{10,... | collective-permute-start | bytes 393224 | tf_op jit(solution)/shard_map/ppermute | solution.py:344
  157.2 26.9 %copy-start.4 = (bf16[512,128]{1,0:T(8,128)(2,1)}, bf16[512,128]{1,0:T(8,128)(2,1)S(1)}, u32[]{:S(2)}) copy-start(bf16[512,128]{1,0:T(8,128)(2,1)S(1)} %collective-permute-done.31.refs_2_) | copy-start | bytes 393220
  157.2 14.6 %collective-permute-start.33 = (bf16[512,128]{1,0:T(8,128)(2,1)}, bf16[512,128]{1,0:T(8,128)(2,1)S(1)}, u32[]{:S(2)}, u32[]{:S(2)}) collective-permute-start(bf16[512,128]{1,0:T(8,128)(2,1)} %get-tuple-element.43), channel_id=1, source_target_pairs={{0,4},{1,5},{2,6},{3,7},{4,0},{5,1},{6,2},{7,3},{8,12},{9,13},{10,... | collective-permute-start | bytes 393224 | tf_op jit(solution)/shard_map/ppermute | solution.py:344
  159.9 14.1 %collective-permute-start.34 = (bf16[512,128]{1,0:T(8,128)(2,1)}, bf16[512,128]{1,0:T(8,128)(2,1)S(1)}, u32[]{:S(2)}, u32[]{:S(2)}) collective-permute-start(bf16[512,128]{1,0:T(8,128)(2,1)} %get-tuple-element.44), channel_id=1, source_target_pairs={{0,5},{1,6},{2,7},{3,0},{4,1},{5,2},{6,3},{7,4},{8,13},{9,14},{10,... | collective-permute-start | bytes 393224 | tf_op jit(solution)/shard_map/ppermute | solution.py:344
  166.9 17.1 %collective-permute-start.35 = (bf16[512,128]{1,0:T(8,128)(2,1)}, bf16[512,128]{1,0:T(8,128)(2,1)S(1)}, u32[]{:S(2)}, u32[]{:S(2)}) collective-permute-start(bf16[512,128]{1,0:T(8,128)(2,1)} %get-tuple-element.45), channel_id=1, source_target_pairs={{0,6},{1,7},{2,0},{3,1},{4,2},{5,3},{6,4},{7,5},{8,14},{9,15},{10,... | collective-permute-start | bytes 393224 | tf_op jit(solution)/shard_map/ppermute | solution.py:344
  166.9 17.1 %collective-permute-start.36 = (bf16[512,128]{1,0:T(8,128)(2,1)}, bf16[512,128]{1,0:T(8,128)(2,1)S(1)}, u32[]{:S(2)}, u32[]{:S(2)}) collective-permute-start(bf16[512,128]{1,0:T(8,128)(2,1)} %get-tuple-element.46), channel_id=1, source_target_pairs={{0,7},{1,0},{2,1},{3,2},{4,3},{5,4},{6,5},{7,6},{8,15},{9,8},{10,9... | collective-permute-start | bytes 393224 | tf_op jit(solution)/shard_map/ppermute | solution.py:344
  171.8 12.2 %copy-start.5 = (bf16[512,128]{1,0:T(8,128)(2,1)}, bf16[512,128]{1,0:T(8,128)(2,1)S(1)}, u32[]{:S(2)}) copy-start(bf16[512,128]{1,0:T(8,128)(2,1)S(1)} %collective-permute-done.32.refs_3_) | copy-start | bytes 393220
  171.8 12.2 %copy-start.6 = (bf16[512,128]{1,0:T(8,128)(2,1)}, bf16[512,128]{1,0:T(8,128)(2,1)S(1)}, u32[]{:S(2)}) copy-start(bf16[512,128]{1,0:T(8,128)(2,1)S(1)} %collective-permute-done.33.refs_4_) | copy-start | bytes 393220
  174.0 10.0 %copy-start.7 = (bf16[512,128]{1,0:T(8,128)(2,1)}, bf16[512,128]{1,0:T(8,128)(2,1)S(1)}, u32[]{:S(2)}) copy-start(bf16[512,128]{1,0:T(8,128)(2,1)S(1)} %collective-permute-done.34.refs_5_) | copy-start | bytes 393220
  183.9 0.7 copy-start.8
  184.0 0.7 copy-start.9

commit v5 on v4

--- a/solution.py
+++ b/solution.py
@@ -12,6 +12,9 @@
 F32 = jnp.float32
 BF16 = jnp.bfloat16
 
+LIMIT = pltpu.CompilerParams(vmem_limit_bytes=50 * 2**20)
+LIMIT_LAST = pltpu.CompilerParams(vmem_limit_bytes=50 * 2**20)
+
 
 def feature(real):
     return jnp.where(real > 0, real + 1.0, jnp.exp(jnp.minimum(real, 0.0)))
@@ -51,13 +54,16 @@
     return [fn(*items) for items in zip(*lists)]
 
 
-def key_state_kernel(step, k_ref, v_ref, state_ref, sum_ref):
+def key_sum_kernel(step, k_ref, sum_ref):
+    for j in range(step):
+        fk = feature(k_ref[:, columns(j)].astype(F32)).astype(BF16)
+        put_rows(sum_ref, step, j, jnp.sum(fk.astype(F32), axis=0, keepdims=True))
+
+
+def key_state_kernel(step, k_ref, v_ref, state_ref):
     heads = range(step)
     fk = [feature(k_ref[:, columns(j)].astype(F32)).astype(BF16) for j in heads]
     states = [dot_tn(fk[j], v_ref[:, columns(j)]) for j in heads]
-    for j in heads:
-        row = jnp.sum(fk[j].astype(F32), axis=0, keepdims=True)
-        put_rows(sum_ref, step, j, row)
     for j in heads:
         state_ref[j] = states[j].astype(BF16)
 
@@ -95,7 +101,18 @@
     return [-(s * i) * i for s, i in zip(shared, inverse)]
 
 
-def query_grad_kernel(step, q_ref, k_ref, v_ref, g_ref, z_ref, s_ref, gq_ref, dfk_ref, gv_ref, sum_ref):
+def query_grad_kernel(step, q_ref, k_ref, v_ref, g_ref, z_ref, s_away, *refs):
+    gq_ref, dfk_ref, gv_ref, sum_ref, s_all, sems = refs
+    now = pl.program_id(0)
+
+    def load(i):
+        return pltpu.make_async_copy(s_away.at[pl.ds(i * step, step)], s_all.at[i], sems.at[i])
+
+    @pl.when(now == 0)
+    def _():
+        for i in range(s_all.shape[0]):
+            load(i).start()
+
     mask = causal(q_ref.shape[0])
     heads = range(step)
     fq32 = [feature(q_ref[:, columns(j)].astype(F32)) for j in heads]
@@ -104,6 +121,8 @@
     zrows = [head_row(z_ref, step, j) for j in heads]
     v = [v_ref[:, columns(j)] for j in heads]
     weights, inverse = scores_of(fq, fk, zrows, mask)
+    load(now).wait()
+    s_ref = s_all.at[now]
     num = num_of(fq, weights, v, s_ref)
     dnum = [(g_ref[:, columns(j)].astype(F32) * inverse[j]).astype(BF16) for j in heads]
     pair = each(dot_nt, dnum, v)
@@ -124,8 +143,8 @@
 
 
 def key_grad_kernel(place_ref, k_hbm, v_hbm, dfk_hbm, gv_hbm, rz_ref, *refs):
-    group = len(refs) - 7
-    pieces, (gk_ref, gv_out_ref), loaded, sems = refs[:group], refs[group : group + 2], refs[-5:-1], refs[-1]
+    group = len(refs) - 8
+    pieces, (gk_ref, gv_out_ref), loaded, sems = refs[:group], refs[group : group + 2], refs[-6:-1], refs[-1]
     rows = pieces[0].shape[0]
     owners = [lax.rem(place_ref[0] + group - d, group) for d in range(group)]
     ats = [pl.multiple_of(owner * rows, rows) for owner in owners]
@@ -134,19 +153,20 @@
             pltpu.make_async_copy(src.at[:, pl.ds(at, rows)], dst.at[d], sems.at[n, d])
             for n, (src, dst) in enumerate(zip((k_hbm, v_hbm, dfk_hbm, gv_hbm), loaded))
         ]
+        + [pltpu.make_async_copy(pieces[d], loaded[-1].at[d], sems.at[4, d])]
         for d, at in enumerate(ats)
     ]
     for some in copies:
         for copy in some:
             copy.start()
-    k, v, dfk_in, gv_in = loaded
+    k, v, dfk_in, gv_in, suffix = loaded
     for first in range(0, group, 2):
         work = []
         for d in (first, first + 1):
             for copy in copies[d]:
                 copy.wait()
             work += [(d, j) for j in range(rows // HD)]
-        states = [pieces[d][columns(j), :] for d, j in work]
+        states = [suffix[d, columns(j), :] for d, j in work]
         fk32 = [feature(k[d, :, columns(j)].astype(F32)) for d, j in work]
         dfk = [dot_nt(v[d, :, columns(j)], state) for (d, j), state in zip(work, states)]
         gv = [dot_nn(f.astype(BF16), state) for f, state in zip(fk32, states)]
@@ -165,11 +185,12 @@
     whole, away = pl.BlockSpec(memory_space=pltpu.VMEM), pl.BlockSpec(memory_space=pl.ANY)
     return pl.pallas_call(
         key_grad_kernel,
-        in_specs=[pl.BlockSpec(memory_space=pltpu.SMEM)] + [away] * 4 + [whole] * (1 + group),
+        in_specs=[pl.BlockSpec(memory_space=pltpu.SMEM)] + [away] * 4 + [whole] + [away] * group,
         out_specs=[whole] * 2,
         out_shape=[jax.ShapeDtypeStruct((tokens, width), BF16)] * 2,
         scratch_shapes=[pltpu.VMEM((group, tokens, rows), x.dtype) for x in (k, v, dfk, gv)]
-        + [pltpu.SemaphoreType.DMA((4, group))],
+        + [pltpu.VMEM((group, rows, HD), BF16), pltpu.SemaphoreType.DMA((5, group))],
+        compiler_params=LIMIT_LAST,
     )(place, k, v, dfk, gv, r, *pieces)
 
 
@@ -178,7 +199,7 @@
     square = pl.BlockSpec((step, HD, HD), lambda i: (i, 0, 0))
     rows = pl.BlockSpec((heads, HD), lambda i: (0, 0))
     copies = pl.BlockSpec((group, heads, HD), lambda i: (0, 0, 0))
-    specs = {"g": copies, "w": wide, "f": wide, "s": square, "r": rows}
+    specs = {"a": pl.BlockSpec(memory_space=pl.ANY), "g": copies, "w": wide, "f": wide, "s": square, "r": rows}
     shapes = {
         "g": jax.ShapeDtypeStruct((group, heads, HD), F32),
         "w": jax.ShapeDtypeStruct((tokens, heads * HD), BF16),
@@ -192,7 +213,13 @@
         in_specs=[specs[t] for t in kinds_in],
         out_specs=[specs[t] for t in kinds_out],
         out_shape=[shapes[t] for t in kinds_out],
-        compiler_params=pltpu.CompilerParams(dimension_semantics=("arbitrary",)),
+        scratch_shapes=[
+            pltpu.VMEM((heads // step, step, HD, HD), BF16),
+            pltpu.SemaphoreType.DMA((heads // step,)),
+        ]
+        if "a" in kinds_in
+        else [],
+        compiler_params=LIMIT if "a" in kinds_in else None,
     )(*arrays)
 
 
@@ -316,10 +343,11 @@
 
     ranks = jnp.arange(group)[:, None, None]
     where = jnp.full((1,), place, jnp.int32)
-    key_state, key_sum = call(key_state_kernel, 16, "ww", "sg", (keys, values))
+    (key_sum,) = call(key_sum_kernel, 16, "w", "g", (keys,))
     sums = z_gather(key_sum)
     before = jnp.sum(jnp.where(ranks < place, sums, 0.0), axis=0)
     total = jnp.sum(sums, axis=0)
+    (key_state,) = call(key_state_kernel, 16, "ww", "s", (keys, values))
     key_state, before, total = lax.optimization_barrier((key_state, before, total))
     key_parts = to_owners(key_state)
     z = before + ctx_running(total, ctx, True, F32, False)
@@ -335,7 +363,7 @@
     query_base = ctx_running(query_total, ctx, False, BF16, True)
     spread = z_spread(where, query_parts, query_base)
     grad_queries, dfk, gv, query_sum = call(
-        query_grad_kernel, 8, "wwwwrs", "wffg", (queries, keys, values, out_grad, z, prefix)
+        query_grad_kernel, 8, "wwwwra", "wffg", (queries, keys, values, out_grad, z, prefix)
     )
     sums = z_gather(query_sum)
     pieces = [spread[0]] + [None] * (group - 1)

time: 194 us -> 194 us (level)
  waiting for transfers between devices: 75.6 us -> 70.4 us
  other arithmetic: 3.55 us -> 5.74 us
  Pallas kernels: 26.7 us -> 28.7 us
    all_to_all x2, waiting for transfers between devices: 15.1 us -> 11.2 us  [z_gather(): return lax.all_to_all(copies, 'head', 0, 0, tiled=True)]
    pallas_call x3 -> x4, Pallas kernels: 15.7 us -> 18.6 us  [head_call(): pl.pallas_call(functools.partial(kernel, step), grid=(heads // step,), in...]
    all_to_all x1, waiting for transfers between devices: 16.7 us -> 14.3 us  [from_owners(): return lax.all_to_all(x, 'head', 0, 0, tiled=True).reshape(heads, HD, HD)]
  transfers between devices with their start and end apart: 42 -> 42, of which waited for: 24 -> 25; matrix products, arithmetic and copies ran while one was open for 2% -> 3% of each run, Pallas kernels for 9% -> 11%
where the time goes in v5:
time: 194 us; the launch traced here: 191 us
  starting transfers between devices  83.9 us (43%)
  waiting for transfers between devices  70.4 us (36%)
  Pallas kernels  28.7 us (15%)
  other arithmetic  5.74 us (3%)
    ppermute x24, starting transfers between devices, hop(): return lax.ppermute(value, 'ctx', pairs)  39.1 us
    ppermute x7, waiting for transfers between devices, shards(): pieces[d] = lax.ppermute(spread[d], 'head', pairs)  19.4 us
    pallas_call x4, Pallas kernels, head_call(): pl.pallas_call(functools.partial(kernel, step), grid=(heads // step,), in...  18.6 us
    ppermute x24, waiting for transfers between devices, hop(): return lax.ppermute(value, 'ctx', pairs)  14.3 us
    all_to_all x1, waiting for transfers between devices, from_owners(): return lax.all_to_all(x, 'head', 0, 0, tiled=True).reshape(heads, HD, HD)  14.3 us
    all_to_all x2, starting transfers between devices, z_gather(): return lax.all_to_all(copies, 'head', 0, 0, tiled=True)  12.4 us
    all_to_all x2, waiting for transfers between devices, z_gather(): return lax.all_to_all(copies, 'head', 0, 0, tiled=True)  11.2 us
    ppermute x7, starting transfers between devices, shards(): pieces[d] = lax.ppermute(spread[d], 'head', pairs)  10.5 us
  transfers between devices with their start and end apart: 42, of which 25 were waited for; matrix products, arithmetic and copies ran while one was open for 3% of the time, Pallas kernels for 11%

profile of v5, /device:TPU:1, one launch (start us, length us, event | category | flops | bytes accessed | tf_op | source)
XLA Modules:
  0.0 190.9 jit_solution(3588148067940138231)
XLA Ops:
  0.6 2.4 %shard_map.68 = f32[8,32,128]{2,1,0:T(8,128)} custom-call(bf16[128,4096]{1,0:T(8,128)(2,1)} %k_hbm.1), custom_call_target="tpu_custom_call" | custom-call | tf_op jit(solution)/shard_map/pallas_call | solution.py:210
  3.0 9.0 %all-to-all-start = ((f32[8,32,128]{2,1,0:T(8,128)}), f32[8,32,128]{2,1,0:T(8,128)S(1)}, u32[]{:S(2)}, u32[]{:S(2)}) async-start(f32[8,32,128]{2,1,0:T(8,128)} %shard_map.68), calls=%async_computation | async-start | bytes 262144 | tf_op jit(solution)/shard_map/all_to_all | solution.py:328
  12.0 3.0 %shard_map.67 = bf16[32,128,128]{2,1,0:T(8,128)(2,1)} custom-call(bf16[128,4096]{1,0:T(8,128)(2,1)} %k_hbm.1, bf16[128,4096]{1,0:T(8,128)(2,1)} %v_hbm.1), custom_call_target="tpu_custom_call" | custom-call | tf_op jit(solution)/shard_map/pallas_call | solution.py:210
  15.1 4.7 %all-to-all-done = f32[8,32,128]{2,1,0:T(8,128)S(1)} async-done(((f32[8,32,128]{2,1,0:T(8,128)}), f32[8,32,128]{2,1,0:T(8,128)S(1)}, u32[]{:S(2)}, u32[]{:S(2)}) %all-to-all-start) | async-done | bytes 131104 | tf_op jit(solution)/shard_map/all_to_all | solution.py:328
  19.9 3.6 %all-to-all-start.1 = ((bf16[8,512,128]{2,1,0:T(8,128)(2,1)}), bf16[8,512,128]{2,1,0:T(8,128)(2,1)S(1)}, u32[]{:S(2)}, u32[]{:S(2)}) async-start(bf16[8,512,128]{2,1,0:T(8,128)(2,1)} %bitcast.4), calls=%async_computation.1 | async-start | bytes 2097152 | tf_op jit(solution)/shard_map/all_to_all | solution.py:339
  23.5 2.4 %collective-permute-start = (f32[32,128]{1,0:T(8,128)S(1)}, f32[32,128]{1,0:T(8,128)S(1)}, u32[]{:S(2)}, u32[]{:S(2)}) collective-permute-start(f32[32,128]{1,0:T(8,128)S(1)} %get-tuple-element.25), channel_id=1, source_target_pairs={{0,8},{8,0},{16,24},{24,16},{32,40},{40,32},{48,56},{56,48},{64,72... | collective-permute-start | bytes 49160 | tf_op jit(solution)/shard_map/ppermute | solution.py:305
  25.8 0.8 collective-permute-done
  26.7 2.7 %collective-permute-start.3 = (f32[32,128]{1,0:T(8,128)S(1)}, f32[32,128]{1,0:T(8,128)S(1)}, u32[]{:S(2)}, u32[]{:S(2)}) collective-permute-start(f32[32,128]{1,0:T(8,128)S(1)} %add.142), channel_id=1, source_target_pairs={{0,48},{8,56},{16,0},{24,8},{32,16},{40,24},{48,32},{56,40},{64,11... | collective-permute-start | bytes 49160 | tf_op jit(solution)/shard_map/ppermute | solution.py:299
  30.5 3.3 %collective-permute-done.2 = f32[32,128]{1,0:T(8,128)S(1)} collective-permute-done((f32[32,128]{1,0:T(8,128)S(1)}, f32[32,128]{1,0:T(8,128)S(1)}, u32[]{:S(2)}, u32[]{:S(2)}) %collective-permute-start.2) | collective-permute-done | bytes 16416 | tf_op jit(solution)/shard_map/ppermute | solution.py:299
  34.0 4.4 %collective-permute-start.6 = (f32[32,128]{1,0:T(8,128)S(1)}, f32[32,128]{1,0:T(8,128)S(1)}, u32[]{:S(2)}, u32[]{:S(2)}) collective-permute-start(f32[32,128]{1,0:T(8,128)S(1)} %add_add_fusion.3), channel_id=1, source_target_pairs={{0,192},{8,200},{16,208},{24,216},{32,224},{40,232},{48,240},{56,2... | collective-permute-start | bytes 49160 | tf_op jit(solution)/shard_map/ppermute | solution.py:299
  38.4 1.3 collective-permute-start.5
  39.7 2.5 %collective-permute-start.4 = (f32[32,128]{1,0:T(8,128)S(1)}, f32[32,128]{1,0:T(8,128)S(1)}, u32[]{:S(2)}, u32[]{:S(2)}) collective-permute-start(f32[32,128]{1,0:T(8,128)S(1)} %add_add_fusion.3), channel_id=1, source_target_pairs={{0,64},{8,72},{16,80},{24,88},{32,96},{40,104},{48,112},{56,120},{... | collective-permute-start | bytes 49160 | tf_op jit(solution)/shard_map/ppermute | solution.py:299
  42.2 0.8 collective-permute-done.4
  43.6 4.5 %shard_map.69 = bf16[32,128,128]{2,1,0:T(8,128)(2,1)} custom-call(bf16[128,4096]{1,0:T(8,128)(2,1)} %q_ref.3, bf16[128,4096]{1,0:T(8,128)(2,1)} %k_hbm.1, bf16[128,4096]{1,0:T(8,128)(2,1)} %g_ref.3, f32[32,128]{1,0:T(8,128)} %add_add_fusion.2.z_ref), custom_call_target="tpu_custom_call" | custom-call | tf_op jit(solution)/shard_map/pallas_call | solution.py:210
  48.1 4.4 %all-to-all-done.1.x_ref = bf16[8,512,128]{2,1,0:T(8,128)(2,1)S(1)} async-done(((bf16[8,512,128]{2,1,0:T(8,128)(2,1)}), bf16[8,512,128]{2,1,0:T(8,128)(2,1)S(1)}, u32[]{:S(2)}, u32[]{:S(2)}) %all-to-all-start.1) | async-done | bytes 1048608 | tf_op jit(solution)/shard_map/all_to_all | solution.py:339
  52.5 4.2 %all-to-all-start.2 = ((bf16[8,512,128]{2,1,0:T(8,128)(2,1)}), bf16[8,512,128]{2,1,0:T(8,128)(2,1)}, u32[]{:S(2)}, u32[]{:S(2)}) async-start(bf16[8,512,128]{2,1,0:T(8,128)(2,1)} %bitcast.5), calls=%async_computation.2 | async-start | bytes 2097152 | tf_op jit(solution)/shard_map/all_to_all | solution.py:339
  56.9 1.3 collective-permute-start.7
  58.2 1.2 collective-permute-done.7
  59.4 2.2 %collective-permute-start.10 = (bf16[256,128]{1,0:T(8,128)(2,1)S(1)}, bf16[256,128]{1,0:T(8,128)(2,1)S(1)}, u32[]{:S(2)}, u32[]{:S(2)}) collective-permute-start(bf16[256,128]{1,0:T(8,128)(2,1)S(1)} %fusion.8), channel_id=1, source_target_pairs={{0,48},{8,56},{16,0},{24,8},{32,16},{40,24},{48,32},{56,40},{64,11... | collective-permute-start | bytes 196616 | tf_op jit(solution)/shard_map/ppermute | solution.py:299
  61.9 0.7 collective-permute-start.8
  63.0 3.6 %collective-permute-done.9 = bf16[256,128]{1,0:T(8,128)(2,1)S(1)} collective-permute-done((bf16[256,128]{1,0:T(8,128)(2,1)S(1)}, bf16[256,128]{1,0:T(8,128)(2,1)S(1)}, u32[]{:S(2)}, u32[]{:S(2)}) %collective-permute-start.9) | collective-permute-done | bytes 65568 | tf_op jit(solution)/shard_map/ppermute | solution.py:299
  66.6 1.5 collective-permute-done.8
  68.2 4.4 %collective-permute-start.13 = (bf16[256,128]{1,0:T(8,128)(2,1)S(1)}, bf16[256,128]{1,0:T(8,128)(2,1)S(1)}, u32[]{:S(2)}, u32[]{:S(2)}) collective-permute-start(bf16[256,128]{1,0:T(8,128)(2,1)S(1)} %fusion.3), channel_id=1, source_target_pairs={{0,192},{8,200},{16,208},{24,216},{32,224},{40,232},{48,240},{56,2... | collective-permute-start | bytes 196616 | tf_op jit(solution)/shard_map/ppermute | solution.py:299
  72.6 1.3 collective-permute-start.12
  73.9 2.5 %collective-permute-start.11 = (bf16[256,128]{1,0:T(8,128)(2,1)S(1)}, bf16[256,128]{1,0:T(8,128)(2,1)S(1)}, u32[]{:S(2)}, u32[]{:S(2)}) collective-permute-start(bf16[256,128]{1,0:T(8,128)(2,1)S(1)} %fusion.3), channel_id=1, source_target_pairs={{0,64},{8,72},{16,80},{24,88},{32,96},{40,104},{48,112},{56,120},{... | collective-permute-start | bytes 196616 | tf_op jit(solution)/shard_map/ppermute | solution.py:299
  76.4 1.3 collective-permute-done.11
  77.7 2.1 %collective-permute-start.14 = (f32[256,128]{1,0:T(8,128)S(1)}, f32[256,128]{1,0:T(8,128)S(1)}, u32[]{:S(2)}, u32[]{:S(2)}) collective-permute-start(f32[256,128]{1,0:T(8,128)S(1)} %fusion.2), channel_id=1, source_target_pairs={{0,8},{8,0},{16,24},{24,16},{32,40},{40,32},{48,56},{56,48},{64,72... | collective-permute-start | bytes 393224 | tf_op jit(solution)/shard_map/ppermute | solution.py:305
  79.8 1.0 collective-permute-done.14
  80.8 0.7 maximum_add_fusion.base_ref
  81.6 2.4 %shard_map.70 = bf16[8,512,128]{2,1,0:T(8,128)(2,1)} custom-call(bf16[8,512,128]{2,1,0:T(8,128)(2,1)} %copy-done.5, f32[512,128]{1,0:T(8,128)} %maximum_add_fusion.base_ref), custom_call_target="tpu_custom_call" | custom-call | tf_op jit(solution)/shard_map/pallas_call | solution.py:250
  84.0 1.9 %all-to-all-done.2.x_ref = bf16[8,512,128]{2,1,0:T(8,128)(2,1)} async-done(((bf16[8,512,128]{2,1,0:T(8,128)(2,1)}), bf16[8,512,128]{2,1,0:T(8,128)(2,1)}, u32[]{:S(2)}, u32[]{:S(2)}) %all-to-all-start.2) | async-done | bytes 1048608 | tf_op jit(solution)/shard_map/all_to_all | solution.py:339
  85.9 5.2 %all-to-all-start.3 = ((bf16[8,512,128]{2,1,0:T(8,128)(2,1)}), bf16[8,512,128]{2,1,0:T(8,128)(2,1)}, u32[]{:S(2)}, u32[]{:S(2)}) async-start(bf16[8,512,128]{2,1,0:T(8,128)(2,1)} %shard_map.70), calls=%async_computation.3 | async-start | bytes 2097152 | tf_op jit(solution)/shard_map/all_to_all | solution.py:342
  91.1 1.4 convert_reduce_fusion
  92.5 0.7 collective-permute-start.22
  93.2 1.2 collective-permute-done.22
  94.8 2.6 %collective-permute-start.24 = (bf16[256,128]{1,0:T(8,128)(2,1)S(1)}, bf16[256,128]{1,0:T(8,128)(2,1)S(1)}, u32[]{:S(2)}, u32[]{:S(2)}) collective-permute-start(bf16[256,128]{1,0:T(8,128)(2,1)S(1)} %fusion.9), channel_id=1, source_target_pairs={{0,32},{8,40},{16,48},{24,56},{32,0},{40,8},{48,16},{56,24},{64,96... | collective-permute-start | bytes 196616 | tf_op jit(solution)/shard_map/ppermute | solution.py:299
  97.4 1.1 collective-permute-start.23
  98.8 1.9 collective-permute-done.24
  100.7 0.9 collective-permute-done.23
  102.3 1.3 collective-permute-start.28
  103.6 1.3 collective-permute-start.27
  104.9 1.3 collective-permute-start.26
  106.2 14.3 %all-to-all-done.3 = bf16[8,512,128]{2,1,0:T(8,128)(2,1)} async-done(((bf16[8,512,128]{2,1,0:T(8,128)(2,1)}), bf16[8,512,128]{2,1,0:T(8,128)(2,1)}, u32[]{:S(2)}, u32[]{:S(2)}) %all-to-all-start.3) | async-done | bytes 1048608 | tf_op jit(solution)/shard_map/all_to_all | solution.py:342
  120.5 8.7 %shard_map.71 = (bf16[128,4096]{1,0:T(8,128)(2,1)}, f32[128,4096]{1,0:T(8,128)}, f32[128,4096]{1,0:T(8,128)}, f32[8,32,128]{2,1,0:T(8,128)}) custom-call(bf16[128,4096]{1,0:T(8,128)(2,1)S(1)} %copy-done.2, bf16[128,4096]{1,0:T(8,128)(2,1)S(1)} %copy-done, bf16[128,4096]{1,0:T(8,128)(2,1)S(1)} %copy-done.1, bf16[128,4096]{1,0:T(8,128)(2,1)} %g_ref.3, ...), custom_call_target="tpu_custom_call" | custom-call | tf_op jit(solution)/shard_map/pallas_call | solution.py:210
  129.2 3.4 %all-to-all-start.4 = ((f32[8,32,128]{2,1,0:T(8,128)}), f32[8,32,128]{2,1,0:T(8,128)S(1)}, u32[]{:S(2)}, u32[]{:S(2)}) async-start(f32[8,32,128]{2,1,0:T(8,128)} %get-tuple-element.33), calls=%async_computation.4 | async-start | bytes 262144 | tf_op jit(solution)/shard_map/all_to_all | solution.py:328
  132.6 1.0 fusion.6
  134.2 6.5 %all-to-all-done.4 = f32[8,32,128]{2,1,0:T(8,128)S(1)} async-done(((f32[8,32,128]{2,1,0:T(8,128)}), f32[8,32,128]{2,1,0:T(8,128)S(1)}, u32[]{:S(2)}, u32[]{:S(2)}) %all-to-all-start.4) | async-done | bytes 131104 | tf_op jit(solution)/shard_map/all_to_all | solution.py:328
  140.7 2.0 %collective-permute-start.15 = (f32[32,128]{1,0:T(8,128)S(1)}, f32[32,128]{1,0:T(8,128)S(1)}, u32[]{:S(2)}, u32[]{:S(2)}) collective-permute-start(f32[32,128]{1,0:T(8,128)S(1)} %get-tuple-element.45), channel_id=1, source_target_pairs={{0,8},{8,0},{16,24},{24,16},{32,40},{40,32},{48,56},{56,48},{64,72... | collective-permute-start | bytes 49160 | tf_op jit(solution)/shard_map/ppermute | solution.py:305
  142.7 0.8 collective-permute-done.15
  143.8 2.6 %collective-permute-start.17 = (f32[32,128]{1,0:T(8,128)S(1)}, f32[32,128]{1,0:T(8,128)S(1)}, u32[]{:S(2)}, u32[]{:S(2)}) collective-permute-start(f32[32,128]{1,0:T(8,128)S(1)} %add.163), channel_id=1, source_target_pairs={{0,32},{8,40},{16,48},{24,56},{32,0},{40,8},{48,16},{56,24},{64,96... | collective-permute-start | bytes 49160 | tf_op jit(solution)/shard_map/ppermute | solution.py:299
  146.4 1.1 collective-permute-start.16
  147.5 0.7 maximum_add_fusion.1.base_ref
  148.2 2.4 %shard_map.72 = (bf16[512,128]{1,0:T(8,128)(2,1)}, bf16[512,128]{1,0:T(8,128)(2,1)}, bf16[512,128]{1,0:T(8,128)(2,1)}, bf16[512,128]{1,0:T(8,128)(2,1)}, bf16[51...) custom-call(s32[1]{0:T(128)} %bitcast.3.place_ref, ...), custom_call_target="tpu_custom_call" | custom-call | tf_op jit(solution)/shard_map/pallas_call | solution.py:261
  151.1 1.3 collective-permute-start.21
  152.4 1.3 collective-permute-start.20
  153.7 1.3 collective-permute-start.19
  155.0 2.7 %collective-permute-done.30.refs_1_ = bf16[512,128]{1,0:T(8,128)(2,1)S(1)} collective-permute-done((bf16[512,128]{1,0:T(8,128)(2,1)}, bf16[512,128]{1,0:T(8,128)(2,1)S(1)}, u32[]{:S(2)}, u32[]{:S(2)}) %collective-permute-start.30) | collective-permute-done | bytes 131104 | tf_op jit(solution)/shard_map/ppermute | solution.py:372
  157.7 2.7 %collective-permute-start.33 = (bf16[512,128]{1,0:T(8,128)(2,1)}, bf16[512,128]{1,0:T(8,128)(2,1)S(1)}, u32[]{:S(2)}, u32[]{:S(2)}) collective-permute-start(bf16[512,128]{1,0:T(8,128)(2,1)} %get-tuple-element.39), channel_id=1, source_target_pairs={{0,4},{1,5},{2,6},{3,7},{4,0},{5,1},{6,2},{7,3},{8,12},{9,13},{10,... | collective-permute-start | bytes 393224 | tf_op jit(solution)/shard_map/ppermute | solution.py:372
  160.4 7.0 %collective-permute-start.34 = (bf16[512,128]{1,0:T(8,128)(2,1)}, bf16[512,128]{1,0:T(8,128)(2,1)S(1)}, u32[]{:S(2)}, u32[]{:S(2)}) collective-permute-start(bf16[512,128]{1,0:T(8,128)(2,1)} %get-tuple-element.40), channel_id=1, source_target_pairs={{0,5},{1,6},{2,7},{3,0},{4,1},{5,2},{6,3},{7,4},{8,13},{9,14},{10,... | collective-permute-start | bytes 393224 | tf_op jit(solution)/shard_map/ppermute | solution.py:372
  167.8 4.6 %collective-permute-done.32.refs_3_ = bf16[512,128]{1,0:T(8,128)(2,1)S(1)} collective-permute-done((bf16[512,128]{1,0:T(8,128)(2,1)}, bf16[512,128]{1,0:T(8,128)(2,1)S(1)}, u32[]{:S(2)}, u32[]{:S(2)}) %collective-permute-start.32) | collective-permute-done | bytes 131104 | tf_op jit(solution)/shard_map/ppermute | solution.py:372
  172.4 2.3 %collective-permute-done.34.refs_5_ = bf16[512,128]{1,0:T(8,128)(2,1)S(1)} collective-permute-done((bf16[512,128]{1,0:T(8,128)(2,1)}, bf16[512,128]{1,0:T(8,128)(2,1)S(1)}, u32[]{:S(2)}, u32[]{:S(2)}) %collective-permute-start.34) | collective-permute-done | bytes 131104 | tf_op jit(solution)/shard_map/ppermute | solution.py:372
  174.6 9.8 %collective-permute-done.35.refs_6_ = bf16[512,128]{1,0:T(8,128)(2,1)S(1)} collective-permute-done((bf16[512,128]{1,0:T(8,128)(2,1)}, bf16[512,128]{1,0:T(8,128)(2,1)S(1)}, u32[]{:S(2)}, u32[]{:S(2)}) %collective-permute-start.35) | collective-permute-done | bytes 131104 | tf_op jit(solution)/shard_map/ppermute | solution.py:372
  184.5 0.9 copy-done.4
  185.4 5.3 %shard_map.73 = (bf16[128,4096]{1,0:T(8,128)(2,1)}, bf16[128,4096]{1,0:T(8,128)(2,1)}) custom-call(s32[1]{0:T(128)} %bitcast.3.place_ref, bf16[128,4096]{1,0:T(8,128)(2,1)S(1)} %copy-done, bf16[128,4096]{1,0:T(8,128)(2,1)S(1)} %copy-done.1, f32[128,4096]{1,0:T(8,128)} %get-tuple-element.31.dfk_hbm, f32[128,4096]{1,0:T(8,128)} %get-tuple-element.32.gv_hbm, ...), custom_call_target="tpu_custom_call" | custom-call | tf_op jit(solution)/shard_map/pallas_call | solution.py:186
  (65 shorter events, 6.3 us)
Async XLA Ops:
  3.0 16.8 %all-to-all-start = ((f32[8,32,128]{2,1,0:T(8,128)}), f32[8,32,128]{2,1,0:T(8,128)S(1)}, u32[]{:S(2)}, u32[]{:S(2)}) async-start(f32[8,32,128]{2,1,0:T(8,128)} %shard_map.68), calls=%async_computation | async-start | bytes 262144 | tf_op jit(solution)/shard_map/all_to_all | solution.py:328
  19.9 32.6 %all-to-all-start.1 = ((bf16[8,512,128]{2,1,0:T(8,128)(2,1)}), bf16[8,512,128]{2,1,0:T(8,128)(2,1)S(1)}, u32[]{:S(2)}, u32[]{:S(2)}) async-start(bf16[8,512,128]{2,1,0:T(8,128)(2,1)} %bitcast.4), calls=%async_computation.1 | async-start | bytes 2097152 | tf_op jit(solution)/shard_map/all_to_all | solution.py:339
  23.5 3.2 %collective-permute-start = (f32[32,128]{1,0:T(8,128)S(1)}, f32[32,128]{1,0:T(8,128)S(1)}, u32[]{:S(2)}, u32[]{:S(2)}) collective-permute-start(f32[32,128]{1,0:T(8,128)S(1)} %get-tuple-element.25), channel_id=1, source_target_pairs={{0,8},{8,0},{16,24},{24,16},{32,40},{40,32},{48,56},{56,48},{64,72... | collective-permute-start | bytes 49160 | tf_op jit(solution)/shard_map/ppermute | solution.py:305
  26.7 3.8 %collective-permute-start.3 = (f32[32,128]{1,0:T(8,128)S(1)}, f32[32,128]{1,0:T(8,128)S(1)}, u32[]{:S(2)}, u32[]{:S(2)}) collective-permute-start(f32[32,128]{1,0:T(8,128)S(1)} %add.142), channel_id=1, source_target_pairs={{0,48},{8,56},{16,0},{24,8},{32,16},{40,24},{48,32},{56,40},{64,11... | collective-permute-start | bytes 49160 | tf_op jit(solution)/shard_map/ppermute | solution.py:299
  29.4 4.4 %collective-permute-start.2 = (f32[32,128]{1,0:T(8,128)S(1)}, f32[32,128]{1,0:T(8,128)S(1)}, u32[]{:S(2)}, u32[]{:S(2)}) collective-permute-start(f32[32,128]{1,0:T(8,128)S(1)} %add.142), channel_id=1, source_target_pairs={{0,32},{8,40},{16,48},{24,56},{32,0},{40,8},{48,16},{56,24},{64,96... | collective-permute-start | bytes 49160 | tf_op jit(solution)/shard_map/ppermute | solution.py:299
  29.8 4.2 %collective-permute-start.1 = (f32[32,128]{1,0:T(8,128)S(1)}, f32[32,128]{1,0:T(8,128)S(1)}, u32[]{:S(2)}, u32[]{:S(2)}) collective-permute-start(f32[32,128]{1,0:T(8,128)S(1)} %add.142), channel_id=1, source_target_pairs={{0,16},{8,24},{16,32},{24,40},{32,48},{40,56},{48,0},{56,8},{64,80... | collective-permute-start | bytes 49160 | tf_op jit(solution)/shard_map/ppermute | solution.py:299
  34.0 8.2 %collective-permute-start.6 = (f32[32,128]{1,0:T(8,128)S(1)}, f32[32,128]{1,0:T(8,128)S(1)}, u32[]{:S(2)}, u32[]{:S(2)}) collective-permute-start(f32[32,128]{1,0:T(8,128)S(1)} %add_add_fusion.3), channel_id=1, source_target_pairs={{0,192},{8,200},{16,208},{24,216},{32,224},{40,232},{48,240},{56,2... | collective-permute-start | bytes 49160 | tf_op jit(solution)/shard_map/ppermute | solution.py:299
  38.4 3.8 %collective-permute-start.5 = (f32[32,128]{1,0:T(8,128)S(1)}, f32[32,128]{1,0:T(8,128)S(1)}, u32[]{:S(2)}, u32[]{:S(2)}) collective-permute-start(f32[32,128]{1,0:T(8,128)S(1)} %add_add_fusion.3), channel_id=1, source_target_pairs={{0,128},{8,136},{16,144},{24,152},{32,160},{40,168},{48,176},{56,1... | collective-permute-start | bytes 49160 | tf_op jit(solution)/shard_map/ppermute | solution.py:299
  39.7 3.3 %collective-permute-start.4 = (f32[32,128]{1,0:T(8,128)S(1)}, f32[32,128]{1,0:T(8,128)S(1)}, u32[]{:S(2)}, u32[]{:S(2)}) collective-permute-start(f32[32,128]{1,0:T(8,128)S(1)} %add_add_fusion.3), channel_id=1, source_target_pairs={{0,64},{8,72},{16,80},{24,88},{32,96},{40,104},{48,112},{56,120},{... | collective-permute-start | bytes 49160 | tf_op jit(solution)/shard_map/ppermute | solution.py:299
  52.5 6.9 %copy-start.5 = (bf16[8,512,128]{2,1,0:T(8,128)(2,1)}, bf16[8,512,128]{2,1,0:T(8,128)(2,1)S(1)}, u32[]{:S(2)}) copy-start(bf16[8,512,128]{2,1,0:T(8,128)(2,1)S(1)} %all-to-all-done.1.x_ref) | copy-start | bytes 3145732
  52.5 33.4 %all-to-all-start.2 = ((bf16[8,512,128]{2,1,0:T(8,128)(2,1)}), bf16[8,512,128]{2,1,0:T(8,128)(2,1)}, u32[]{:S(2)}, u32[]{:S(2)}) async-start(bf16[8,512,128]{2,1,0:T(8,128)(2,1)} %bitcast.5), calls=%async_computation.2 | async-start | bytes 2097152 | tf_op jit(solution)/shard_map/all_to_all | solution.py:339
  56.9 2.4 %collective-permute-start.7 = (f32[512,128]{1,0:T(8,128)S(1)}, f32[512,128]{1,0:T(8,128)S(1)}, u32[]{:S(2)}, u32[]{:S(2)}) collective-permute-start(f32[512,128]{1,0:T(8,128)S(1)} %convert_reduce_fusion.1), channel_id=1, source_target_pairs={{0,8},{8,0},{16,24},{24,16},{32,40},{40,32},{48,56},{56,48},{64,72... | collective-permute-start | bytes 786440 | tf_op jit(solution)/shard_map/ppermute | solution.py:305
  59.4 3.6 %collective-permute-start.10 = (bf16[256,128]{1,0:T(8,128)(2,1)S(1)}, bf16[256,128]{1,0:T(8,128)(2,1)S(1)}, u32[]{:S(2)}, u32[]{:S(2)}) collective-permute-start(bf16[256,128]{1,0:T(8,128)(2,1)S(1)} %fusion.8), channel_id=1, source_target_pairs={{0,48},{8,56},{16,0},{24,8},{32,16},{40,24},{48,32},{56,40},{64,11... | collective-permute-start | bytes 196616 | tf_op jit(solution)/shard_map/ppermute | solution.py:299
  61.6 5.0 %collective-permute-start.9 = (bf16[256,128]{1,0:T(8,128)(2,1)S(1)}, bf16[256,128]{1,0:T(8,128)(2,1)S(1)}, u32[]{:S(2)}, u32[]{:S(2)}) collective-permute-start(bf16[256,128]{1,0:T(8,128)(2,1)S(1)} %fusion.8), channel_id=1, source_target_pairs={{0,32},{8,40},{16,48},{24,56},{32,0},{40,8},{48,16},{56,24},{64,96... | collective-permute-start | bytes 196616 | tf_op jit(solution)/shard_map/ppermute | solution.py:299
  61.9 6.2 %collective-permute-start.8 = (bf16[256,128]{1,0:T(8,128)(2,1)S(1)}, bf16[256,128]{1,0:T(8,128)(2,1)S(1)}, u32[]{:S(2)}, u32[]{:S(2)}) collective-permute-start(bf16[256,128]{1,0:T(8,128)(2,1)S(1)} %fusion.8), channel_id=1, source_target_pairs={{0,16},{8,24},{16,32},{24,40},{32,48},{40,56},{48,0},{56,8},{64,80... | collective-permute-start | bytes 196616 | tf_op jit(solution)/shard_map/ppermute | solution.py:299
  68.2 8.2 %collective-permute-start.13 = (bf16[256,128]{1,0:T(8,128)(2,1)S(1)}, bf16[256,128]{1,0:T(8,128)(2,1)S(1)}, u32[]{:S(2)}, u32[]{:S(2)}) collective-permute-start(bf16[256,128]{1,0:T(8,128)(2,1)S(1)} %fusion.3), channel_id=1, source_target_pairs={{0,192},{8,200},{16,208},{24,216},{32,224},{40,232},{48,240},{56,2... | collective-permute-start | bytes 196616 | tf_op jit(solution)/shard_map/ppermute | solution.py:299
  72.6 3.8 %collective-permute-start.12 = (bf16[256,128]{1,0:T(8,128)(2,1)S(1)}, bf16[256,128]{1,0:T(8,128)(2,1)S(1)}, u32[]{:S(2)}, u32[]{:S(2)}) collective-permute-start(bf16[256,128]{1,0:T(8,128)(2,1)S(1)} %fusion.3), channel_id=1, source_target_pairs={{0,128},{8,136},{16,144},{24,152},{32,160},{40,168},{48,176},{56,1... | collective-permute-start | bytes 196616 | tf_op jit(solution)/shard_map/ppermute | solution.py:299
  73.9 3.8 %collective-permute-start.11 = (bf16[256,128]{1,0:T(8,128)(2,1)S(1)}, bf16[256,128]{1,0:T(8,128)(2,1)S(1)}, u32[]{:S(2)}, u32[]{:S(2)}) collective-permute-start(bf16[256,128]{1,0:T(8,128)(2,1)S(1)} %fusion.3), channel_id=1, source_target_pairs={{0,64},{8,72},{16,80},{24,88},{32,96},{40,104},{48,112},{56,120},{... | collective-permute-start | bytes 196616 | tf_op jit(solution)/shard_map/ppermute | solution.py:299
  77.7 3.1 %collective-permute-start.14 = (f32[256,128]{1,0:T(8,128)S(1)}, f32[256,128]{1,0:T(8,128)S(1)}, u32[]{:S(2)}, u32[]{:S(2)}) collective-permute-start(f32[256,128]{1,0:T(8,128)S(1)} %fusion.2), channel_id=1, source_target_pairs={{0,8},{8,0},{16,24},{24,16},{32,40},{40,32},{48,56},{56,48},{64,72... | collective-permute-start | bytes 393224 | tf_op jit(solution)/shard_map/ppermute | solution.py:305
  84.0 36.5 %copy-start = (bf16[128,4096]{1,0:T(8,128)(2,1)S(1)}, bf16[128,4096]{1,0:T(8,128)(2,1)}, u32[]{:S(2)}) copy-start(bf16[128,4096]{1,0:T(8,128)(2,1)} %k_hbm.1) | copy-start | bytes 3145732
  84.0 36.5 %copy-start.1 = (bf16[128,4096]{1,0:T(8,128)(2,1)S(1)}, bf16[128,4096]{1,0:T(8,128)(2,1)}, u32[]{:S(2)}) copy-start(bf16[128,4096]{1,0:T(8,128)(2,1)} %v_hbm.1) | copy-start | bytes 3145732
  84.0 36.5 %copy-start.2 = (bf16[128,4096]{1,0:T(8,128)(2,1)S(1)}, bf16[128,4096]{1,0:T(8,128)(2,1)}, u32[]{:S(2)}) copy-start(bf16[128,4096]{1,0:T(8,128)(2,1)} %q_ref.3) | copy-start | bytes 3145732
  84.0 36.5 %copy-start.3 = (f32[32,128]{1,0:T(8,128)S(1)}, f32[32,128]{1,0:T(8,128)}, u32[]{:S(2)}) copy-start(f32[32,128]{1,0:T(8,128)} %add_add_fusion.2.z_ref) | copy-start | bytes 49156
  85.9 34.5 %all-to-all-start.3 = ((bf16[8,512,128]{2,1,0:T(8,128)(2,1)}), bf16[8,512,128]{2,1,0:T(8,128)(2,1)}, u32[]{:S(2)}, u32[]{:S(2)}) async-start(bf16[8,512,128]{2,1,0:T(8,128)(2,1)} %shard_map.70), calls=%async_computation.3 | async-start | bytes 2097152 | tf_op jit(solution)/shard_map/all_to_all | solution.py:342
  92.5 1.9 collective-permute-start.22
  94.4 4.4 %collective-permute-start.25 = (bf16[256,128]{1,0:T(8,128)(2,1)S(1)}, bf16[256,128]{1,0:T(8,128)(2,1)S(1)}, u32[]{:S(2)}, u32[]{:S(2)}) collective-permute-start(bf16[256,128]{1,0:T(8,128)(2,1)S(1)} %fusion.9), channel_id=1, source_target_pairs={{0,16},{8,24},{16,32},{24,40},{32,48},{40,56},{48,0},{56,8},{64,80... | collective-permute-start | bytes 196616 | tf_op jit(solution)/shard_map/ppermute | solution.py:299
  94.8 5.9 %collective-permute-start.24 = (bf16[256,128]{1,0:T(8,128)(2,1)S(1)}, bf16[256,128]{1,0:T(8,128)(2,1)S(1)}, u32[]{:S(2)}, u32[]{:S(2)}) collective-permute-start(bf16[256,128]{1,0:T(8,128)(2,1)S(1)} %fusion.9), channel_id=1, source_target_pairs={{0,32},{8,40},{16,48},{24,56},{32,0},{40,8},{48,16},{56,24},{64,96... | collective-permute-start | bytes 196616 | tf_op jit(solution)/shard_map/ppermute | solution.py:299
  97.4 4.2 %collective-permute-start.23 = (bf16[256,128]{1,0:T(8,128)(2,1)S(1)}, bf16[256,128]{1,0:T(8,128)(2,1)S(1)}, u32[]{:S(2)}, u32[]{:S(2)}) collective-permute-start(bf16[256,128]{1,0:T(8,128)(2,1)S(1)} %fusion.9), channel_id=1, source_target_pairs={{0,48},{8,56},{16,0},{24,8},{32,16},{40,24},{48,32},{56,40},{64,11... | collective-permute-start | bytes 196616 | tf_op jit(solution)/shard_map/ppermute | solution.py:299
  101.6 0.7 copy-start.6
  102.3 30.3 %collective-permute-start.28 = (bf16[256,128]{1,0:T(8,128)(2,1)}, bf16[256,128]{1,0:T(8,128)(2,1)}, u32[]{:S(2)}, u32[]{:S(2)}) collective-permute-start(bf16[256,128]{1,0:T(8,128)(2,1)} %fusion.7), channel_id=1, source_target_pairs={{192,0},{200,8},{208,16},{216,24},{224,32},{232,40},{240,48},{248,... | collective-permute-start | bytes 196616 | tf_op jit(solution)/shard_map/ppermute | solution.py:299
  103.6 29.0 %collective-permute-start.27 = (bf16[256,128]{1,0:T(8,128)(2,1)}, bf16[256,128]{1,0:T(8,128)(2,1)}, u32[]{:S(2)}, u32[]{:S(2)}) collective-permute-start(bf16[256,128]{1,0:T(8,128)(2,1)} %fusion.7), channel_id=1, source_target_pairs={{128,0},{136,8},{144,16},{152,24},{160,32},{168,40},{176,48},{184,... | collective-permute-start | bytes 196616 | tf_op jit(solution)/shard_map/ppermute | solution.py:299
  104.9 27.7 %collective-permute-start.26 = (bf16[256,128]{1,0:T(8,128)(2,1)}, bf16[256,128]{1,0:T(8,128)(2,1)}, u32[]{:S(2)}, u32[]{:S(2)}) collective-permute-start(bf16[256,128]{1,0:T(8,128)(2,1)} %fusion.7), channel_id=1, source_target_pairs={{64,0},{72,8},{80,16},{88,24},{96,32},{104,40},{112,48},{120,56},{... | collective-permute-start | bytes 196616 | tf_op jit(solution)/shard_map/ppermute | solution.py:299
  129.2 11.5 %all-to-all-start.4 = ((f32[8,32,128]{2,1,0:T(8,128)}), f32[8,32,128]{2,1,0:T(8,128)S(1)}, u32[]{:S(2)}, u32[]{:S(2)}) async-start(f32[8,32,128]{2,1,0:T(8,128)} %get-tuple-element.33), calls=%async_computation.4 | async-start | bytes 262144 | tf_op jit(solution)/shard_map/all_to_all | solution.py:328
  133.6 9.1 %collective-permute-start.29 = (f32[256,128]{1,0:T(8,128)S(1)}, f32[256,128]{1,0:T(8,128)S(1)}, u32[]{:S(2)}, u32[]{:S(2)}) collective-permute-start(f32[256,128]{1,0:T(8,128)S(1)} %fusion.6), channel_id=1, source_target_pairs={{0,8},{8,0},{16,24},{24,16},{32,40},{40,32},{48,56},{56,48},{64,72... | collective-permute-start | bytes 393224 | tf_op jit(solution)/shard_map/ppermute | solution.py:305
  140.7 2.8 %collective-permute-start.15 = (f32[32,128]{1,0:T(8,128)S(1)}, f32[32,128]{1,0:T(8,128)S(1)}, u32[]{:S(2)}, u32[]{:S(2)}) collective-permute-start(f32[32,128]{1,0:T(8,128)S(1)} %get-tuple-element.45), channel_id=1, source_target_pairs={{0,8},{8,0},{16,24},{24,16},{32,40},{40,32},{48,56},{56,48},{64,72... | collective-permute-start | bytes 49160 | tf_op jit(solution)/shard_map/ppermute | solution.py:305
  143.5 7.6 %collective-permute-start.18 = (f32[32,128]{1,0:T(8,128)S(1)}, f32[32,128]{1,0:T(8,128)S(1)}, u32[]{:S(2)}, u32[]{:S(2)}) collective-permute-start(f32[32,128]{1,0:T(8,128)S(1)} %add.163), channel_id=1, source_target_pairs={{0,16},{8,24},{16,32},{24,40},{32,48},{40,56},{48,0},{56,8},{64,80... | collective-permute-start | bytes 49160 | tf_op jit(solution)/shard_map/ppermute | solution.py:299
  143.8 7.3 %collective-permute-start.17 = (f32[32,128]{1,0:T(8,128)S(1)}, f32[32,128]{1,0:T(8,128)S(1)}, u32[]{:S(2)}, u32[]{:S(2)}) collective-permute-start(f32[32,128]{1,0:T(8,128)S(1)} %add.163), channel_id=1, source_target_pairs={{0,32},{8,40},{16,48},{24,56},{32,0},{40,8},{48,16},{56,24},{64,96... | collective-permute-start | bytes 49160 | tf_op jit(solution)/shard_map/ppermute | solution.py:299
  146.4 4.7 %collective-permute-start.16 = (f32[32,128]{1,0:T(8,128)S(1)}, f32[32,128]{1,0:T(8,128)S(1)}, u32[]{:S(2)}, u32[]{:S(2)}) collective-permute-start(f32[32,128]{1,0:T(8,128)S(1)} %add.163), channel_id=1, source_target_pairs={{0,48},{8,56},{16,0},{24,8},{32,16},{40,24},{48,32},{56,40},{64,11... | collective-permute-start | bytes 49160 | tf_op jit(solution)/shard_map/ppermute | solution.py:299
  150.7 7.0 %collective-permute-start.30 = (bf16[512,128]{1,0:T(8,128)(2,1)}, bf16[512,128]{1,0:T(8,128)(2,1)S(1)}, u32[]{:S(2)}, u32[]{:S(2)}) collective-permute-start(bf16[512,128]{1,0:T(8,128)(2,1)} %get-tuple-element.36), channel_id=1, source_target_pairs={{0,1},{1,2},{2,3},{3,4},{4,5},{5,6},{6,7},{7,0},{8,9},{9,10},{10,1... | collective-permute-start | bytes 393224 | tf_op jit(solution)/shard_map/ppermute | solution.py:372
  151.0 6.7 %collective-permute-start.31 = (bf16[512,128]{1,0:T(8,128)(2,1)}, bf16[512,128]{1,0:T(8,128)(2,1)S(1)}, u32[]{:S(2)}, u32[]{:S(2)}) collective-permute-start(bf16[512,128]{1,0:T(8,128)(2,1)} %get-tuple-element.37), channel_id=1, source_target_pairs={{0,2},{1,3},{2,4},{3,5},{4,6},{5,7},{6,0},{7,1},{8,10},{9,11},{10,... | collective-permute-start | bytes 393224 | tf_op jit(solution)/shard_map/ppermute | solution.py:372
  151.1 9.3 %collective-permute-start.21 = (f32[32,128]{1,0:T(8,128)S(1)}, f32[32,128]{1,0:T(8,128)S(1)}, u32[]{:S(2)}, u32[]{:S(2)}) collective-permute-start(f32[32,128]{1,0:T(8,128)S(1)} %add_add_fusion.1), channel_id=1, source_target_pairs={{192,0},{200,8},{208,16},{216,24},{224,32},{232,40},{240,48},{248,... | collective-permute-start | bytes 49160 | tf_op jit(solution)/shard_map/ppermute | solution.py:299
  152.4 15.0 %collective-permute-start.20 = (f32[32,128]{1,0:T(8,128)S(1)}, f32[32,128]{1,0:T(8,128)S(1)}, u32[]{:S(2)}, u32[]{:S(2)}) collective-permute-start(f32[32,128]{1,0:T(8,128)S(1)} %add_add_fusion.1), channel_id=1, source_target_pairs={{128,0},{136,8},{144,16},{152,24},{160,32},{168,40},{176,48},{184,... | collective-permute-start | bytes 49160 | tf_op jit(solution)/shard_map/ppermute | solution.py:299
  153.7 13.7 %collective-permute-start.19 = (f32[32,128]{1,0:T(8,128)S(1)}, f32[32,128]{1,0:T(8,128)S(1)}, u32[]{:S(2)}, u32[]{:S(2)}) collective-permute-start(f32[32,128]{1,0:T(8,128)S(1)} %add_add_fusion.1), channel_id=1, source_target_pairs={{64,0},{72,8},{80,16},{88,24},{96,32},{104,40},{112,48},{120,56},{... | collective-permute-start | bytes 49160 | tf_op jit(solution)/shard_map/ppermute | solution.py:299
  157.7 14.7 %collective-permute-start.32 = (bf16[512,128]{1,0:T(8,128)(2,1)}, bf16[512,128]{1,0:T(8,128)(2,1)S(1)}, u32[]{:S(2)}, u32[]{:S(2)}) collective-permute-start(bf16[512,128]{1,0:T(8,128)(2,1)} %get-tuple-element.38), channel_id=1, source_target_pairs={{0,3},{1,4},{2,5},{3,6},{4,7},{5,0},{6,1},{7,2},{8,11},{9,12},{10,... | collective-permute-start | bytes 393224 | tf_op jit(solution)/shard_map/ppermute | solution.py:372
  157.7 14.7 %collective-permute-start.33 = (bf16[512,128]{1,0:T(8,128)(2,1)}, bf16[512,128]{1,0:T(8,128)(2,1)S(1)}, u32[]{:S(2)}, u32[]{:S(2)}) collective-permute-start(bf16[512,128]{1,0:T(8,128)(2,1)} %get-tuple-element.39), channel_id=1, source_target_pairs={{0,4},{1,5},{2,6},{3,7},{4,0},{5,1},{6,2},{7,3},{8,12},{9,13},{10,... | collective-permute-start | bytes 393224 | tf_op jit(solution)/shard_map/ppermute | solution.py:372
  160.4 14.2 %collective-permute-start.34 = (bf16[512,128]{1,0:T(8,128)(2,1)}, bf16[512,128]{1,0:T(8,128)(2,1)S(1)}, u32[]{:S(2)}, u32[]{:S(2)}) collective-permute-start(bf16[512,128]{1,0:T(8,128)(2,1)} %get-tuple-element.40), channel_id=1, source_target_pairs={{0,5},{1,6},{2,7},{3,0},{4,1},{5,2},{6,3},{7,4},{8,13},{9,14},{10,... | collective-permute-start | bytes 393224 | tf_op jit(solution)/shard_map/ppermute | solution.py:372
  167.4 17.1 %collective-permute-start.35 = (bf16[512,128]{1,0:T(8,128)(2,1)}, bf16[512,128]{1,0:T(8,128)(2,1)S(1)}, u32[]{:S(2)}, u32[]{:S(2)}) collective-permute-start(bf16[512,128]{1,0:T(8,128)(2,1)} %get-tuple-element.41), channel_id=1, source_target_pairs={{0,6},{1,7},{2,0},{3,1},{4,2},{5,3},{6,4},{7,5},{8,14},{9,15},{10,... | collective-permute-start | bytes 393224 | tf_op jit(solution)/shard_map/ppermute | solution.py:372
  167.4 17.1 %collective-permute-start.36 = (bf16[512,128]{1,0:T(8,128)(2,1)}, bf16[512,128]{1,0:T(8,128)(2,1)S(1)}, u32[]{:S(2)}, u32[]{:S(2)}) collective-permute-start(bf16[512,128]{1,0:T(8,128)(2,1)} %get-tuple-element.42), channel_id=1, source_target_pairs={{0,7},{1,0},{2,1},{3,2},{4,3},{5,4},{6,5},{7,6},{8,15},{9,8},{10,9... | collective-permute-start | bytes 393224 | tf_op jit(solution)/shard_map/ppermute | solution.py:372
  184.5 0.9 copy-start.4

commit v6 on v5

--- a/solution.py
+++ b/solution.py
@@ -101,18 +101,42 @@
     return [-(s * i) * i for s, i in zip(shared, inverse)]
 
 
-def query_grad_kernel(step, q_ref, k_ref, v_ref, g_ref, z_ref, s_away, *refs):
-    gq_ref, dfk_ref, gv_ref, sum_ref, s_all, sems = refs
+def load_states(away, held, sems, step):
     now = pl.program_id(0)
 
     def load(i):
-        return pltpu.make_async_copy(s_away.at[pl.ds(i * step, step)], s_all.at[i], sems.at[i])
+        return pltpu.make_async_copy(away.at[pl.ds(i * step, step)], held.at[i], sems.at[i])
 
     @pl.when(now == 0)
     def _():
-        for i in range(s_all.shape[0]):
+        for i in range(held.shape[0]):
             load(i).start()
 
+    def ready():
+        load(now).wait()
+        return held.at[now]
+
+    return ready
+
+
+def query_sum_kernel(step, q_ref, k_ref, v_ref, g_ref, z_ref, s_away, sum_ref, s_all, sems):
+    ready = load_states(s_away, s_all, sems, step)
+    mask = causal(q_ref.shape[0])
+    heads = range(step)
+    fq = [feature(q_ref[:, columns(j)].astype(F32)).astype(BF16) for j in heads]
+    fk = [feature(k_ref[:, columns(j)].astype(F32)).astype(BF16) for j in heads]
+    weights, inverse = scores_of(fq, fk, [head_row(z_ref, step, j) for j in heads], mask)
+    num = num_of(fq, weights, [v_ref[:, columns(j)] for j in heads], ready())
+    dden = dden_of(g_ref, num, inverse)
+    for j in heads:
+        row = jnp.sum(dden[j] * fq[j].astype(F32), axis=0, keepdims=True)
+        put_rows(sum_ref, step, j, row)
+
+
+def query_grad_kernel(
+    step, q_ref, k_ref, v_ref, g_ref, z_ref, s_away, gq_ref, dfk_ref, gv_ref, s_all, sems
+):
+    ready = load_states(s_away, s_all, sems, step)
     mask = causal(q_ref.shape[0])
     heads = range(step)
     fq32 = [feature(q_ref[:, columns(j)].astype(F32)) for j in heads]
@@ -121,16 +145,12 @@
     zrows = [head_row(z_ref, step, j) for j in heads]
     v = [v_ref[:, columns(j)] for j in heads]
     weights, inverse = scores_of(fq, fk, zrows, mask)
-    load(now).wait()
-    s_ref = s_all.at[now]
+    s_ref = ready()
     num = num_of(fq, weights, v, s_ref)
     dnum = [(g_ref[:, columns(j)].astype(F32) * inverse[j]).astype(BF16) for j in heads]
     pair = each(dot_nt, dnum, v)
     dden = dden_of(g_ref, num, inverse)
     mixing = [jnp.where(mask, p + d, 0.0).astype(BF16) for p, d in zip(pair, dden)]
-    for j in heads:
-        row = jnp.sum(dden[j] * fq[j].astype(F32), axis=0, keepdims=True)
-        put_rows(sum_ref, step, j, row)
     for j in heads:
         gv_ref[:, columns(j)] = dot_tn(weights[j], dnum[j])
     dfq = [
@@ -362,10 +382,10 @@
     query_total = z_total(query_parts)
     query_base = ctx_running(query_total, ctx, False, BF16, True)
     spread = z_spread(where, query_parts, query_base)
-    grad_queries, dfk, gv, query_sum = call(
-        query_grad_kernel, 8, "wwwwra", "wffg", (queries, keys, values, out_grad, z, prefix)
-    )
+    locals_in = (queries, keys, values, out_grad, z, prefix)
+    (query_sum,) = call(query_sum_kernel, 16, "wwwwra", "g", locals_in)
     sums = z_gather(query_sum)
+    grad_queries, dfk, gv = call(query_grad_kernel, 8, "wwwwra", "wff", locals_in)
     pieces = [spread[0]] + [None] * (group - 1)
     for d in sorted(range(1, group), key=lambda d: -min(d, group - d)):
         pairs = [(i, (i + d) % group) for i in range(group)]

time: 194 us -> 200 us (1.031)
  Pallas kernels: 28.7 us -> 33.5 us
  other arithmetic: 5.74 us -> 8.1 us
    pallas_call x4 -> x5, Pallas kernels: 18.6 us -> 23.4 us  [head_call(): pl.pallas_call(functools.partial(kernel, step), grid=(heads // step,), in...]
  transfers between devices with their start and end apart: 42 -> 42, of which waited for: 25 -> 24; matrix products, arithmetic and copies ran while one was open for 3% -> 4% of each run, Pallas kernels for 11% -> 13%
where the time goes in v6:
time: 200 us; the launch traced here: 197 us
  starting transfers between devices  84.1 us (42%)
  waiting for transfers between devices  69 us (34%)
  Pallas kernels  33.5 us (17%)
  other arithmetic  8.1 us (4%)
    ppermute x24, starting transfers between devices, hop(): return lax.ppermute(value, 'ctx', pairs)  39.2 us
    pallas_call x5, Pallas kernels, head_call(): pl.pallas_call(functools.partial(kernel, step), grid=(heads // step,), in...  23.4 us
    ppermute x7, waiting for transfers between devices, shards(): pieces[d] = lax.ppermute(spread[d], 'head', pairs)  19.4 us
    all_to_all x1, waiting for transfers between devices, from_owners(): return lax.all_to_all(x, 'head', 0, 0, tiled=True).reshape(heads, HD, HD)  14.9 us
    ppermute x24, waiting for transfers between devices, hop(): return lax.ppermute(value, 'ctx', pairs)  14.3 us
    all_to_all x2, starting transfers between devices, z_gather(): return lax.all_to_all(copies, 'head', 0, 0, tiled=True)  13 us
    all_to_all x2, waiting for transfers between devices, z_gather(): return lax.all_to_all(copies, 'head', 0, 0, tiled=True)  10 us
    ppermute x7, starting transfers between devices, shards(): pieces[d] = lax.ppermute(spread[d], 'head', pairs)  9.89 us
  transfers between devices with their start and end apart: 42, of which 24 were waited for; matrix products, arithmetic and copies ran while one was open for 4% of the time, Pallas kernels for 13%

profile of v6, /device:TPU:1, one launch (start us, length us, event | category | flops | bytes accessed | tf_op | source)
XLA Modules:
  0.0 197.2 jit_solution(16971741870781020106)
XLA Ops:
  0.6 2.4 %shard_map.68 = f32[8,32,128]{2,1,0:T(8,128)} custom-call(bf16[128,4096]{1,0:T(8,128)(2,1)} %k_hbm.1), custom_call_target="tpu_custom_call" | custom-call | tf_op jit(solution)/shard_map/pallas_call | solution.py:230
  3.0 9.0 %all-to-all-start = ((f32[8,32,128]{2,1,0:T(8,128)}), f32[8,32,128]{2,1,0:T(8,128)S(1)}, u32[]{:S(2)}, u32[]{:S(2)}) async-start(f32[8,32,128]{2,1,0:T(8,128)} %shard_map.68), calls=%async_computation | async-start | bytes 262144 | tf_op jit(solution)/shard_map/all_to_all | solution.py:348
  12.0 3.0 %shard_map.67 = bf16[32,128,128]{2,1,0:T(8,128)(2,1)} custom-call(bf16[128,4096]{1,0:T(8,128)(2,1)} %k_hbm.1, bf16[128,4096]{1,0:T(8,128)(2,1)} %v_hbm.1), custom_call_target="tpu_custom_call" | custom-call | tf_op jit(solution)/shard_map/pallas_call | solution.py:230
  15.1 4.7 %all-to-all-done = f32[8,32,128]{2,1,0:T(8,128)S(1)} async-done(((f32[8,32,128]{2,1,0:T(8,128)}), f32[8,32,128]{2,1,0:T(8,128)S(1)}, u32[]{:S(2)}, u32[]{:S(2)}) %all-to-all-start) | async-done | bytes 131104 | tf_op jit(solution)/shard_map/all_to_all | solution.py:348
  19.9 3.6 %all-to-all-start.1 = ((bf16[8,512,128]{2,1,0:T(8,128)(2,1)}), bf16[8,512,128]{2,1,0:T(8,128)(2,1)S(1)}, u32[]{:S(2)}, u32[]{:S(2)}) async-start(bf16[8,512,128]{2,1,0:T(8,128)(2,1)} %bitcast.4), calls=%async_computation.1 | async-start | bytes 2097152 | tf_op jit(solution)/shard_map/all_to_all | solution.py:359
  23.5 2.4 %collective-permute-start = (f32[32,128]{1,0:T(8,128)S(1)}, f32[32,128]{1,0:T(8,128)S(1)}, u32[]{:S(2)}, u32[]{:S(2)}) collective-permute-start(f32[32,128]{1,0:T(8,128)S(1)} %get-tuple-element.24), channel_id=1, source_target_pairs={{0,8},{8,0},{16,24},{24,16},{32,40},{40,32},{48,56},{56,48},{64,72... | collective-permute-start | bytes 49160 | tf_op jit(solution)/shard_map/ppermute | solution.py:325
  25.8 0.8 collective-permute-done
  26.7 2.7 %collective-permute-start.3 = (f32[32,128]{1,0:T(8,128)S(1)}, f32[32,128]{1,0:T(8,128)S(1)}, u32[]{:S(2)}, u32[]{:S(2)}) collective-permute-start(f32[32,128]{1,0:T(8,128)S(1)} %add.142), channel_id=1, source_target_pairs={{0,48},{8,56},{16,0},{24,8},{32,16},{40,24},{48,32},{56,40},{64,11... | collective-permute-start | bytes 49160 | tf_op jit(solution)/shard_map/ppermute | solution.py:319
  30.5 3.3 %collective-permute-done.2 = f32[32,128]{1,0:T(8,128)S(1)} collective-permute-done((f32[32,128]{1,0:T(8,128)S(1)}, f32[32,128]{1,0:T(8,128)S(1)}, u32[]{:S(2)}, u32[]{:S(2)}) %collective-permute-start.2) | collective-permute-done | bytes 16416 | tf_op jit(solution)/shard_map/ppermute | solution.py:319
  34.0 4.4 %collective-permute-start.6 = (f32[32,128]{1,0:T(8,128)S(1)}, f32[32,128]{1,0:T(8,128)S(1)}, u32[]{:S(2)}, u32[]{:S(2)}) collective-permute-start(f32[32,128]{1,0:T(8,128)S(1)} %add_add_fusion.3), channel_id=1, source_target_pairs={{0,192},{8,200},{16,208},{24,216},{32,224},{40,232},{48,240},{56,2... | collective-permute-start | bytes 49160 | tf_op jit(solution)/shard_map/ppermute | solution.py:319
  38.4 1.3 collective-permute-start.5
  39.7 2.5 %collective-permute-start.4 = (f32[32,128]{1,0:T(8,128)S(1)}, f32[32,128]{1,0:T(8,128)S(1)}, u32[]{:S(2)}, u32[]{:S(2)}) collective-permute-start(f32[32,128]{1,0:T(8,128)S(1)} %add_add_fusion.3), channel_id=1, source_target_pairs={{0,64},{8,72},{16,80},{24,88},{32,96},{40,104},{48,112},{56,120},{... | collective-permute-start | bytes 49160 | tf_op jit(solution)/shard_map/ppermute | solution.py:319
  42.2 0.8 collective-permute-done.4
  43.6 4.5 %shard_map.69 = bf16[32,128,128]{2,1,0:T(8,128)(2,1)} custom-call(bf16[128,4096]{1,0:T(8,128)(2,1)} %q_ref.5, bf16[128,4096]{1,0:T(8,128)(2,1)} %k_hbm.1, bf16[128,4096]{1,0:T(8,128)(2,1)} %g_ref.5, f32[32,128]{1,0:T(8,128)} %add_add_fusion.2.z_ref), custom_call_target="tpu_custom_call" | custom-call | tf_op jit(solution)/shard_map/pallas_call | solution.py:230
  48.1 4.4 %all-to-all-done.1.x_ref = bf16[8,512,128]{2,1,0:T(8,128)(2,1)S(1)} async-done(((bf16[8,512,128]{2,1,0:T(8,128)(2,1)}), bf16[8,512,128]{2,1,0:T(8,128)(2,1)S(1)}, u32[]{:S(2)}, u32[]{:S(2)}) %all-to-all-start.1) | async-done | bytes 1048608 | tf_op jit(solution)/shard_map/all_to_all | solution.py:359
  52.5 4.2 %all-to-all-start.2 = ((bf16[8,512,128]{2,1,0:T(8,128)(2,1)}), bf16[8,512,128]{2,1,0:T(8,128)(2,1)}, u32[]{:S(2)}, u32[]{:S(2)}) async-start(bf16[8,512,128]{2,1,0:T(8,128)(2,1)} %bitcast.5), calls=%async_computation.2 | async-start | bytes 2097152 | tf_op jit(solution)/shard_map/all_to_all | solution.py:359
  56.9 1.3 collective-permute-start.7
  58.2 1.2 collective-permute-done.7
  59.4 2.2 %collective-permute-start.10 = (bf16[256,128]{1,0:T(8,128)(2,1)S(1)}, bf16[256,128]{1,0:T(8,128)(2,1)S(1)}, u32[]{:S(2)}, u32[]{:S(2)}) collective-permute-start(bf16[256,128]{1,0:T(8,128)(2,1)S(1)} %fusion.8), channel_id=1, source_target_pairs={{0,48},{8,56},{16,0},{24,8},{32,16},{40,24},{48,32},{56,40},{64,11... | collective-permute-start | bytes 196616 | tf_op jit(solution)/shard_map/ppermute | solution.py:319
  63.0 3.6 %collective-permute-done.9 = bf16[256,128]{1,0:T(8,128)(2,1)S(1)} collective-permute-done((bf16[256,128]{1,0:T(8,128)(2,1)S(1)}, bf16[256,128]{1,0:T(8,128)(2,1)S(1)}, u32[]{:S(2)}, u32[]{:S(2)}) %collective-permute-start.9) | collective-permute-done | bytes 65568 | tf_op jit(solution)/shard_map/ppermute | solution.py:319
  66.6 1.5 collective-permute-done.8
  68.2 4.4 %collective-permute-start.13 = (bf16[256,128]{1,0:T(8,128)(2,1)S(1)}, bf16[256,128]{1,0:T(8,128)(2,1)S(1)}, u32[]{:S(2)}, u32[]{:S(2)}) collective-permute-start(bf16[256,128]{1,0:T(8,128)(2,1)S(1)} %fusion.3), channel_id=1, source_target_pairs={{0,192},{8,200},{16,208},{24,216},{32,224},{40,232},{48,240},{56,2... | collective-permute-start | bytes 196616 | tf_op jit(solution)/shard_map/ppermute | solution.py:319
  72.6 1.3 collective-permute-start.12
  73.9 2.5 %collective-permute-start.11 = (bf16[256,128]{1,0:T(8,128)(2,1)S(1)}, bf16[256,128]{1,0:T(8,128)(2,1)S(1)}, u32[]{:S(2)}, u32[]{:S(2)}) collective-permute-start(bf16[256,128]{1,0:T(8,128)(2,1)S(1)} %fusion.3), channel_id=1, source_target_pairs={{0,64},{8,72},{16,80},{24,88},{32,96},{40,104},{48,112},{56,120},{... | collective-permute-start | bytes 196616 | tf_op jit(solution)/shard_map/ppermute | solution.py:319
  76.4 1.3 collective-permute-done.11
  77.7 2.1 %collective-permute-start.14 = (f32[256,128]{1,0:T(8,128)S(1)}, f32[256,128]{1,0:T(8,128)S(1)}, u32[]{:S(2)}, u32[]{:S(2)}) collective-permute-start(f32[256,128]{1,0:T(8,128)S(1)} %fusion.2), channel_id=1, source_target_pairs={{0,8},{8,0},{16,24},{24,16},{32,40},{40,32},{48,56},{56,48},{64,72... | collective-permute-start | bytes 393224 | tf_op jit(solution)/shard_map/ppermute | solution.py:325
  79.8 1.0 collective-permute-done.14
  80.8 0.7 maximum_add_fusion.base_ref
  81.6 2.4 %shard_map.70 = bf16[8,512,128]{2,1,0:T(8,128)(2,1)} custom-call(bf16[8,512,128]{2,1,0:T(8,128)(2,1)} %copy-done.5, f32[512,128]{1,0:T(8,128)} %maximum_add_fusion.base_ref), custom_call_target="tpu_custom_call" | custom-call | tf_op jit(solution)/shard_map/pallas_call | solution.py:270
  84.0 1.9 all-to-all-done.2.x_ref
  85.9 5.2 %all-to-all-start.3 = ((bf16[8,512,128]{2,1,0:T(8,128)(2,1)}), bf16[8,512,128]{2,1,0:T(8,128)(2,1)}, u32[]{:S(2)}, u32[]{:S(2)}) async-start(bf16[8,512,128]{2,1,0:T(8,128)(2,1)} %shard_map.70), calls=%async_computation.3 | async-start | bytes 2097152 | tf_op jit(solution)/shard_map/all_to_all | solution.py:362
  91.1 1.4 convert_reduce_fusion
  93.2 1.2 collective-permute-done.22
  94.8 2.6 %collective-permute-start.24 = (bf16[256,128]{1,0:T(8,128)(2,1)S(1)}, bf16[256,128]{1,0:T(8,128)(2,1)S(1)}, u32[]{:S(2)}, u32[]{:S(2)}) collective-permute-start(bf16[256,128]{1,0:T(8,128)(2,1)S(1)} %fusion.9), channel_id=1, source_target_pairs={{0,32},{8,40},{16,48},{24,56},{32,0},{40,8},{48,16},{56,24},{64,96... | collective-permute-start | bytes 196616 | tf_op jit(solution)/shard_map/ppermute | solution.py:319
  97.4 1.1 collective-permute-start.23
  98.9 1.9 collective-permute-done.24
  100.7 0.9 collective-permute-done.23
  101.7 1.3 collective-permute-start.28
  103.0 1.3 collective-permute-start.27
  104.3 1.3 collective-permute-start.26
  105.6 14.9 %all-to-all-done.3 = bf16[8,512,128]{2,1,0:T(8,128)(2,1)} async-done(((bf16[8,512,128]{2,1,0:T(8,128)(2,1)}), bf16[8,512,128]{2,1,0:T(8,128)(2,1)}, u32[]{:S(2)}, u32[]{:S(2)}) %all-to-all-start.3) | async-done | bytes 1048608 | tf_op jit(solution)/shard_map/all_to_all | solution.py:362
  120.5 5.0 %shard_map.72 = f32[8,32,128]{2,1,0:T(8,128)} custom-call(bf16[128,4096]{1,0:T(8,128)(2,1)S(1)} %copy-done.2, bf16[128,4096]{1,0:T(8,128)(2,1)S(1)} %copy-done, bf16[128,4096]{1,0:T(8,128)(2,1)S(1)} %copy-done.1, bf16[128,4096]{1,0:T(8,128)(2,1)} %g_ref.5, f32[32,128]{1,0:T(8,128)S(1)} %copy-done.3, bf16[32,128,128]{2,1,0:T(8,128)(2,1)} %bitcast.2.s_away), custom_call_target="tpu_custom_call" | custom-call | tf_op jit(solution)/shard_map/pallas_call | solution.py:230
  125.4 4.0 %all-to-all-start.4 = ((f32[8,32,128]{2,1,0:T(8,128)}), f32[8,32,128]{2,1,0:T(8,128)}, u32[]{:S(2)}, u32[]{:S(2)}) async-start(f32[8,32,128]{2,1,0:T(8,128)} %shard_map.72), calls=%async_computation.4 | async-start | bytes 262144 | tf_op jit(solution)/shard_map/all_to_all | solution.py:348
  130.1 1.1 fusion.6
  132.3 5.3 %all-to-all-done.4 = f32[8,32,128]{2,1,0:T(8,128)} async-done(((f32[8,32,128]{2,1,0:T(8,128)}), f32[8,32,128]{2,1,0:T(8,128)}, u32[]{:S(2)}, u32[]{:S(2)}) %all-to-all-start.4) | async-done | bytes 131104 | tf_op jit(solution)/shard_map/all_to_all | solution.py:348
  137.6 1.6 fusion.10
  139.2 1.9 collective-permute-start.15
  141.1 0.9 broadcast_select_fusion.1
  142.9 2.6 %collective-permute-start.17 = (f32[32,128]{1,0:T(8,128)S(1)}, f32[32,128]{1,0:T(8,128)S(1)}, u32[]{:S(2)}, u32[]{:S(2)}) collective-permute-start(f32[32,128]{1,0:T(8,128)S(1)} %add.163), channel_id=1, source_target_pairs={{0,32},{8,40},{16,48},{24,56},{32,0},{40,8},{48,16},{56,24},{64,96... | collective-permute-start | bytes 49160 | tf_op jit(solution)/shard_map/ppermute | solution.py:319
  145.5 1.1 collective-permute-start.16
  147.3 2.5 %shard_map.73 = (bf16[512,128]{1,0:T(8,128)(2,1)}, bf16[512,128]{1,0:T(8,128)(2,1)}, bf16[512,128]{1,0:T(8,128)(2,1)}, bf16[512,128]{1,0:T(8,128)(2,1)}, bf16[51...) custom-call(s32[1]{0:T(128)} %bitcast.3.place_ref, ...), custom_call_target="tpu_custom_call" | custom-call | tf_op jit(solution)/shard_map/pallas_call | solution.py:281
  150.3 1.4 collective-permute-start.21
  151.8 1.3 collective-permute-start.20
  153.1 1.3 collective-permute-start.19
  154.4 8.5 %shard_map.71 = (bf16[128,4096]{1,0:T(8,128)(2,1)}, f32[128,4096]{1,0:T(8,128)}, f32[128,4096]{1,0:T(8,128)}) custom-call(bf16[128,4096]{1,0:T(8,128)(2,1)S(1)} %copy-done.2, bf16[128,4096]{1,0:T(8,128)(2,1)S(1)} %copy-done, bf16[128,4096]{1,0:T(8,128)(2,1)S(1)} %copy-done.1, bf16[128,4096]{1,0:T(8,128)(2,1)} %g_ref.5, f32[32,128]{1,0:T(8,128)S(1)} %copy-done.3, ...), custom_call_target="tpu_custom_call" | custom-call | tf_op jit(solution)/shard_map/pallas_call | solution.py:230
  162.9 2.2 %collective-permute-start.32 = (bf16[512,128]{1,0:T(8,128)(2,1)S(1)}, bf16[512,128]{1,0:T(8,128)(2,1)S(1)}, u32[]{:S(2)}, u32[]{:S(2)}) collective-permute-start(bf16[512,128]{1,0:T(8,128)(2,1)S(1)} %copy-done.17), channel_id=1, source_target_pairs={{0,3},{1,4},{2,5},{3,6},{4,7},{5,0},{6,1},{7,2},{8,11},{9,12},{10,... | collective-permute-start | bytes 393224 | tf_op jit(solution)/shard_map/ppermute | solution.py:392
  165.1 3.2 %collective-permute-start.33 = (bf16[512,128]{1,0:T(8,128)(2,1)S(1)}, bf16[512,128]{1,0:T(8,128)(2,1)S(1)}, u32[]{:S(2)}, u32[]{:S(2)}) collective-permute-start(bf16[512,128]{1,0:T(8,128)(2,1)S(1)} %copy-done.16), channel_id=1, source_target_pairs={{0,4},{1,5},{2,6},{3,7},{4,0},{5,1},{6,2},{7,3},{8,12},{9,13},{10,... | collective-permute-start | bytes 393224 | tf_op jit(solution)/shard_map/ppermute | solution.py:392
  168.3 1.2 collective-permute-start.34
  169.4 2.5 %collective-permute-start.35 = (bf16[512,128]{1,0:T(8,128)(2,1)S(1)}, bf16[512,128]{1,0:T(8,128)(2,1)S(1)}, u32[]{:S(2)}, u32[]{:S(2)}) collective-permute-start(bf16[512,128]{1,0:T(8,128)(2,1)S(1)} %copy-done.14), channel_id=1, source_target_pairs={{0,6},{1,7},{2,0},{3,1},{4,2},{5,3},{6,4},{7,5},{8,14},{9,15},{10,... | collective-permute-start | bytes 393224 | tf_op jit(solution)/shard_map/ppermute | solution.py:392
  172.4 2.9 %collective-permute-done.32.refs_3_ = bf16[512,128]{1,0:T(8,128)(2,1)S(1)} collective-permute-done((bf16[512,128]{1,0:T(8,128)(2,1)S(1)}, bf16[512,128]{1,0:T(8,128)(2,1)S(1)}, u32[]{:S(2)}, u32[]{:S(2)}) %collective-permute-start.32) | collective-permute-done | bytes 131104 | tf_op jit(solution)/shard_map/ppermute | solution.py:392
  175.3 5.4 %collective-permute-done.33.refs_4_ = bf16[512,128]{1,0:T(8,128)(2,1)S(1)} collective-permute-done((bf16[512,128]{1,0:T(8,128)(2,1)S(1)}, bf16[512,128]{1,0:T(8,128)(2,1)S(1)}, u32[]{:S(2)}, u32[]{:S(2)}) %collective-permute-start.33) | collective-permute-done | bytes 131104 | tf_op jit(solution)/shard_map/ppermute | solution.py:392
  181.2 8.4 %collective-permute-done.35.refs_6_ = bf16[512,128]{1,0:T(8,128)(2,1)S(1)} collective-permute-done((bf16[512,128]{1,0:T(8,128)(2,1)S(1)}, bf16[512,128]{1,0:T(8,128)(2,1)S(1)}, u32[]{:S(2)}, u32[]{:S(2)}) %collective-permute-start.35) | collective-permute-done | bytes 131104 | tf_op jit(solution)/shard_map/ppermute | solution.py:392
  189.6 2.2 %collective-permute-done.36.refs_7_ = bf16[512,128]{1,0:T(8,128)(2,1)S(1)} collective-permute-done((bf16[512,128]{1,0:T(8,128)(2,1)S(1)}, bf16[512,128]{1,0:T(8,128)(2,1)S(1)}, u32[]{:S(2)}, u32[]{:S(2)}) %collective-permute-start.36) | collective-permute-done | bytes 131104 | tf_op jit(solution)/shard_map/ppermute | solution.py:392
  191.8 5.3 %shard_map.74 = (bf16[128,4096]{1,0:T(8,128)(2,1)}, bf16[128,4096]{1,0:T(8,128)(2,1)}) custom-call(s32[1]{0:T(128)} %bitcast.3.place_ref, bf16[128,4096]{1,0:T(8,128)(2,1)S(1)} %copy-done, bf16[128,4096]{1,0:T(8,128)(2,1)S(1)} %copy-done.1, f32[128,4096]{1,0:T(8,128)} %get-tuple-element.30.dfk_hbm, f32[128,4096]{1,0:T(8,128)} %get-tuple-element.31.gv_hbm, ...), custom_call_target="tpu_custom_call" | custom-call | tf_op jit(solution)/shard_map/pallas_call | solution.py:206
  (88 shorter events, 10.0 us)
Async XLA Ops:
  3.0 16.8 %all-to-all-start = ((f32[8,32,128]{2,1,0:T(8,128)}), f32[8,32,128]{2,1,0:T(8,128)S(1)}, u32[]{:S(2)}, u32[]{:S(2)}) async-start(f32[8,32,128]{2,1,0:T(8,128)} %shard_map.68), calls=%async_computation | async-start | bytes 262144 | tf_op jit(solution)/shard_map/all_to_all | solution.py:348
  19.9 32.6 %all-to-all-start.1 = ((bf16[8,512,128]{2,1,0:T(8,128)(2,1)}), bf16[8,512,128]{2,1,0:T(8,128)(2,1)S(1)}, u32[]{:S(2)}, u32[]{:S(2)}) async-start(bf16[8,512,128]{2,1,0:T(8,128)(2,1)} %bitcast.4), calls=%async_computation.1 | async-start | bytes 2097152 | tf_op jit(solution)/shard_map/all_to_all | solution.py:359
  23.5 3.2 %collective-permute-start = (f32[32,128]{1,0:T(8,128)S(1)}, f32[32,128]{1,0:T(8,128)S(1)}, u32[]{:S(2)}, u32[]{:S(2)}) collective-permute-start(f32[32,128]{1,0:T(8,128)S(1)} %get-tuple-element.24), channel_id=1, source_target_pairs={{0,8},{8,0},{16,24},{24,16},{32,40},{40,32},{48,56},{56,48},{64,72... | collective-permute-start | bytes 49160 | tf_op jit(solution)/shard_map/ppermute | solution.py:325
  26.7 3.8 %collective-permute-start.3 = (f32[32,128]{1,0:T(8,128)S(1)}, f32[32,128]{1,0:T(8,128)S(1)}, u32[]{:S(2)}, u32[]{:S(2)}) collective-permute-start(f32[32,128]{1,0:T(8,128)S(1)} %add.142), channel_id=1, source_target_pairs={{0,48},{8,56},{16,0},{24,8},{32,16},{40,24},{48,32},{56,40},{64,11... | collective-permute-start | bytes 49160 | tf_op jit(solution)/shard_map/ppermute | solution.py:319
  29.4 4.4 %collective-permute-start.2 = (f32[32,128]{1,0:T(8,128)S(1)}, f32[32,128]{1,0:T(8,128)S(1)}, u32[]{:S(2)}, u32[]{:S(2)}) collective-permute-start(f32[32,128]{1,0:T(8,128)S(1)} %add.142), channel_id=1, source_target_pairs={{0,32},{8,40},{16,48},{24,56},{32,0},{40,8},{48,16},{56,24},{64,96... | collective-permute-start | bytes 49160 | tf_op jit(solution)/shard_map/ppermute | solution.py:319
  29.8 4.2 %collective-permute-start.1 = (f32[32,128]{1,0:T(8,128)S(1)}, f32[32,128]{1,0:T(8,128)S(1)}, u32[]{:S(2)}, u32[]{:S(2)}) collective-permute-start(f32[32,128]{1,0:T(8,128)S(1)} %add.142), channel_id=1, source_target_pairs={{0,16},{8,24},{16,32},{24,40},{32,48},{40,56},{48,0},{56,8},{64,80... | collective-permute-start | bytes 49160 | tf_op jit(solution)/shard_map/ppermute | solution.py:319
  34.0 8.2 %collective-permute-start.6 = (f32[32,128]{1,0:T(8,128)S(1)}, f32[32,128]{1,0:T(8,128)S(1)}, u32[]{:S(2)}, u32[]{:S(2)}) collective-permute-start(f32[32,128]{1,0:T(8,128)S(1)} %add_add_fusion.3), channel_id=1, source_target_pairs={{0,192},{8,200},{16,208},{24,216},{32,224},{40,232},{48,240},{56,2... | collective-permute-start | bytes 49160 | tf_op jit(solution)/shard_map/ppermute | solution.py:319
  38.4 3.8 %collective-permute-start.5 = (f32[32,128]{1,0:T(8,128)S(1)}, f32[32,128]{1,0:T(8,128)S(1)}, u32[]{:S(2)}, u32[]{:S(2)}) collective-permute-start(f32[32,128]{1,0:T(8,128)S(1)} %add_add_fusion.3), channel_id=1, source_target_pairs={{0,128},{8,136},{16,144},{24,152},{32,160},{40,168},{48,176},{56,1... | collective-permute-start | bytes 49160 | tf_op jit(solution)/shard_map/ppermute | solution.py:319
  39.7 3.3 %collective-permute-start.4 = (f32[32,128]{1,0:T(8,128)S(1)}, f32[32,128]{1,0:T(8,128)S(1)}, u32[]{:S(2)}, u32[]{:S(2)}) collective-permute-start(f32[32,128]{1,0:T(8,128)S(1)} %add_add_fusion.3), channel_id=1, source_target_pairs={{0,64},{8,72},{16,80},{24,88},{32,96},{40,104},{48,112},{56,120},{... | collective-permute-start | bytes 49160 | tf_op jit(solution)/shard_map/ppermute | solution.py:319
  52.5 6.9 %copy-start.5 = (bf16[8,512,128]{2,1,0:T(8,128)(2,1)}, bf16[8,512,128]{2,1,0:T(8,128)(2,1)S(1)}, u32[]{:S(2)}) copy-start(bf16[8,512,128]{2,1,0:T(8,128)(2,1)S(1)} %all-to-all-done.1.x_ref) | copy-start | bytes 3145732
  52.5 33.4 %all-to-all-start.2 = ((bf16[8,512,128]{2,1,0:T(8,128)(2,1)}), bf16[8,512,128]{2,1,0:T(8,128)(2,1)}, u32[]{:S(2)}, u32[]{:S(2)}) async-start(bf16[8,512,128]{2,1,0:T(8,128)(2,1)} %bitcast.5), calls=%async_computation.2 | async-start | bytes 2097152 | tf_op jit(solution)/shard_map/all_to_all | solution.py:359
  56.9 2.4 %collective-permute-start.7 = (f32[512,128]{1,0:T(8,128)S(1)}, f32[512,128]{1,0:T(8,128)S(1)}, u32[]{:S(2)}, u32[]{:S(2)}) collective-permute-start(f32[512,128]{1,0:T(8,128)S(1)} %convert_reduce_fusion.1), channel_id=1, source_target_pairs={{0,8},{8,0},{16,24},{24,16},{32,40},{40,32},{48,56},{56,48},{64,72... | collective-permute-start | bytes 786440 | tf_op jit(solution)/shard_map/ppermute | solution.py:325
  59.4 3.6 %collective-permute-start.10 = (bf16[256,128]{1,0:T(8,128)(2,1)S(1)}, bf16[256,128]{1,0:T(8,128)(2,1)S(1)}, u32[]{:S(2)}, u32[]{:S(2)}) collective-permute-start(bf16[256,128]{1,0:T(8,128)(2,1)S(1)} %fusion.8), channel_id=1, source_target_pairs={{0,48},{8,56},{16,0},{24,8},{32,16},{40,24},{48,32},{56,40},{64,11... | collective-permute-start | bytes 196616 | tf_op jit(solution)/shard_map/ppermute | solution.py:319
  61.6 5.0 %collective-permute-start.9 = (bf16[256,128]{1,0:T(8,128)(2,1)S(1)}, bf16[256,128]{1,0:T(8,128)(2,1)S(1)}, u32[]{:S(2)}, u32[]{:S(2)}) collective-permute-start(bf16[256,128]{1,0:T(8,128)(2,1)S(1)} %fusion.8), channel_id=1, source_target_pairs={{0,32},{8,40},{16,48},{24,56},{32,0},{40,8},{48,16},{56,24},{64,96... | collective-permute-start | bytes 196616 | tf_op jit(solution)/shard_map/ppermute | solution.py:319
  61.9 6.2 %collective-permute-start.8 = (bf16[256,128]{1,0:T(8,128)(2,1)S(1)}, bf16[256,128]{1,0:T(8,128)(2,1)S(1)}, u32[]{:S(2)}, u32[]{:S(2)}) collective-permute-start(bf16[256,128]{1,0:T(8,128)(2,1)S(1)} %fusion.8), channel_id=1, source_target_pairs={{0,16},{8,24},{16,32},{24,40},{32,48},{40,56},{48,0},{56,8},{64,80... | collective-permute-start | bytes 196616 | tf_op jit(solution)/shard_map/ppermute | solution.py:319
  68.2 8.2 %collective-permute-start.13 = (bf16[256,128]{1,0:T(8,128)(2,1)S(1)}, bf16[256,128]{1,0:T(8,128)(2,1)S(1)}, u32[]{:S(2)}, u32[]{:S(2)}) collective-permute-start(bf16[256,128]{1,0:T(8,128)(2,1)S(1)} %fusion.3), channel_id=1, source_target_pairs={{0,192},{8,200},{16,208},{24,216},{32,224},{40,232},{48,240},{56,2... | collective-permute-start | bytes 196616 | tf_op jit(solution)/shard_map/ppermute | solution.py:319
  72.6 3.8 %collective-permute-start.12 = (bf16[256,128]{1,0:T(8,128)(2,1)S(1)}, bf16[256,128]{1,0:T(8,128)(2,1)S(1)}, u32[]{:S(2)}, u32[]{:S(2)}) collective-permute-start(bf16[256,128]{1,0:T(8,128)(2,1)S(1)} %fusion.3), channel_id=1, source_target_pairs={{0,128},{8,136},{16,144},{24,152},{32,160},{40,168},{48,176},{56,1... | collective-permute-start | bytes 196616 | tf_op jit(solution)/shard_map/ppermute | solution.py:319
  73.9 3.8 %collective-permute-start.11 = (bf16[256,128]{1,0:T(8,128)(2,1)S(1)}, bf16[256,128]{1,0:T(8,128)(2,1)S(1)}, u32[]{:S(2)}, u32[]{:S(2)}) collective-permute-start(bf16[256,128]{1,0:T(8,128)(2,1)S(1)} %fusion.3), channel_id=1, source_target_pairs={{0,64},{8,72},{16,80},{24,88},{32,96},{40,104},{48,112},{56,120},{... | collective-permute-start | bytes 196616 | tf_op jit(solution)/shard_map/ppermute | solution.py:319
  77.7 3.1 %collective-permute-start.14 = (f32[256,128]{1,0:T(8,128)S(1)}, f32[256,128]{1,0:T(8,128)S(1)}, u32[]{:S(2)}, u32[]{:S(2)}) collective-permute-start(f32[256,128]{1,0:T(8,128)S(1)} %fusion.2), channel_id=1, source_target_pairs={{0,8},{8,0},{16,24},{24,16},{32,40},{40,32},{48,56},{56,48},{64,72... | collective-permute-start | bytes 393224 | tf_op jit(solution)/shard_map/ppermute | solution.py:325
  84.0 36.5 %copy-start = (bf16[128,4096]{1,0:T(8,128)(2,1)S(1)}, bf16[128,4096]{1,0:T(8,128)(2,1)}, u32[]{:S(2)}) copy-start(bf16[128,4096]{1,0:T(8,128)(2,1)} %k_hbm.1) | copy-start | bytes 3145732
  84.0 36.5 %copy-start.1 = (bf16[128,4096]{1,0:T(8,128)(2,1)S(1)}, bf16[128,4096]{1,0:T(8,128)(2,1)}, u32[]{:S(2)}) copy-start(bf16[128,4096]{1,0:T(8,128)(2,1)} %v_hbm.1) | copy-start | bytes 3145732
  84.0 36.5 %copy-start.2 = (bf16[128,4096]{1,0:T(8,128)(2,1)S(1)}, bf16[128,4096]{1,0:T(8,128)(2,1)}, u32[]{:S(2)}) copy-start(bf16[128,4096]{1,0:T(8,128)(2,1)} %q_ref.5) | copy-start | bytes 3145732
  84.0 36.5 %copy-start.3 = (f32[32,128]{1,0:T(8,128)S(1)}, f32[32,128]{1,0:T(8,128)}, u32[]{:S(2)}) copy-start(f32[32,128]{1,0:T(8,128)} %add_add_fusion.2.z_ref) | copy-start | bytes 49156
  85.9 34.5 %all-to-all-start.3 = ((bf16[8,512,128]{2,1,0:T(8,128)(2,1)}), bf16[8,512,128]{2,1,0:T(8,128)(2,1)}, u32[]{:S(2)}, u32[]{:S(2)}) async-start(bf16[8,512,128]{2,1,0:T(8,128)(2,1)} %shard_map.70), calls=%async_computation.3 | async-start | bytes 2097152 | tf_op jit(solution)/shard_map/all_to_all | solution.py:362
  92.5 1.9 collective-permute-start.22
  94.4 4.4 %collective-permute-start.25 = (bf16[256,128]{1,0:T(8,128)(2,1)S(1)}, bf16[256,128]{1,0:T(8,128)(2,1)S(1)}, u32[]{:S(2)}, u32[]{:S(2)}) collective-permute-start(bf16[256,128]{1,0:T(8,128)(2,1)S(1)} %fusion.9), channel_id=1, source_target_pairs={{0,16},{8,24},{16,32},{24,40},{32,48},{40,56},{48,0},{56,8},{64,80... | collective-permute-start | bytes 196616 | tf_op jit(solution)/shard_map/ppermute | solution.py:319
  94.8 5.9 %collective-permute-start.24 = (bf16[256,128]{1,0:T(8,128)(2,1)S(1)}, bf16[256,128]{1,0:T(8,128)(2,1)S(1)}, u32[]{:S(2)}, u32[]{:S(2)}) collective-permute-start(bf16[256,128]{1,0:T(8,128)(2,1)S(1)} %fusion.9), channel_id=1, source_target_pairs={{0,32},{8,40},{16,48},{24,56},{32,0},{40,8},{48,16},{56,24},{64,96... | collective-permute-start | bytes 196616 | tf_op jit(solution)/shard_map/ppermute | solution.py:319
  97.4 4.2 %collective-permute-start.23 = (bf16[256,128]{1,0:T(8,128)(2,1)S(1)}, bf16[256,128]{1,0:T(8,128)(2,1)S(1)}, u32[]{:S(2)}, u32[]{:S(2)}) collective-permute-start(bf16[256,128]{1,0:T(8,128)(2,1)S(1)} %fusion.9), channel_id=1, source_target_pairs={{0,48},{8,56},{16,0},{24,8},{32,16},{40,24},{48,32},{56,40},{64,11... | collective-permute-start | bytes 196616 | tf_op jit(solution)/shard_map/ppermute | solution.py:319
  98.8 2.8 %copy-start.6 = (bf16[256,128]{1,0:T(8,128)(2,1)}, bf16[256,128]{1,0:T(8,128)(2,1)S(1)}, u32[]{:S(2)}) copy-start(bf16[256,128]{1,0:T(8,128)(2,1)S(1)} %collective-permute-done.25) | copy-start | bytes 196612
  100.7 2.2 %copy-start.7 = (bf16[256,128]{1,0:T(8,128)(2,1)}, bf16[256,128]{1,0:T(8,128)(2,1)S(1)}, u32[]{:S(2)}) copy-start(bf16[256,128]{1,0:T(8,128)(2,1)S(1)} %collective-permute-done.24) | copy-start | bytes 196612
  101.6 2.7 %copy-start.8 = (bf16[256,128]{1,0:T(8,128)(2,1)}, bf16[256,128]{1,0:T(8,128)(2,1)S(1)}, u32[]{:S(2)}) copy-start(bf16[256,128]{1,0:T(8,128)(2,1)S(1)} %collective-permute-done.23) | copy-start | bytes 196612
  101.7 27.8 %collective-permute-start.28 = (bf16[256,128]{1,0:T(8,128)(2,1)S(1)}, bf16[256,128]{1,0:T(8,128)(2,1)S(1)}, u32[]{:S(2)}, u32[]{:S(2)}) collective-permute-start(bf16[256,128]{1,0:T(8,128)(2,1)S(1)} %fusion.7), channel_id=1, source_target_pairs={{192,0},{200,8},{208,16},{216,24},{224,32},{232,40},{240,48},{248,... | collective-permute-start | bytes 196616 | tf_op jit(solution)/shard_map/ppermute | solution.py:319
  103.0 26.5 %collective-permute-start.27 = (bf16[256,128]{1,0:T(8,128)(2,1)S(1)}, bf16[256,128]{1,0:T(8,128)(2,1)}, u32[]{:S(2)}, u32[]{:S(2)}) collective-permute-start(bf16[256,128]{1,0:T(8,128)(2,1)S(1)} %fusion.7), channel_id=1, source_target_pairs={{128,0},{136,8},{144,16},{152,24},{160,32},{168,40},{176,48},{184,... | collective-permute-start | bytes 196616 | tf_op jit(solution)/shard_map/ppermute | solution.py:319
  104.3 25.8 %collective-permute-start.26 = (bf16[256,128]{1,0:T(8,128)(2,1)S(1)}, bf16[256,128]{1,0:T(8,128)(2,1)}, u32[]{:S(2)}, u32[]{:S(2)}) collective-permute-start(bf16[256,128]{1,0:T(8,128)(2,1)S(1)} %fusion.7), channel_id=1, source_target_pairs={{64,0},{72,8},{80,16},{88,24},{96,32},{104,40},{112,48},{120,56},{... | collective-permute-start | bytes 196616 | tf_op jit(solution)/shard_map/ppermute | solution.py:319
  125.4 12.1 %all-to-all-start.4 = ((f32[8,32,128]{2,1,0:T(8,128)}), f32[8,32,128]{2,1,0:T(8,128)}, u32[]{:S(2)}, u32[]{:S(2)}) async-start(f32[8,32,128]{2,1,0:T(8,128)} %shard_map.72), calls=%async_computation.4 | async-start | bytes 262144 | tf_op jit(solution)/shard_map/all_to_all | solution.py:348
  129.5 0.6 copy-start.9
  131.2 9.9 %collective-permute-start.29 = (f32[256,128]{1,0:T(8,128)S(1)}, f32[256,128]{1,0:T(8,128)}, u32[]{:S(2)}, u32[]{:S(2)}) collective-permute-start(f32[256,128]{1,0:T(8,128)S(1)} %fusion.6), channel_id=1, source_target_pairs={{0,8},{8,0},{16,24},{24,16},{32,40},{40,32},{48,56},{56,48},{64,72... | collective-permute-start | bytes 393224 | tf_op jit(solution)/shard_map/ppermute | solution.py:325
  139.2 2.8 %collective-permute-start.15 = (f32[32,128]{1,0:T(8,128)S(1)}, f32[32,128]{1,0:T(8,128)S(1)}, u32[]{:S(2)}, u32[]{:S(2)}) collective-permute-start(f32[32,128]{1,0:T(8,128)S(1)} %get-tuple-element.43), channel_id=1, source_target_pairs={{0,8},{8,0},{16,24},{24,16},{32,40},{40,32},{48,56},{56,48},{64,72... | collective-permute-start | bytes 49160 | tf_op jit(solution)/shard_map/ppermute | solution.py:325
  142.0 0.6 copy-start.11
  142.6 7.6 %collective-permute-start.18 = (f32[32,128]{1,0:T(8,128)S(1)}, f32[32,128]{1,0:T(8,128)S(1)}, u32[]{:S(2)}, u32[]{:S(2)}) collective-permute-start(f32[32,128]{1,0:T(8,128)S(1)} %add.163), channel_id=1, source_target_pairs={{0,16},{8,24},{16,32},{24,40},{32,48},{40,56},{48,0},{56,8},{64,80... | collective-permute-start | bytes 49160 | tf_op jit(solution)/shard_map/ppermute | solution.py:319
  142.9 7.3 %collective-permute-start.17 = (f32[32,128]{1,0:T(8,128)S(1)}, f32[32,128]{1,0:T(8,128)S(1)}, u32[]{:S(2)}, u32[]{:S(2)}) collective-permute-start(f32[32,128]{1,0:T(8,128)S(1)} %add.163), channel_id=1, source_target_pairs={{0,32},{8,40},{16,48},{24,56},{32,0},{40,8},{48,16},{56,24},{64,96... | collective-permute-start | bytes 49160 | tf_op jit(solution)/shard_map/ppermute | solution.py:319
  145.5 4.7 %collective-permute-start.16 = (f32[32,128]{1,0:T(8,128)S(1)}, f32[32,128]{1,0:T(8,128)S(1)}, u32[]{:S(2)}, u32[]{:S(2)}) collective-permute-start(f32[32,128]{1,0:T(8,128)S(1)} %add.163), channel_id=1, source_target_pairs={{0,48},{8,56},{16,0},{24,8},{32,16},{40,24},{48,32},{56,40},{64,11... | collective-permute-start | bytes 49160 | tf_op jit(solution)/shard_map/ppermute | solution.py:319
  149.8 13.1 %collective-permute-start.30 = (bf16[512,128]{1,0:T(8,128)(2,1)}, bf16[512,128]{1,0:T(8,128)(2,1)S(1)}, u32[]{:S(2)}, u32[]{:S(2)}) collective-permute-start(bf16[512,128]{1,0:T(8,128)(2,1)} %get-tuple-element.34), channel_id=1, source_target_pairs={{0,1},{1,2},{2,3},{3,4},{4,5},{5,6},{6,7},{7,0},{8,9},{9,10},{10,1... | collective-permute-start | bytes 393224 | tf_op jit(solution)/shard_map/ppermute | solution.py:392
  150.1 15.0 %collective-permute-start.31 = (bf16[512,128]{1,0:T(8,128)(2,1)}, bf16[512,128]{1,0:T(8,128)(2,1)S(1)}, u32[]{:S(2)}, u32[]{:S(2)}) collective-permute-start(bf16[512,128]{1,0:T(8,128)(2,1)} %get-tuple-element.35), channel_id=1, source_target_pairs={{0,2},{1,3},{2,4},{3,5},{4,6},{5,7},{6,0},{7,1},{8,10},{9,11},{10,... | collective-permute-start | bytes 393224 | tf_op jit(solution)/shard_map/ppermute | solution.py:392
  150.2 12.7 %copy-start.17 = (bf16[512,128]{1,0:T(8,128)(2,1)S(1)}, bf16[512,128]{1,0:T(8,128)(2,1)}, u32[]{:S(2)}) copy-start(bf16[512,128]{1,0:T(8,128)(2,1)} %get-tuple-element.36) | copy-start | bytes 393220
  150.3 14.8 %copy-start.16 = (bf16[512,128]{1,0:T(8,128)(2,1)S(1)}, bf16[512,128]{1,0:T(8,128)(2,1)}, u32[]{:S(2)}) copy-start(bf16[512,128]{1,0:T(8,128)(2,1)} %get-tuple-element.37) | copy-start | bytes 393220
  150.3 18.0 %copy-start.15 = (bf16[512,128]{1,0:T(8,128)(2,1)S(1)}, bf16[512,128]{1,0:T(8,128)(2,1)}, u32[]{:S(2)}) copy-start(bf16[512,128]{1,0:T(8,128)(2,1)} %get-tuple-element.38) | copy-start | bytes 393220
  150.3 19.2 %copy-start.14 = (bf16[512,128]{1,0:T(8,128)(2,1)S(1)}, bf16[512,128]{1,0:T(8,128)(2,1)}, u32[]{:S(2)}) copy-start(bf16[512,128]{1,0:T(8,128)(2,1)} %get-tuple-element.39) | copy-start | bytes 393220
  150.3 21.6 %copy-start.13 = (bf16[512,128]{1,0:T(8,128)(2,1)S(1)}, bf16[512,128]{1,0:T(8,128)(2,1)}, u32[]{:S(2)}) copy-start(bf16[512,128]{1,0:T(8,128)(2,1)} %get-tuple-element.40) | copy-start | bytes 393220
  150.3 22.1 %copy-start.10 = (f32[32,128]{1,0:T(8,128)S(1)}, f32[32,128]{1,0:T(8,128)}, u32[]{:S(2)}) copy-start(f32[32,128]{1,0:T(8,128)} %get-tuple-element.44) | copy-start | bytes 49156
  150.3 22.1 %copy-start.12 = (f32[32,128]{1,0:T(8,128)S(1)}, f32[32,128]{1,0:T(8,128)}, u32[]{:S(2)}) copy-start(f32[32,128]{1,0:T(8,128)} %copy-done.11) | copy-start | bytes 49156
  150.3 41.5 %copy-start.4 = (bf16[512,128]{1,0:T(8,128)(2,1)S(1)}, bf16[512,128]{1,0:T(8,128)(2,1)}, u32[]{:S(2)}) copy-start(bf16[512,128]{1,0:T(8,128)(2,1)} %get-tuple-element.33.refs_0_) | copy-start | bytes 393220
  150.3 18.0 %collective-permute-start.21 = (f32[32,128]{1,0:T(8,128)S(1)}, f32[32,128]{1,0:T(8,128)S(1)}, u32[]{:S(2)}, u32[]{:S(2)}) collective-permute-start(f32[32,128]{1,0:T(8,128)S(1)} %add_add_fusion.1), channel_id=1, source_target_pairs={{192,0},{200,8},{208,16},{216,24},{224,32},{232,40},{240,48},{248,... | collective-permute-start | bytes 49160 | tf_op jit(solution)/shard_map/ppermute | solution.py:319
  151.8 17.7 %collective-permute-start.20 = (f32[32,128]{1,0:T(8,128)S(1)}, f32[32,128]{1,0:T(8,128)S(1)}, u32[]{:S(2)}, u32[]{:S(2)}) collective-permute-start(f32[32,128]{1,0:T(8,128)S(1)} %add_add_fusion.1), channel_id=1, source_target_pairs={{128,0},{136,8},{144,16},{152,24},{160,32},{168,40},{176,48},{184,... | collective-permute-start | bytes 49160 | tf_op jit(solution)/shard_map/ppermute | solution.py:319
  153.1 18.9 %collective-permute-start.19 = (f32[32,128]{1,0:T(8,128)S(1)}, f32[32,128]{1,0:T(8,128)S(1)}, u32[]{:S(2)}, u32[]{:S(2)}) collective-permute-start(f32[32,128]{1,0:T(8,128)S(1)} %add_add_fusion.1), channel_id=1, source_target_pairs={{64,0},{72,8},{80,16},{88,24},{96,32},{104,40},{112,48},{120,56},{... | collective-permute-start | bytes 49160 | tf_op jit(solution)/shard_map/ppermute | solution.py:319
  162.9 12.4 %collective-permute-start.32 = (bf16[512,128]{1,0:T(8,128)(2,1)S(1)}, bf16[512,128]{1,0:T(8,128)(2,1)S(1)}, u32[]{:S(2)}, u32[]{:S(2)}) collective-permute-start(bf16[512,128]{1,0:T(8,128)(2,1)S(1)} %copy-done.17), channel_id=1, source_target_pairs={{0,3},{1,4},{2,5},{3,6},{4,7},{5,0},{6,1},{7,2},{8,11},{9,12},{10,... | collective-permute-start | bytes 393224 | tf_op jit(solution)/shard_map/ppermute | solution.py:392
  165.1 15.7 %collective-permute-start.33 = (bf16[512,128]{1,0:T(8,128)(2,1)S(1)}, bf16[512,128]{1,0:T(8,128)(2,1)S(1)}, u32[]{:S(2)}, u32[]{:S(2)}) collective-permute-start(bf16[512,128]{1,0:T(8,128)(2,1)S(1)} %copy-done.16), channel_id=1, source_target_pairs={{0,4},{1,5},{2,6},{3,7},{4,0},{5,1},{6,2},{7,3},{8,12},{9,13},{10,... | collective-permute-start | bytes 393224 | tf_op jit(solution)/shard_map/ppermute | solution.py:392
  168.3 13.0 %collective-permute-start.34 = (bf16[512,128]{1,0:T(8,128)(2,1)S(1)}, bf16[512,128]{1,0:T(8,128)(2,1)S(1)}, u32[]{:S(2)}, u32[]{:S(2)}) collective-permute-start(bf16[512,128]{1,0:T(8,128)(2,1)S(1)} %copy-done.15), channel_id=1, source_target_pairs={{0,5},{1,6},{2,7},{3,0},{4,1},{5,2},{6,3},{7,4},{8,13},{9,14},{10,... | collective-permute-start | bytes 393224 | tf_op jit(solution)/shard_map/ppermute | solution.py:392
  169.4 20.2 %collective-permute-start.35 = (bf16[512,128]{1,0:T(8,128)(2,1)S(1)}, bf16[512,128]{1,0:T(8,128)(2,1)S(1)}, u32[]{:S(2)}, u32[]{:S(2)}) collective-permute-start(bf16[512,128]{1,0:T(8,128)(2,1)S(1)} %copy-done.14), channel_id=1, source_target_pairs={{0,6},{1,7},{2,0},{3,1},{4,2},{5,3},{6,4},{7,5},{8,14},{9,15},{10,... | collective-permute-start | bytes 393224 | tf_op jit(solution)/shard_map/ppermute | solution.py:392
  171.9 19.9 %collective-permute-start.36 = (bf16[512,128]{1,0:T(8,128)(2,1)S(1)}, bf16[512,128]{1,0:T(8,128)(2,1)S(1)}, u32[]{:S(2)}, u32[]{:S(2)}) collective-permute-start(bf16[512,128]{1,0:T(8,128)(2,1)S(1)} %copy-done.13), channel_id=1, source_target_pairs={{0,7},{1,0},{2,1},{3,2},{4,3},{5,4},{6,5},{7,6},{8,15},{9,8},{10,9... | collective-permute-start | bytes 393224 | tf_op jit(solution)/shard_map/ppermute | solution.py:392
